TPU v7x, 32 devices: a whole 2x2x4 slice. The times are simulated.
32 devices in a mesh: trk: 8 (over z, x), sub: 4 (over y, core).
Axes of the slice: x: 2, y: 2, z: 4, core: 2. Of those that a mesh axis runs over, the one named last changes fastest.
Arguments:
- particle_cells: int32 [3, 262144], P(None, ('trk', 'sub')), may hold values from 0 to 126, as said below
- offsets: float32 [3, 262144], P(None, ('trk', 'sub')), may hold values from 0 to 1
- momenta: float32 [3, 262144], P(None, ('trk', 'sub')), may hold values from -3 to 3
- live_counts: int32 [32], P(('trk', 'sub')), may hold values from 1024 to 8192, as said below
- green_hat: float32 [256, 256, 256], P('trk', None, 'sub'), may hold values from 0.001953125 to 2560, as said below
- orders: int32 [4], replicated, may hold values from 2 to 5
- strengths: float32 [4], replicated, may hold values from -1 to 1
Outputs:
- new_coords: float32 [3, 262144], P(None, ('trk', 'sub'))
- new_momenta: float32 [3, 262144], P(None, ('trk', 'sub'))
Inputs may be any that keep to these rules, and one draw needn't show every extreme that they name: cells[0] and cells[1] are at most 126; rows r of particle_cells have a z cell in [s * 16, (s + 1) * 16) with s = r // 32768, and at most 126. `live_counts`: some entry equals 8192 in every draw. `green_hat`: positive.
All inputs are finite; a program needn't handle non-finite values.
Results may differ from a plain program's by a relative error of at most 0.0003.
Values sent between devices are 32-bit elements; how exact they have to be, the bound alone decides.
No kernel may reach another device: no remote copies, remote signals or barrier semaphores. Data moves between devices by JAX's collectives and lax.ppermute only.
A program may use at most 64 MiB of HBM per device.

v0:
```python
import math

import jax
import jax.numpy as jnp
from jax import lax
from jax.sharding import PartitionSpec as P

NG = 128


HIGHEST = lax.Precision.HIGHEST


def multipole_push(particle_cells, offsets, orders, strengths):
    centre = 0.5 * NG
    real_u = (particle_cells[0].astype(jnp.float32) + offsets[0] - centre) / centre
    imag_u = (particle_cells[1].astype(jnp.float32) + offsets[1] - centre) / centre
    power_re = real_u
    power_im = imag_u
    push_x = jnp.zeros_like(real_u)
    push_y = jnp.zeros_like(real_u)
    for degree in range(1, 5):
        coeff = jnp.sum(jnp.where(orders - 1 == degree, strengths, jnp.zeros_like(strengths)))
        push_x = push_x - coeff * power_re
        push_y = push_y + coeff * power_im
        power_re, power_im = (
            power_re * real_u - power_im * imag_u,
            power_re * imag_u + power_im * real_u,
        )
    return (push_x, push_y)


def wave_table(freq_ids, place_ids, length):
    phase_int = freq_ids[:, None] * place_ids[None, :] % length
    angle = 2.0 * math.pi / length * phase_int.astype(jnp.float32)
    return (jnp.cos(angle), jnp.sin(angle))


def tent_weights(cells, fraction, length):
    places = jnp.arange(length, dtype=jnp.int32)
    lower = jnp.where(places[None, :] == cells[:, None], (1.0 - fraction)[:, None], 0.0)
    upper = jnp.where(places[None, :] == cells[:, None] + 1, fraction[:, None], 0.0)
    return lower + upper


def block_weights(cells_x, cells_y, cells_z, frac_x, frac_y, frac_z, depth):
    weight_x = tent_weights(cells_x, frac_x, NG)
    weight_y = tent_weights(cells_y, frac_y, NG)
    weight_z = tent_weights(cells_z, frac_z, depth)
    plane_xz = (weight_x[:, :, None] * weight_z[:, None, :]).reshape(cells_x.shape[0], -1)
    return (plane_xz, weight_y)


def per_device(particle_cells, offsets, momenta, live_counts, green_hat, orders, strengths):
    trk_count = lax.axis_size("trk")
    sub_count = lax.axis_size("sub")
    slab_depth = NG // trk_count
    depth = slab_depth + 1
    doubled = 2 * NG
    count_here = particle_cells.shape[1]
    count_all = count_here * trk_count * sub_count
    row_ids = jnp.arange(count_here, dtype=jnp.int32)
    unit_charge = float(NG**3) / float(count_all)
    charge = jnp.where(
        row_ids < live_counts[0],
        jnp.full((count_here,), unit_charge, jnp.float32),
        jnp.zeros((count_here,), jnp.float32),
    )
    local_z = particle_cells[2] - lax.axis_index("trk") * slab_depth
    block_len = math.gcd(count_here, 512)
    block_count = count_here // block_len
    blocked_x = particle_cells[0].reshape(block_count, block_len)
    blocked_y = particle_cells[1].reshape(block_count, block_len)
    blocked_z = local_z.reshape(block_count, block_len)
    blocked_off = offsets.reshape(3, block_count, block_len).transpose(1, 0, 2)
    blocked_charge = charge.reshape(block_count, block_len)

    def deposit_step(total, items):
        bx, by, bz, boff, bcharge = items
        plane_xz, weight_y = block_weights(bx, by, bz, boff[0], boff[1], boff[2], depth)
        charged = plane_xz * bcharge[:, None]
        return (total + jnp.einsum("pa,py->ay", charged, weight_y, precision=HIGHEST), None)

    start_total = jnp.zeros((NG * depth, NG), jnp.float32)
    deposit, _ = lax.scan(
        deposit_step, start_total, (blocked_x, blocked_y, blocked_z, blocked_off, blocked_charge)
    )
    deposit = deposit.reshape(NG, depth, NG)
    density = lax.psum_scatter(deposit, "sub", scatter_dimension=0, tiled=True)
    freq_all = jnp.arange(doubled, dtype=jnp.int32)
    cell_ids = jnp.arange(NG, dtype=jnp.int32)
    cos_cells, sin_cells = wave_table(freq_all, cell_ids, doubled)
    spec_re = jnp.einsum("xzy,ky->xzk", density, cos_cells, precision=HIGHEST)
    spec_im = -jnp.einsum("xzy,ky->xzk", density, sin_cells, precision=HIGHEST)
    part_re = lax.all_to_all(spec_re, "sub", split_axis=2, concat_axis=0, tiled=True)
    part_im = lax.all_to_all(spec_im, "sub", split_axis=2, concat_axis=0, tiled=True)
    out_re = jnp.einsum("kn,nzq->kzq", cos_cells, part_re, precision=HIGHEST) + jnp.einsum(
        "kn,nzq->kzq", sin_cells, part_im, precision=HIGHEST
    )
    out_im = jnp.einsum("kn,nzq->kzq", cos_cells, part_im, precision=HIGHEST) - jnp.einsum(
        "kn,nzq->kzq", sin_cells, part_re, precision=HIGHEST
    )
    xspec_re = out_re
    xspec_im = out_im
    slab_starts = jnp.arange(trk_count, dtype=jnp.int32)[:, None] * slab_depth
    forward_places = (slab_starts + jnp.arange(slab_depth + 1, dtype=jnp.int32)[None, :]).reshape(
        -1
    )
    cos_fwd, sin_fwd = wave_table(freq_all, forward_places, doubled)
    part_re = lax.all_to_all(xspec_re, "trk", split_axis=0, concat_axis=1, tiled=True)
    part_im = lax.all_to_all(xspec_im, "trk", split_axis=0, concat_axis=1, tiled=True)
    out_re = jnp.einsum("kn,xnq->xkq", cos_fwd, part_re, precision=HIGHEST) + jnp.einsum(
        "kn,xnq->xkq", sin_fwd, part_im, precision=HIGHEST
    )
    out_im = jnp.einsum("kn,xnq->xkq", cos_fwd, part_im, precision=HIGHEST) - jnp.einsum(
        "kn,xnq->xkq", sin_fwd, part_re, precision=HIGHEST
    )
    zspec_re = out_re
    zspec_im = out_im
    scaled_re = zspec_re * green_hat
    scaled_im = zspec_im * green_hat
    back_places = (slab_starts - 1 + jnp.arange(slab_depth + 3, dtype=jnp.int32)[None, :]).reshape(
        -1
    )
    inside = ((back_places >= 0) & (back_places < NG)).astype(jnp.float32) / doubled
    cos_back, sin_back = wave_table(back_places, freq_all, doubled)
    cos_back = cos_back * inside[:, None]
    sin_back = sin_back * inside[:, None]
    plane_re = jnp.einsum("nk,xkq->xnq", cos_back, scaled_re, precision=HIGHEST) - jnp.einsum(
        "nk,xkq->xnq", sin_back, scaled_im, precision=HIGHEST
    )
    plane_im = jnp.einsum("nk,xkq->xnq", sin_back, scaled_re, precision=HIGHEST) + jnp.einsum(
        "nk,xkq->xnq", cos_back, scaled_im, precision=HIGHEST
    )
    cos_inverse = jnp.transpose(cos_cells) / doubled
    sin_inverse = jnp.transpose(sin_cells) / doubled
    part_re = lax.all_to_all(plane_re, "trk", split_axis=1, concat_axis=0, tiled=True)
    part_im = lax.all_to_all(plane_im, "trk", split_axis=1, concat_axis=0, tiled=True)
    out_re = jnp.einsum("nk,kzq->nzq", cos_inverse, part_re, precision=HIGHEST) - jnp.einsum(
        "nk,kzq->nzq", sin_inverse, part_im, precision=HIGHEST
    )
    out_im = jnp.einsum("nk,kzq->nzq", sin_inverse, part_re, precision=HIGHEST) + jnp.einsum(
        "nk,kzq->nzq", cos_inverse, part_im, precision=HIGHEST
    )
    cos_final = cos_cells / doubled
    sin_final = sin_cells / doubled
    part_re = lax.all_to_all(out_re, "sub", split_axis=0, concat_axis=2, tiled=True)
    part_im = lax.all_to_all(out_im, "sub", split_axis=0, concat_axis=2, tiled=True)
    block_rows = jnp.einsum("xzk,ky->xzy", part_re, cos_final, precision=HIGHEST) - jnp.einsum(
        "xzk,ky->xzy", part_im, sin_final, precision=HIGHEST
    )
    potential = lax.all_gather(block_rows, "sub", axis=0, tiled=True)
    middle = potential[:, 1 : slab_depth + 2]
    around_x = jnp.pad(middle, ((1, 1), (0, 0), (0, 0)))
    field_x = -0.5 * (around_x[2:] - around_x[:-2])
    around_y = jnp.pad(middle, ((0, 0), (0, 0), (1, 1)))
    field_y = -0.5 * (around_y[:, :, 2:] - around_y[:, :, :-2])
    field_z = -0.5 * (potential[:, 2 : slab_depth + 3] - potential[:, : slab_depth + 1])
    field_table = jnp.stack([field_x, field_y, field_z], axis=2).reshape(NG * depth, 3 * NG)

    def sample_step(carry, items):
        bx, by, bz, boff = items
        plane_xz, weight_y = block_weights(bx, by, bz, boff[0], boff[1], boff[2], depth)
        lines = jnp.dot(plane_xz, field_table, precision=HIGHEST).reshape(bx.shape[0], 3, NG)
        return (carry, jnp.sum(lines * weight_y[:, None, :], axis=2))

    _, sampled = lax.scan(
        sample_step, jnp.zeros((), jnp.float32), (blocked_x, blocked_y, blocked_z, blocked_off)
    )
    kick = sampled.reshape(count_here, 3).transpose(1, 0)
    push_x, push_y = multipole_push(particle_cells, offsets, orders, strengths)
    push = jnp.stack([push_x, push_y, jnp.zeros_like(push_x)])
    new_momenta = momenta + kick + push
    new_coords = particle_cells.astype(jnp.float32) + offsets + new_momenta
    return (new_coords, new_momenta)


def solution(mesh):
    in_specs = (
        P(None, ("trk", "sub")),
        P(None, ("trk", "sub")),
        P(None, ("trk", "sub")),
        P(("trk", "sub")),
        P("trk", None, "sub"),
        P(),
        P(),
    )
    out_specs = (P(None, ("trk", "sub")), P(None, ("trk", "sub")))
    return jax.shard_map(
        per_device, mesh=mesh, in_specs=in_specs, out_specs=out_specs, check_vma=False
    )
```

profile of v0, /device:TPU:0, one launch (start us, length us, event | category | flops | bytes accessed | tf_op | source)
XLA Modules:
  0.0 929.0 jit_solution(12447481894327090690)
XLA Ops:
  9.3 249.0 %while.22 = (s32[]{:T(128)}, f32[2176,128]{1,0:T(8,128)S(1)}, s32[16,512]{1,0:T(8,128)S(1)}, f32[16,3,512]{2,1,0:T(4,128)}, s32[16,512]{1,0:T(8,128)S(1)}, /*ind...) while((s32[]{:T(128)}, f32[2176,128]{1,0:T(8,128)S(1)}, ...), condition=%wide.region_1.2_spmd.clone, body=%wide.region_0.1_spmd.clone.sunk | while | flops 1714763264 | bytes 20727976 | solution.py:85
  13.8 5.5 mul.1078
  29.4 5.5 mul.1078
  44.9 5.5 mul.1078
  60.5 5.5 mul.1078
  91.6 5.5 mul.1078
  138.3 5.5 mul.1078
  153.9 5.5 mul.1078
  169.4 5.5 mul.1078
  185.0 5.5 mul.1078
  200.5 5.5 mul.1078
  216.1 5.5 mul.1078
  247.2 5.5 mul.1078
  259.6 31.0 %reduce-scatter.2.cloned.1.call-done = f32[32,17,128]{2,1,0:T(8,128)} async-done(((f32[128,17,128]{2,1,0:T(8,128)}), f32[32,17,128]{2,1,0:T(8,128)}) %reduce-scatter.2.cloned.1.call-update) | async-done | bytes 278544 | tf_op jit(solution)/shard_map/reduce_scatter | solution.py:89
  345.4 6.2 all-to-all-start.2
  360.2 19.1 %all-to-all-done.2 = f32[8,1,34816]{2,1,0:T(1,128)} async-done(((f32[8,1,34816]{2,1,0:T(1,128)}), f32[8,1,34816]{2,1,0:T(1,128)}, u32[]{:S(2)}, u32[]{:S(2)}) %all-to-all-start.2) | async-done | bytes 1114144 | tf_op jit(solution)/shard_map/all_to_all | solution.py:110
  384.0 5.6 reduce.14
  396.4 14.3 %all-to-all-done.3 = f32[8,1,34816]{2,1,0:T(1,128)} async-done(((f32[8,1,34816]{2,1,0:T(1,128)}), f32[8,1,34816]{2,1,0:T(1,128)}, u32[]{:S(2)}, u32[]{:S(2)}) %all-to-all-start.3) | async-done | bytes 1114144 | tf_op jit(solution)/shard_map/all_to_all | solution.py:111
  463.4 18.0 %all-to-all-done.5 = f32[8,1,38912]{2,1,0:T(1,128)} async-done(((f32[8,1,38912]{2,1,0:T(1,128)}), f32[8,1,38912]{2,1,0:T(1,128)}, u32[]{:S(2)}, u32[]{:S(2)}) %all-to-all-start.5) | async-done | bytes 1245216 | tf_op jit(solution)/shard_map/all_to_all | solution.py:138
  486.1 6.0 reduce.17
  499.9 15.8 %all-to-all-done.4 = f32[8,1,38912]{2,1,0:T(1,128)} async-done(((f32[8,1,38912]{2,1,0:T(1,128)}), f32[8,1,38912]{2,1,0:T(1,128)}, u32[]{:S(2)}, u32[]{:S(2)}) %all-to-all-start.4) | async-done | bytes 1245216 | tf_op jit(solution)/shard_map/all_to_all | solution.py:137
  576.8 12.3 %all-gather.2.cloned.1.call-done = f32[128,19,128]{2,0,1:T(8,128)} async-done(((f32[32,19,128]{2,0,1:T(8,128)}), f32[128,19,128]{2,0,1:T(8,128)}) %all-gather.2.cloned.1.call-update) | async-done | bytes 1245200 | tf_op jit(solution)/shard_map/all_gather | solution.py:152
  600.5 319.3 %while.21 = (s32[]{:T(128)}, f32[16,512,3]{1,2,0:T(4,128)}, s32[16,512]{1,0:T(8,128)}, f32[16,3,512]{2,1,0:T(4,128)}, s32[16,512]{1,0:T(8,128)}, /*index=5*/f32[...) while((s32[]{:T(128)}, f32[16,512,3]{1,2,0:T(4,128)}, ...), condition=%wide.region_5.6_spmd, body=%wide.region_3.5_spmd.sunk | while | flops 5136035840 | bytes 22381208 | solution.py:167
  612.0 7.8 fusion.238
  632.0 7.8 fusion.238
  651.9 7.8 fusion.238
  671.9 7.8 fusion.238
  686.3 5.5 mul.1072
  691.8 7.8 fusion.238
  706.2 5.5 mul.1072
  711.8 7.8 fusion.238
  731.7 7.8 fusion.238
  746.1 5.5 mul.1072
  751.7 7.8 fusion.238
  766.1 5.5 mul.1072
  771.6 7.8 fusion.238
  786.0 5.5 mul.1072
  791.6 7.8 fusion.238
  806.0 5.5 mul.1072
  811.6 7.8 fusion.238
  825.9 5.5 mul.1072
  831.5 7.8 fusion.238
  851.5 7.8 fusion.238
  871.4 7.8 fusion.238
  885.8 5.5 mul.1072
  891.4 7.8 fusion.238
  905.7 5.5 mul.1072
  911.3 7.8 fusion.238
  (610 shorter events, 540.9 us)
Async XLA Ops:
  7.2 283.5 %reduce-scatter.2.cloned.1.call-start = ((), (), s32[]{:S(2)}) async-start(), calls=%async_computation.9 | async-start | bytes 1966080 | tf_op jit(solution)/shard_map/reduce_scatter | solution.py:89
  258.3 1.3 copy-start.15
  258.3 1.3 copy-start.16
  258.3 1.3 copy-start.17
  295.9 6.0 copy-start.11
  297.8 13.4 %all-to-all-start = ((f32[4,1,34816]{2,1,0:T(1,128)}), f32[4,1,34816]{2,1,0:T(1,128)}, u32[]{:S(2)}, u32[]{:S(2)}) async-start(f32[4,1,34816]{2,1,0:T(1,128)} %reshape.589), calls=%async_computation.1 | async-start | bytes 1114112 | tf_op jit(solution)/shard_map/all_to_all | solution.py:95
  311.2 17.2 %all-to-all-start.1 = ((f32[4,1,34816]{2,1,0:T(1,128)}), f32[4,1,34816]{2,1,0:T(1,128)}, u32[]{:S(2)}, u32[]{:S(2)}) async-start(f32[4,1,34816]{2,1,0:T(1,128)} %reshape.591), calls=%async_computation.2 | async-start | bytes 1114112 | tf_op jit(solution)/shard_map/all_to_all | solution.py:96
  325.8 2.5 copy-start.6
  336.5 3.3 copy-start.10
  338.2 1.6 copy-start.8
  345.4 6.2 copy-start.7
  345.4 7.7 copy-start.9
  345.4 34.0 %all-to-all-start.2 = ((f32[8,1,34816]{2,1,0:T(1,128)}), f32[8,1,34816]{2,1,0:T(1,128)}, u32[]{:S(2)}, u32[]{:S(2)}) async-start(f32[8,1,34816]{2,1,0:T(1,128)} %reshape.593), calls=%async_computation.3 | async-start | bytes 2228224 | tf_op jit(solution)/shard_map/all_to_all | solution.py:110
  379.4 31.3 %all-to-all-start.3 = ((f32[8,1,34816]{2,1,0:T(1,128)}), f32[8,1,34816]{2,1,0:T(1,128)}, u32[]{:S(2)}, u32[]{:S(2)}) async-start(f32[8,1,34816]{2,1,0:T(1,128)} %reshape.595), calls=%async_computation.4 | async-start | bytes 2228224 | tf_op jit(solution)/shard_map/all_to_all | solution.py:111
  425.5 2.5 copy-start.2
  428.0 2.5 copy-start.5
  433.1 2.6 copy-start.3
  435.6 2.7 copy-start
  447.4 4.4 copy-start.4
  447.4 34.0 %all-to-all-start.5 = ((f32[8,1,38912]{2,1,0:T(1,128)}), f32[8,1,38912]{2,1,0:T(1,128)}, u32[]{:S(2)}, u32[]{:S(2)}) async-start(f32[8,1,38912]{2,1,0:T(1,128)} %reshape.599), calls=%async_computation.6 | async-start | bytes 2490368 | tf_op jit(solution)/shard_map/all_to_all | solution.py:138
  451.8 2.5 copy-start.1
  481.4 34.3 %all-to-all-start.4 = ((f32[8,1,38912]{2,1,0:T(1,128)}), f32[8,1,38912]{2,1,0:T(1,128)}, u32[]{:S(2)}, u32[]{:S(2)}) async-start(f32[8,1,38912]{2,1,0:T(1,128)} %reshape.597), calls=%async_computation.5 | async-start | bytes 2490368 | tf_op jit(solution)/shard_map/all_to_all | solution.py:137
  537.0 13.4 %all-to-all-start.7 = ((f32[4,1,38912]{2,1,0:T(1,128)}), f32[4,1,38912]{2,1,0:T(1,128)S(1)}, u32[]{:S(2)}, u32[]{:S(2)}) async-start(f32[4,1,38912]{2,1,0:T(1,128)} %reshape.603), calls=%async_computation.8 | async-start | bytes 1245184 | tf_op jit(solution)/shard_map/all_to_all | solution.py:148
  550.3 14.1 %all-to-all-start.6 = ((f32[4,1,38912]{2,1,0:T(1,128)}), f32[4,1,38912]{2,1,0:T(1,128)}, u32[]{:S(2)}, u32[]{:S(2)}) async-start(f32[4,1,38912]{2,1,0:T(1,128)} %reshape.601), calls=%async_computation.7 | async-start | bytes 1245184 | tf_op jit(solution)/shard_map/all_to_all | solution.py:147
  554.5 34.7 %all-gather.2.cloned.1.call-start = ((), (), s32[]{:S(2)}) async-start(), calls=%async_computation.10 | async-start | bytes 1556480 | tf_op jit(solution)/shard_map/all_gather | solution.py:152
  569.4 3.8 copy-start.18
  569.4 3.8 copy-start.19
  569.4 5.2 copy-start.12
  569.4 5.2 copy-start.14
  600.5 319.3 %copy-start.13 = (s32[3,8192]{1,0:T(4,128)S(1)}, s32[3,8192]{1,0:T(4,128)}, u32[]{:S(2)}) copy-start(s32[3,8192]{1,0:T(4,128)} %param.11) | copy-start | bytes 294916
Sparse Core Ops, SparseCore 0:
  259.7 30.8 reduce-scatter.1
  573.3 15.7 all-gather.1
where the time goes:
time: 943 us; the launch traced here: 929 us
  local copies, waits for them, and re-layouts  329 us (35%)
  matrix products  258 us (27%)
  other arithmetic  165 us (17%)
  waiting for transfers between devices  123 us (13%)
  starting transfers between devices  35.9 us (4%)
  between operations  16.5 us (2%)
    mul x32, local copies, waits for them, and re-layouts, block_weights(): weight_x[:, :, None] * weight_z[:, None, :]  177 us
    dot_general x16, matrix products, sample_step(): jnp.dot(plane_xz, field_table, precision=HIGHEST)  125 us
    mul x32, other arithmetic, block_weights(): weight_x[:, :, None] * weight_z[:, None, :]  113 us
    dot_general x16, matrix products, deposit_step(): jnp.einsum('pa,py->ay', charged, weight_y, precision=HIGHEST)  87.7 us
    unnamed x57, local copies, waits for them, and re-layouts  36.1 us
    reduce_scatter x1, waiting for transfers between devices, per_device(): density = lax.psum_scatter(deposit, 'sub', scatter_dimension=0, tiled=True)  31 us
    dynamic_slice x80, local copies, waits for them, and re-layouts, per_device(): lax.scan(deposit_step, start_total, (blocked_x, blocked_y, blocked_z, blo...  24.2 us
    all_to_all x1, waiting for transfers between devices, per_device(): lax.all_to_all(xspec_re, 'trk', split_axis=0, concat_axis=1, tiled=True)  19.1 us
  transfers between devices with their start and end apart: 10, of which 9 were waited for; matrix products, arithmetic and copies ran while one was open for 8% of the time, Pallas kernels for 0%

commit v1 on v0

--- a/solution.py
+++ b/solution.py
@@ -2,7 +2,11 @@
 
 import jax
 import jax.numpy as jnp
+import ml_dtypes
+import numpy as np
 from jax import lax
+from jax.experimental import pallas as pl
+from jax.experimental.pallas import tpu as pltpu
 from jax.sharding import PartitionSpec as P
 
 NG = 128
@@ -175,6 +179,562 @@
     return (new_coords, new_momenta)
 
 
+def halves(values):
+    upper = values.astype(jnp.bfloat16)
+    return (upper, (values - upper.astype(jnp.float32)).astype(jnp.bfloat16))
+
+
+def table_halves(table):
+    upper = table.astype(ml_dtypes.bfloat16)
+    lower = (table - upper.astype(np.float64)).astype(ml_dtypes.bfloat16)
+    return (jnp.asarray(upper), jnp.asarray(lower))
+
+
+def mm(left, right):
+    return jnp.dot(left, right, preferred_element_type=jnp.float32)
+
+
+def mm_t(left, right):
+    return lax.dot_general(left, right, (((1,), (1,)), ((), ())), preferred_element_type=jnp.float32)
+
+
+def mm3(left, right):
+    return mm(left[0], right[0]) + (mm(left[0], right[1]) + mm(left[1], right[0]))
+
+
+def turn_blocks(parts):
+    lanes = lax.broadcasted_iota(jnp.int32, parts[0].shape, 1)
+    low = lanes < 64
+    even = (lanes // 32) % 2 == 0
+    pairs = []
+    for first, second in ((parts[0], parts[2]), (parts[1], parts[3])):
+        pairs.append(
+            (
+                jnp.where(low, first, pltpu.roll(second, 64, 1)),
+                jnp.where(low, pltpu.roll(first, 64, 1), second),
+            )
+        )
+    result = []
+    for half in (0, 1):
+        first, second = pairs[0][half], pairs[1][half]
+        result.append(jnp.where(even, first, pltpu.roll(second, 32, 1)))
+        result.append(jnp.where(even, pltpu.roll(first, 96, 1), second))
+    return result
+
+
+def tent(places, cells, fraction):
+    away = places - cells
+    return jnp.where(away == 0.0, 1.0 - fraction, jnp.where(away == 1.0, fraction, 0.0))
+
+
+QUAD = 4
+PLANES = 5
+WIDE = 32
+GROUPS = 9
+SLOTS = 4 * GROUPS
+FWD_ROWS = GROUPS * 2 * QUAD
+BACK_ROWS = FWD_ROWS + 24
+LOT = 512
+PACK = 256
+BIG = 56 * 1024 * 1024
+
+
+def deposit_block(acc_ref, rows, zoff, count):
+    y_ids = lax.broadcasted_iota(jnp.int32, (NG, LOT), 0).astype(jnp.float32)
+    weight_x = halves(tent(y_ids, rows[0:1], rows[3:4]))
+    right = jnp.concatenate([weight_x[0], weight_x[1]], axis=0)
+    weight_y = tent(y_ids, rows[1:2], rows[4:5])
+    cell_z = rows[2:3] - zoff
+    for z in range(count):
+        here = float(z)
+        weight_z = jnp.where(
+            cell_z == here, 1.0 - rows[5:6], jnp.where(cell_z == here - 1.0, rows[5:6], 0.0)
+        )
+        left = halves(weight_y * weight_z)
+        acc_ref[z * NG : (z + 1) * NG, :] += mm_t(left[0], right) + mm_t(left[1], right)
+
+
+def deposit_own(place_ref, rows_ref, acc_ref):
+    acc_ref[...] = jnp.zeros_like(acc_ref)
+    zoff = (place_ref[0] * QUAD).astype(jnp.float32)
+
+    def step(lot, carry):
+        rows = rows_ref[:, pl.ds(pl.multiple_of(lot * LOT, LOT), LOT)]
+        deposit_block(acc_ref, rows, zoff, PLANES)
+        return carry
+
+    lax.fori_loop(0, rows_ref.shape[1] // LOT, step, 0)
+
+
+def deposit_rest(place_ref, rows_ref, start_ref, dens_ref, acc_ref):
+    acc_ref[...] = start_ref[...]
+    me = place_ref[0]
+    members = rows_ref.shape[0] // 8
+    zoff = (me * QUAD).astype(jnp.float32)
+    lots = rows_ref.shape[1] // LOT
+
+    def step(item, carry):
+        owner = lax.rem(me + 1 + item // lots, members)
+        lot = lax.rem(item, lots)
+        rows = rows_ref[
+            pl.ds(pl.multiple_of(owner * 8, 8), 8), pl.ds(pl.multiple_of(lot * LOT, LOT), LOT)
+        ]
+        deposit_block(acc_ref, rows, zoff, PLANES)
+        return carry
+
+    lax.fori_loop(0, lots * (members - 1), step, 0)
+    dens_ref[...] = acc_ref[:, 0:NG] + acc_ref[:, NG : 2 * NG]
+
+
+def forward_planes(dens_ref, rim_ref, ty_hi, ty_lo, tx_hi, tx_lo, out_ref, left_ref, right_ref):
+    half = 16 * GROUPS
+    for z in range(QUAD):
+        plane = dens_ref[z * NG : (z + 1) * NG, :]
+        if z == 0:
+            plane = plane + rim_ref[...]
+        lines = mm3((ty_hi[...], ty_lo[...]), halves(plane))
+        real, imag = lines[0:half], lines[half : 2 * half]
+        left_ref[pl.ds(2 * z, half, stride=8), :] = real
+        right_ref[pl.ds(2 * z, half, stride=8), :] = imag
+        left_ref[pl.ds(2 * z + 1, half, stride=8), :] = imag
+        right_ref[pl.ds(2 * z + 1, half, stride=8), :] = -real
+    for s in range(4):
+        whole = []
+        for i in range(4):
+            start = (i * 4 + s) * FWD_ROWS
+            piece = slice(start, start + FWD_ROWS)
+            lines = jnp.concatenate([left_ref[piece, :], right_ref[piece, :]], axis=1)
+            whole.append(mm3(halves(lines), (tx_hi[...], tx_lo[...])))
+        for th in range(2):
+            turned = turn_blocks([part[:, th * NG : (th + 1) * NG] for part in whole])
+            for t in range(4):
+                out_ref[(th * 4 + t) * 4 + s] = turned[t]
+
+
+def green_pairs(own_ref, far_ref, edge_ref, pick_ref, out_ref, *parts):
+    for side in range(2):
+        lanes = slice(side * NG, (side + 1) * NG)
+        parts[side][...] = own_ref[:, lanes]
+        parts[2 + side][...] = far_ref[:, lanes]
+
+    def pull(refs, start, stride):
+        return jnp.concatenate(
+            [ref[pl.ds(start, WIDE, stride=stride), :] for ref in refs], axis=1
+        )
+
+    for group in range(GROUPS):
+        near, away = [], []
+        for i in range(4):
+            j = group * 4 + i
+            if j > WIDE:
+                near.append(jnp.zeros((WIDE, 2 * NG), jnp.float32))
+                away.append(jnp.zeros((WIDE, 2 * NG), jnp.float32))
+                continue
+            near.append(pull(parts[0:2], j, 2 * WIDE))
+            away.append(edge_ref[...] if j == 0 else pull(parts[2:4], WIDE - j, WIDE))
+        both = jnp.concatenate(
+            [jnp.concatenate(near, axis=0), jnp.concatenate(away, axis=0)], axis=1
+        )
+        high = both.astype(jnp.bfloat16)
+        left = both - high.astype(jnp.float32)
+        mid = left.astype(jnp.bfloat16)
+        low = (left - mid.astype(jnp.float32)).astype(jnp.bfloat16)
+        pick = pick_ref[...]
+        out_ref[:, group * NG : (group + 1) * NG] = 0.5 * (
+            mm_t(pick, high) + (mm_t(pick, mid) + mm_t(pick, low))
+        )
+
+
+def spectrum_stage(in_ref, green_ref, wf_hi, wf_lo, wb_hi, wb_lo, out_ref):
+    slabs = in_ref.shape[0]
+    half = 2 * NG
+    for first in range(0, GROUPS, 2):
+        groups = [g for g in (first, first + 1) if g < GROUPS]
+        data = [in_ref[:, g * 8 : (g + 1) * 8, :].reshape(slabs * 8, NG) for g in groups]
+        data = data[0] if len(data) == 1 else jnp.concatenate(data, axis=1)
+        spec = mm3((wf_hi[...], wf_lo[...]), halves(data))
+        green = green_ref[:, first * NG : (first + len(groups)) * NG]
+        scaled = jnp.concatenate([spec[0:half] * green, spec[half : 2 * half] * green], axis=0)
+        back = mm3((wb_hi[...], wb_lo[...]), halves(scaled))
+        for place, g in enumerate(groups):
+            part = back[:, place * NG : (place + 1) * NG]
+            for slab in range(slabs):
+                row = slab * BACK_ROWS + g * 8
+                out_ref[row : row + 8, :] = part[slab * 8 : slab * 8 + 8]
+            for c in range(2):
+                start = slabs * (8 + c)
+                out_ref[pl.ds(FWD_ROWS + 2 * g + c, slabs, stride=BACK_ROWS), :] = part[
+                    start : start + slabs
+                ]
+    for row in range(FWD_ROWS + 2 * GROUPS, BACK_ROWS):
+        out_ref[pl.ds(row, slabs, stride=BACK_ROWS), :] = jnp.zeros((slabs, NG), jnp.float32)
+
+
+def inverse_planes(
+    in_ref, tx_hi, tx_lo, ty_hi, ty_lo, te_hi, te_lo, out_ref, mid_cos, mid_sin, top_cos, top_sin
+):
+    extra = BACK_ROWS - FWD_ROWS
+    for s in range(4):
+        main, rest = [[], [], [], []], [[], [], [], []]
+        for th in range(2):
+            parts = [in_ref[(th * 4 + t) * 4 + s, 0:FWD_ROWS, :] for t in range(4)]
+            tops = [in_ref[(th * 4 + t) * 4 + s, FWD_ROWS:BACK_ROWS, :] for t in range(4)]
+            for i, block in enumerate(turn_blocks(parts)):
+                main[i].append(block)
+            for i, block in enumerate(turn_blocks(tops)):
+                rest[i].append(block)
+        for i in range(4):
+            row = (i * 4 + s) * FWD_ROWS
+            lines = jnp.concatenate(main[i], axis=1)
+            lines = mm3(halves(lines), (tx_hi[...], tx_lo[...]))
+            mid_cos[row : row + FWD_ROWS, :] = lines[:, 0:NG]
+            mid_sin[row : row + FWD_ROWS, :] = lines[:, NG : 2 * NG]
+            row = (i * 4 + s) * extra
+            lines = jnp.concatenate(rest[i], axis=1)
+            lines = mm3(halves(lines), (tx_hi[...], tx_lo[...]))
+            top_cos[row : row + extra, :] = lines[:, 0:NG]
+            top_sin[row : row + extra, :] = lines[:, NG : 2 * NG]
+
+    def finish(cos_ref, sin_ref, start, count, stride, table):
+        real, imag = pl.ds(start, count, stride=stride), pl.ds(start + 1, count, stride=stride)
+        lines = jnp.concatenate(
+            [cos_ref[real, :] - sin_ref[imag, :], sin_ref[real, :] + cos_ref[imag, :]], axis=0
+        )
+        return mm3((table[0][...], table[1][...]), halves(lines))
+
+    for z in range(QUAD):
+        out_ref[z] = finish(mid_cos, mid_sin, 2 * z, 16 * GROUPS, 8, (ty_hi, ty_lo))
+    out_ref[QUAD] = finish(top_cos, top_sin, 0, 8 * extra, 2, (te_hi, te_lo))
+
+
+SORT_BITS = 13
+
+
+def sort_network(items):
+    shape = (8, NG)
+    lanes = lax.broadcasted_iota(jnp.int32, shape, 1)
+    subs = lax.broadcasted_iota(jnp.int32, shape, 0)
+    ranks = [
+        v + subs * 8 + (lanes // 64) * 64 + (lanes % 64) * 128 for v in range(8)
+    ]
+
+    def across(values, bit):
+        if bit < 3:
+            return [values[v ^ (1 << bit)] for v in range(8)]
+        if bit < 6:
+            index = subs ^ (1 << (bit - 3))
+            return [jnp.take_along_axis(value, index, axis=0) for value in values]
+        index = lanes ^ (64 if bit == 6 else 1 << (bit - 7))
+        return [jnp.take_along_axis(value, index, axis=1) for value in values]
+
+    for size in range(SORT_BITS):
+        for bit in range(size, -1, -1):
+            others = [across(item, bit) for item in items]
+            fresh = [[] for _ in items]
+            for v in range(8):
+                keep = (((ranks[v] >> bit) ^ (ranks[v] >> (size + 1))) & 1) == 0
+                take = (others[0][v] < items[0][v]) == keep
+                for n in range(len(items)):
+                    fresh[n].append(jnp.where(take, others[n][v], items[n][v]))
+            items = fresh
+    return items
+
+
+def laid_out(values):
+    turned = jnp.transpose(jnp.concatenate(values, axis=0), (1, 0))
+    return jnp.concatenate([turned[0:64], turned[64:128]], axis=1)
+
+
+def sort_particles(cells_ref, offs_ref, out_int, out_off):
+    shape = (8, NG)
+    lanes = lax.broadcasted_iota(jnp.int32, shape, 1)
+    subs = lax.broadcasted_iota(jnp.int32, shape, 0)
+    keys, packs, offs = [], [], [[], [], []]
+    for v in range(8):
+        rows = slice(v * 8, v * 8 + 8)
+        label = (
+            (subs + v * 8) * 128 + (lanes // 64) * 64 + (lanes % 8) * 8 + (lanes // 8) % 8
+        )
+        keys.append(cells_ref[1, rows, :] * 8192 + label)
+        packs.append(cells_ref[0, rows, :] * 64 + cells_ref[2, rows, :])
+        for d in range(3):
+            offs[d].append(offs_ref[d, rows, :])
+    items = [laid_out(item) for item in sort_network([keys, packs] + offs)]
+    out_int[0] = items[0] // 8192
+    out_int[1] = items[0] % 8192
+    out_int[2] = items[1] // 64
+    out_int[3] = items[1] % 64
+    for d in range(3):
+        out_off[d] = items[2 + d]
+
+
+def sample(low_ref, high_ref, pot_ref, int_ref, off_ref, out_ref, field_ref, kick_ref):
+    depth = field_ref.shape[1]
+    rows = lax.broadcasted_iota(jnp.int32, (NG, NG), 0)
+    lanes = lax.broadcasted_iota(jnp.int32, (NG, NG), 1)
+    for z in range(depth):
+        plane = pot_ref[z + 1]
+        right = jnp.where(lanes == NG - 1, 0.0, pltpu.roll(plane, NG - 1, 1))
+        left = jnp.where(lanes == 0, 0.0, pltpu.roll(plane, 1, 1))
+        field_ref[0, z] = -0.5 * (right - left)
+        right = jnp.where(rows == NG - 1, 0.0, pltpu.roll(plane, NG - 1, 0))
+        left = jnp.where(rows == 0, 0.0, pltpu.roll(plane, 1, 0))
+        field_ref[1, z] = -0.5 * (right - left)
+        field_ref[2, z] = -0.5 * (pot_ref[z + 2] - pot_ref[z])
+
+    x_ids = lax.broadcasted_iota(jnp.int32, (NG, PACK), 0)
+    z_ids = lax.broadcasted_iota(jnp.int32, (24, PACK), 0)
+    y_ids = lax.broadcasted_iota(jnp.int32, (8, PACK), 0)
+
+    def row(ref, which, pack):
+        return jnp.concatenate(
+            [ref[which, pl.ds(2 * pack, 1), :], ref[which, pl.ds(2 * pack + 1, 1), :]], axis=1
+        )
+
+    def weights(ids, cells, fraction):
+        away = ids - cells
+        return jnp.where(away == 0, 1.0 - fraction, jnp.where(away == 1, fraction, 0.0))
+
+    def pack_step(pack, carry):
+        cell_y = row(int_ref, 0, pack)
+        off_y = row(off_ref, 1, pack)
+        weight_x = halves(weights(x_ids, row(int_ref, 2, pack), row(off_ref, 0, pack)))
+        tall = [jnp.concatenate([part, part], axis=0) for part in weight_x]
+        weight_z = weights(z_ids, row(int_ref, 3, pack), row(off_ref, 2, pack))
+        low = low_ref[pack] // 8
+        high = (high_ref[pack] + 1) // 8
+
+        def chunk_step(chunk, kicks):
+            start = pl.multiple_of(chunk * 8, 8)
+            weight_y = weights(y_ids + start, cell_y, off_y)
+            fresh = []
+            for d in range(3):
+                table = field_ref[d, :, pl.ds(start, 8), :].reshape(depth * 8, NG)
+                part = jnp.concatenate(halves(table), axis=1)
+                lines = mm(part, tall[0]) + mm(part, tall[1])
+                total = lines[0:8] * weight_z[0:1]
+                for z in range(1, depth):
+                    total = total + lines[z * 8 : z * 8 + 8] * weight_z[z : z + 1]
+                fresh.append(kicks[d] + jnp.sum(total * weight_y, axis=0, keepdims=True))
+            return tuple(fresh)
+
+        zero = jnp.zeros((1, PACK), jnp.float32)
+        kicks = lax.fori_loop(low, high + 1, chunk_step, (zero, zero, zero))
+        for d in range(3):
+            kick_ref[d, pl.ds(2 * pack, 1), :] = kicks[d][:, 0:NG]
+            kick_ref[d, pl.ds(2 * pack + 1, 1), :] = kicks[d][:, NG : 2 * NG]
+        return carry
+
+    lax.fori_loop(0, low_ref.shape[0], pack_step, 0)
+    items = [[int_ref[1, v * 8 : v * 8 + 8, :] for v in range(8)]]
+    for d in range(3):
+        items.append([kick_ref[d, v * 8 : v * 8 + 8, :] for v in range(8)])
+    items = sort_network(items)
+    for d in range(3):
+        out_ref[d] = laid_out(items[1 + d])
+
+
+def plane_tables(trk_count, sub_count, unit_charge):
+    doubled = 2 * NG
+    width = doubled // sub_count
+    slots = np.arange(4)[:, None, None] + 4 * np.arange(GROUPS)[None, None, :]
+    slots = np.broadcast_to(slots, (4, sub_count, GROUPS))
+    freq = width * np.arange(sub_count)[None, :, None] + slots
+    used = (slots <= width // 2).astype(np.float64)
+    share = used * np.where((slots == 0) | (slots == width // 2), 1.0, 2.0)
+    cells = np.arange(NG)
+    turn = 2.0 * np.pi / doubled
+    angle = turn * ((freq.reshape(-1)[:, None] * cells[None, :]) % doubled)
+    used = used.reshape(-1)[:, None]
+    share_line = share.reshape(-1)[:, None]
+    ty = np.concatenate([np.cos(angle) * used, -np.sin(angle) * used], axis=0) * unit_charge
+    back = np.concatenate([np.cos(angle) * share_line, -np.sin(angle) * share_line], axis=0)
+    ty_back = back.T / doubled
+    pieces = back.reshape(2, 4 * sub_count, GROUPS, NG)
+    pieces = np.concatenate([pieces, np.zeros((2, 4 * sub_count, 12 - GROUPS, NG))], axis=2)
+    te_back = pieces.reshape(-1, NG).T / doubled
+    angle = turn * ((cells[:, None] * np.arange(doubled)[None, :]) % doubled)
+    tx = np.concatenate([np.cos(angle), np.sin(angle)], axis=0)
+    tx_back = np.concatenate([np.cos(angle).T, np.sin(angle).T], axis=1) / doubled
+    slabs = trk_count * sub_count
+    angle = turn * ((np.arange(doubled)[:, None] * cells[None, :]) % doubled)
+    cos, sin = np.cos(angle), np.sin(angle)
+    wf = np.stack(
+        [np.stack([cos, sin], axis=2), np.stack([-sin, cos], axis=2)], axis=0
+    ).reshape(2 * doubled, 2 * NG)
+    slab = np.arange(slabs)
+    planes = (
+        (slab // sub_count * QUAD * sub_count - 1 + PLANES * (slab % sub_count))[:, None]
+        + np.arange(PLANES)[None, :]
+    )
+    inside = ((planes >= 0) & (planes < NG)).astype(np.float64)[:, :, None] / doubled
+    angle = turn * ((planes[:, :, None] * np.arange(doubled)[None, None, :]) % doubled)
+    cos, sin = np.cos(angle) * inside, np.sin(angle) * inside
+    wb = np.stack([np.concatenate([cos, -sin], axis=2), np.concatenate([sin, cos], axis=2)], axis=2)
+    wb = np.concatenate(
+        [
+            wb[:, :QUAD].reshape(slabs * QUAD * 2, 2 * doubled),
+            wb[:, QUAD, 0],
+            wb[:, QUAD, 1],
+        ],
+        axis=0,
+    )
+    pick = np.zeros((doubled, 2 * doubled))
+    line = np.arange(doubled)
+    pick[line, line] = 1.0
+    pick[line, doubled + (-line) % doubled] = 1.0
+    return ty, tx, wf, wb, tx_back, ty_back, te_back, pick
+
+
+def run(body, shapes, scratch, *args, scalars=0):
+    out_shape = tuple(jax.ShapeDtypeStruct(*shape) for shape in shapes)
+    space = pl.BlockSpec(memory_space=pltpu.VMEM)
+    result = pl.pallas_call(
+        body,
+        out_shape=out_shape,
+        in_specs=[pl.BlockSpec(memory_space=pltpu.SMEM)] * scalars + [space] * (len(args) - scalars),
+        out_specs=tuple(space for _ in out_shape),
+        scratch_shapes=[pltpu.VMEM(*shape) for shape in scratch],
+        compiler_params=pltpu.CompilerParams(vmem_limit_bytes=BIG),
+    )(*args)
+    return result
+
+
+def spread_device(particle_cells, offsets, momenta, live_counts, green_hat, orders, strengths):
+    f32 = jnp.float32
+    trk_count = lax.axis_size("trk")
+    sub_count = lax.axis_size("sub")
+    slabs = trk_count * sub_count
+    slab_depth = NG // trk_count
+    count_here = particle_cells.shape[1]
+    unit_charge = float(NG**3) / float(count_here * slabs)
+    both = ("trk", "sub")
+    tables = plane_tables(trk_count, sub_count, unit_charge)
+    ty, tx, wf, wb, tx_back, ty_back, te_back = [table_halves(table) for table in tables[:7]]
+    pick = jnp.asarray(tables[7].astype(ml_dtypes.bfloat16))
+
+    def flat(t, s):
+        return (t % trk_count) * sub_count + s % sub_count
+
+    pairs = [(t, s) for t in range(trk_count) for s in range(sub_count)]
+    width = green_hat.shape[2]
+    lines = jnp.transpose(green_hat, (0, 2, 1))
+    far = lax.ppermute(
+        lines[:, width // 2 :, :],
+        both,
+        [(flat(t, s), flat(trk_count - 1 - t, sub_count - 1 - s)) for t, s in pairs],
+    )
+    far_row = lax.ppermute(
+        lines[0, width // 2 :, :],
+        both,
+        [(flat(t, s), flat(trk_count - t, sub_count - 1 - s)) for t, s in pairs],
+    )
+    edge = lax.ppermute(
+        lines[:, 0, :],
+        both,
+        [(flat(t, s), flat(trk_count - 1 - t, sub_count - s)) for t, s in pairs],
+    )
+    edge_row = lax.ppermute(
+        lines[0:1, 0, :],
+        both,
+        [(flat(t, s), flat(trk_count - t, sub_count - s)) for t, s in pairs],
+    )
+
+    trk_id = lax.axis_index("trk")
+    place = lax.axis_index("sub").reshape(1)
+    local_z = particle_cells[2] - trk_id * slab_depth
+    row_ids = jnp.arange(count_here, dtype=jnp.int32)
+    live_z = jnp.where(row_ids < live_counts[0], local_z, -100)
+    blank = jnp.zeros((2, count_here), f32)
+    rows = jnp.concatenate(
+        [
+            particle_cells[0:2].astype(f32),
+            live_z.astype(f32)[None],
+            offsets,
+            blank,
+        ],
+        axis=0,
+    )
+    shared = lax.all_gather(rows, "sub", axis=0, tiled=True)
+    acc_shape = ((PLANES * NG, 2 * NG), f32)
+    (start,) = run(deposit_own, [acc_shape], [], place, rows, scalars=1)
+    (dens,) = run(
+        deposit_rest, [((PLANES * NG, NG), f32)], [acc_shape], place, shared, start, scalars=1
+    )
+    rim = lax.ppermute(
+        dens[QUAD * NG :],
+        both,
+        [(flat(t, sub_count - 1), flat(t + 1, 0)) for t in range(trk_count - 1)],
+    )
+    (sent,) = run(
+        forward_planes,
+        [((slabs, FWD_ROWS, NG), f32)],
+        [((16 * FWD_ROWS, NG), f32)] * 2,
+        dens,
+        rim,
+        *ty,
+        *tx,
+    )
+    got = lax.all_to_all(sent, both, split_axis=0, concat_axis=0, tiled=True)
+
+    cells_sq = jnp.concatenate([particle_cells[0:2], local_z[None]], axis=0).reshape(3, 64, NG)
+    offs_sq = offsets.reshape(3, 64, NG)
+    ints, offs = run(
+        sort_particles,
+        [((4, 64, NG), jnp.int32), ((3, 64, NG), f32)],
+        [],
+        cells_sq,
+        offs_sq,
+    )
+    packed = ints[0].reshape(count_here // PACK, PACK)
+    low, high = jnp.min(packed, axis=1), jnp.max(packed, axis=1)
+
+    far = jnp.concatenate([far_row[None], jnp.flip(far[1:], axis=0)], axis=0)
+    edge = jnp.concatenate([edge_row, jnp.flip(edge[1:], axis=0)], axis=0)
+    (green,) = run(
+        green_pairs,
+        [((2 * NG, GROUPS * NG), f32)],
+        [((2 * WIDE * WIDE, NG), f32)] * 2 + [((WIDE * WIDE, NG), f32)] * 2,
+        lines.reshape(-1, 2 * NG),
+        far.reshape(-1, 2 * NG),
+        edge,
+        pick,
+    )
+    (sent,) = run(
+        spectrum_stage, [((slabs * BACK_ROWS, NG), f32)], [], got, green, *wf, *wb
+    )
+    got = lax.all_to_all(
+        sent.reshape(slabs, BACK_ROWS, NG), both, split_axis=0, concat_axis=0, tiled=True
+    )
+    (pot,) = run(
+        inverse_planes,
+        [((PLANES, NG, NG), f32)],
+        [((16 * FWD_ROWS, NG), f32)] * 2 + [((16 * (BACK_ROWS - FWD_ROWS), NG), f32)] * 2,
+        got,
+        *tx_back,
+        *ty_back,
+        *te_back,
+    )
+    pot = lax.all_gather(pot, "sub", axis=0, tiled=True)
+    (kick,) = run(
+        sample,
+        [((3, 64, NG), f32)],
+        [((3, slab_depth + 1, NG, NG), f32), ((3, 64, NG), f32)],
+        low,
+        high,
+        pot,
+        ints,
+        offs,
+        scalars=2,
+    )
+    kick = kick.reshape(3, count_here)
+    push_x, push_y = multipole_push(particle_cells, offsets, orders, strengths)
+    push = jnp.stack([push_x, push_y, jnp.zeros_like(push_x)])
+    new_momenta = momenta + kick + push
+    new_coords = particle_cells.astype(f32) + offsets + new_momenta
+    return (new_coords, new_momenta)
+
+
 def solution(mesh):
     in_specs = (
         P(None, ("trk", "sub")),
@@ -186,6 +746,9 @@
         P(),
     )
     out_specs = (P(None, ("trk", "sub")), P(None, ("trk", "sub")))
+    trk_count, sub_count = mesh.shape["trk"], mesh.shape["sub"]
+    fits = sub_count == 4 and trk_count * WIDE == 2 * NG
+    body = spread_device if fits else per_device
     return jax.shard_map(
-        per_device, mesh=mesh, in_specs=in_specs, out_specs=out_specs, check_vma=False
-    )
+        body, mesh=mesh, in_specs=in_specs, out_specs=out_specs, check_vma=False
+    )

time: 943 us -> 289 us (0.31); the launches traced: 929 us -> 286 us
  local copies, waits for them, and re-layouts: 329 us -> 10.3 us
  matrix products: 258 us -> 0 us
  other arithmetic: 165 us -> 12 us
  Pallas kernels: 0 us -> 115 us
  waiting for transfers between devices: 123 us -> 82.9 us
  starting transfers between devices: 35.9 us -> 50.2 us
    dot_general x44 -> x0, matrix products: 244 us -> none  [the longest x16 125 us: sample_step(): jnp.dot(plane_xz, field_table, precision=HIGHEST)]
    mul x32 -> x0, local copies, waits for them, and re-layouts: 177 us -> none  [block_weights(): weight_x[:, :, None] * weight_z[:, None, :]]
    pallas_call x0 -> x8, Pallas kernels: none -> 115 us  [run(): pl.pallas_call(body, out_shape=out_shape, in_specs=[pl.BlockSpec(memory_s...]
    mul x33 -> x0, other arithmetic: 113 us -> none  [the longest x32 113 us: block_weights(): weight_x[:, :, None] * weight_z[:, None, :]]
    all_to_all x8 -> x2, waiting for transfers between devices: 79.9 us -> 31.3 us  [the longest x1 31.3 us: spread_device(): lax.all_to_all(sent.reshape(slabs, BACK_ROWS, NG), both, split_axis=0, co...]
    ppermute x0 -> x5, waiting for transfers between devices: none -> 38.3 us  [the longest x1 38.3 us: spread_device(): lax.ppermute(lines[:, 0, :], both, [(flat(t, s), flat(trk_count - 1 - t,...]
    all_to_all x8 -> x0, other arithmetic: 35 us -> none  [the longest x1 5.98 us: per_device(): lax.all_to_all(plane_im, 'trk', split_axis=1, concat_axis=0, tiled=True)]
    all_to_all x17 -> x0, local copies, waits for them, and re-layouts: 31.5 us -> none  [the longest x2 7.28 us: per_device(): lax.all_to_all(xspec_im, 'trk', split_axis=0, concat_axis=1, tiled=True)]
  transfers between devices with their start and end apart: 10 -> 9, of which waited for: 9 -> 4; matrix products, arithmetic and copies ran while one was open for 8% -> 5% of each run, Pallas kernels for 0% -> 10%
where the time goes in v1:
time: 289 us; the launch traced here: 286 us
  Pallas kernels  115 us (40%)
  waiting for transfers between devices  82.9 us (29%)
  starting transfers between devices  50.2 us (17%)
  between operations  15.5 us (5%)
  other arithmetic  12 us (4%)
  local copies, waits for them, and re-layouts  10.3 us (4%)
    pallas_call x8, Pallas kernels, run(): pl.pallas_call(body, out_shape=out_shape, in_specs=[pl.BlockSpec(memory_s...  115 us
    ppermute x1, waiting for transfers between devices, spread_device(): lax.ppermute(lines[:, 0, :], both, [(flat(t, s), flat(trk_count - 1 - t,...  38.3 us
    all_to_all x1, starting transfers between devices, spread_device(): lax.all_to_all(sent.reshape(slabs, BACK_ROWS, NG), both, split_axis=0, co...  31.3 us
    all_to_all x1, waiting for transfers between devices, spread_device(): lax.all_to_all(sent.reshape(slabs, BACK_ROWS, NG), both, split_axis=0, co...  31.3 us
    all_gather x1, waiting for transfers between devices, spread_device(): pot = lax.all_gather(pot, 'sub', axis=0, tiled=True)  11.4 us
    all_to_all x1, starting transfers between devices, spread_device(): got = lax.all_to_all(sent, both, split_axis=0, concat_axis=0, tiled=True)  10.5 us
  transfers between devices with their start and end apart: 9, of which 4 were waited for; matrix products, arithmetic and copies ran while one was open for 5% of the time, Pallas kernels for 10%

profile of v1, /device:TPU:0, one launch (start us, length us, event | category | flops | bytes accessed | tf_op | source)
XLA Modules:
  0.0 286.1 jit_solution(18229510900264486281)
XLA Ops:
  7.2 0.0 all-gather.3.cloned.1.call-start
  7.9 0.9 slice_convert_fusion
  8.8 1.0 fusion.1
  9.8 0.1 pad.10.clone
  9.9 1.7 maximum_maximum_fusion.rows_ref
  11.6 0.0 all-gather.3.cloned.1.call-update
  11.6 17.7 %shard_map.222.start_ref = f32[640,256]{1,0:T(8,128)} custom-call(s32[1]{0:T(128)} %bitcast.1.place_ref, f32[8,8192]{1,0:T(8,128)} %maximum_maximum_fusion.rows_ref), custom_call_target="tpu_custom_call" | custom-call | tf_op jit(solution)/shard_map/pallas_call | solution.py:592
  29.3 1.9 all-gather.3.cloned.1.call-done.rows_ref
  31.2 49.7 %shard_map.223.dens_ref = f32[640,128]{1,0:T(8,128)} custom-call(s32[1]{0:T(128)} %bitcast.1.place_ref, f32[32,8192]{1,0:T(8,128)} %all-gather.3.cloned.1.call-done.rows_ref, f32[640,256]{1,0:T(8,128)} %shard_map.222.start_ref), custom_call_target="tpu_custom_call" | custom-call | tf_op jit(solution)/shard_map/pallas_call | solution.py:592
  80.9 0.8 slice.57
  81.7 0.7 collective-permute-start
  82.4 0.6 copy-done.6
  83.0 4.0 %shard_map.224 = f32[32,72,128]{2,1,0:T(8,128)} custom-call(f32[640,128]{1,0:T(8,128)} %shard_map.223.dens_ref, f32[128,128]{1,0:T(8,128)} %copy-done.6, bf16[288,128]{1,0:T(8,128)(2,1)} %constant.70.clone.ty_hi, bf16[288,128]{1,0:T(8,128)(2,1)} %constant.71.clone.ty_lo, bf16[256,256]{1,0:T(8,128)(2,1)} %constant.72.clone.tx_hi, ...), custom_call_target="tpu_custom_call" | custom-call | tf_op jit(solution)/shard_map/pallas_call | solution.py:592
  87.0 10.5 %all-to-all-start = ((f32[32,72,128]{2,1,0:T(8,128)}), f32[32,72,128]{2,1,0:T(8,128)S(1)}, u32[]{:S(2)}, u32[]{:S(2)}) async-start(f32[32,72,128]{2,1,0:T(8,128)} %shard_map.224), calls=%async_computation | async-start | bytes 2359296 | tf_op jit(solution)/shard_map/all_to_all | solution.py:678
  97.5 1.2 copy.43
  98.7 1.1 slice.59
  99.8 5.2 %collective-permute-start.2 = (f32[32,32,256]{2,0,1:T(8,128)}, f32[32,32,256]{2,0,1:T(8,128)}, u32[]{:S(2)}, u32[]{:S(2)}) collective-permute-start(f32[32,32,256]{2,0,1:T(8,128)} %slice.59), channel_id=1, source_target_pairs={{0,31},{1,30},{2,29},{3,28},{4,27},{5,26},{6,25},{7,24},{8,23},{9,... | collective-permute-start | bytes 3145736 | tf_op jit(solution)/shard_map/ppermute | solution.py:622
  105.0 0.5 collective-permute-start.4
  105.4 1.1 collective-permute-start.1
  106.6 0.6 collective-permute-start.3
  107.2 38.3 %collective-permute-done.4 = f32[32,256]{1,0:T(8,128)S(1)} collective-permute-done((f32[32,256]{1,0:T(8,128)S(1)}, f32[32,256]{1,0:T(8,128)S(1)}, u32[]{:S(2)}, u32[]{:S(2)}) %collective-permute-start.4) | collective-permute-done | bytes 32800 | tf_op jit(solution)/shard_map/ppermute | solution.py:632
  145.6 0.1 rev.9
  145.7 0.6 pad_maximum_fusion.1.edge_ref
  146.3 1.4 slice.60
  147.7 0.4 rev.8
  148.1 0.2 pad_maximum_fusion
  148.3 1.6 copy.33
  149.9 6.0 %shard_map.225.green_ref = f32[256,1152]{1,0:T(8,128)} custom-call(f32[2048,256]{1,0:T(8,128)} %bitcast.33, f32[1024,256]{1,0:T(8,128)} %bitcast.39, f32[32,256]{1,0:T(8,128)} %pad_maximum_fusion.1.edge_ref, bf16[256,512]{1,0:T(8,128)(2,1)} %constant.84.clone.pick_ref), custom_call_target="tpu_custom_call" | custom-call | tf_op jit(solution)/shard_map/pallas_call | solution.py:592
  155.8 1.0 copy-done.2
  156.8 5.8 %shard_map.226 = f32[3072,128]{1,0:T(8,128)} custom-call(f32[32,72,128]{2,1,0:T(8,128)} %copy-done.2, f32[256,1152]{1,0:T(8,128)} %shard_map.225.green_ref, bf16[512,256]{1,0:T(8,128)(2,1)} %constant.74.clone.wf_hi, bf16[512,256]{1,0:T(8,128)(2,1)} %constant.75.clone.wf_lo, bf16[320,512]{1,0:T(8,128)(2,1)} %constant.76.clone.wb_hi, ...), custom_call_target="tpu_custom_call" | custom-call | tf_op jit(solution)/shard_map/pallas_call | solution.py:592
  162.7 31.3 %all-to-all-start.1 = ((f32[32,96,128]{2,1,0:T(8,128)}), f32[32,96,128]{2,1,0:T(8,128)S(1)}, u32[]{:S(2)}, u32[]{:S(2)}) async-start(f32[32,96,128]{2,1,0:T(8,128)} %bitcast.35), calls=%async_computation.1 | async-start | bytes 3145728 | tf_op jit(solution)/shard_map/all_to_all | solution.py:706
  194.0 0.2 all-gather.5.cloned.1.call-start
  194.3 0.7 copy.44
  194.9 0.6 pad_add_fusion.cells_ref
  195.6 4.7 %shard_map.221 = (s32[4,64,128]{2,1,0:T(8,128)}, f32[3,64,128]{2,1,0:T(8,128)}) custom-call(s32[3,64,128]{2,1,0:T(8,128)} %pad_add_fusion.cells_ref, f32[3,64,128]{2,1,0:T(8,128)} %bitcast.41), custom_call_target="tpu_custom_call" | custom-call | tf_op jit(solution)/shard_map/pallas_call | solution.py:592
  200.3 31.3 %all-to-all-done.1.in_ref = f32[32,96,128]{2,1,0:T(8,128)S(1)} async-done(((f32[32,96,128]{2,1,0:T(8,128)}), f32[32,96,128]{2,1,0:T(8,128)S(1)}, u32[]{:S(2)}, u32[]{:S(2)}) %all-to-all-start.1) | async-done | bytes 1572896 | tf_op jit(solution)/shard_map/all_to_all | solution.py:706
  231.5 1.2 copy-done.1
  232.7 5.2 %shard_map.227 = f32[5,128,128]{2,1,0:T(8,128)} custom-call(f32[32,96,128]{2,1,0:T(8,128)} %copy-done.1, bf16[256,256]{1,0:T(8,128)(2,1)} %constant.78.clone.tx_hi, bf16[256,256]{1,0:T(8,128)(2,1)} %constant.79.clone.tx_lo, bf16[128,288]{1,0:T(8,128)(2,1)} %constant.80.clone.ty_hi, bf16[128,288]{1,0:T(8,128)(2,1)} %constant.81.clone.ty_lo, ...), custom_call_target="tpu_custom_call" | custom-call | tf_op jit(solution)/shard_map/pallas_call | solution.py:592
  238.0 0.9 slice_reduce_fusion
  238.9 0.1 reduce_max.14
  239.0 0.1 reduce_min.14
  239.1 0.6 reduce_max.18.high_ref
  239.7 0.7 reduce_min.18.low_ref
  240.4 0.7 fusion.2
  241.7 2.3 multiply_subtract_fusion
  244.0 11.4 %all-gather.5.cloned.1.call-done.pot_ref = f32[20,128,128]{2,1,0:T(8,128)} async-done(((f32[5,128,128]{2,1,0:T(8,128)}), f32[20,128,128]{2,1,0:T(8,128)}) %all-gather.5.cloned.1.call-update) | async-done | bytes 1310736 | tf_op jit(solution)/shard_map/all_gather | solution.py:718
  255.4 22.0 %shard_map.228 = f32[3,64,128]{2,1,0:T(8,128)} custom-call(s32[32]{0:T(128)} %reduce_min.18.low_ref, s32[32]{0:T(128)} %reduce_max.18.high_ref, f32[20,128,128]{2,1,0:T(8,128)} %all-gather.5.cloned.1.call-done.pot_ref, s32[4,64,128]{2,1,0:T(8,128)} %get-tuple-element.4.int_ref, f32[3,64,128]{2,1,0:T(8,128)} %get-tuple-element.5.off_ref), custom_call_target="tpu_custom_call" | custom-call | tf_op jit(solution)/shard_map/pallas_call | solution.py:592
  277.4 1.8 add_add_fusion
  (29 shorter events, 0.1 us)
Async XLA Ops:
  7.2 24.0 %all-gather.3.cloned.1.call-start = ((), (), s32[]{:S(2)}) async-start(), calls=%async_computation.2 | async-start | bytes 1310720 | tf_op jit(solution)/shard_map/all_gather | solution.py:658
  81.7 0.7 collective-permute-start
  82.4 0.6 copy-start.6
  87.0 10.5 %copy-start = (f32[32,256,64]{1,2,0:T(8,128)S(1)}, f32[32,256,64]{1,2,0:T(8,128)}, u32[]{:S(2)}) copy-start(f32[32,256,64]{1,2,0:T(8,128)} %param.26) | copy-start | bytes 6291460
  87.0 68.8 %all-to-all-start = ((f32[32,72,128]{2,1,0:T(8,128)}), f32[32,72,128]{2,1,0:T(8,128)S(1)}, u32[]{:S(2)}, u32[]{:S(2)}) async-start(f32[32,72,128]{2,1,0:T(8,128)} %shard_map.224), calls=%async_computation | async-start | bytes 2359296 | tf_op jit(solution)/shard_map/all_to_all | solution.py:678
  99.8 46.6 %collective-permute-start.2 = (f32[32,32,256]{2,0,1:T(8,128)}, f32[32,32,256]{2,0,1:T(8,128)}, u32[]{:S(2)}, u32[]{:S(2)}) collective-permute-start(f32[32,32,256]{2,0,1:T(8,128)} %slice.59), channel_id=1, source_target_pairs={{0,31},{1,30},{2,29},{3,28},{4,27},{5,26},{6,25},{7,24},{8,23},{9,... | collective-permute-start | bytes 3145736 | tf_op jit(solution)/shard_map/ppermute | solution.py:622
  105.0 40.6 %collective-permute-start.4 = (f32[32,256]{1,0:T(8,128)S(1)}, f32[32,256]{1,0:T(8,128)S(1)}, u32[]{:S(2)}, u32[]{:S(2)}) collective-permute-start(f32[32,256]{1,0:T(8,128)S(1)} %slice_bitcast_fusion.1), channel_id=1, source_target_pairs={{0,28},{1,31},{2,30},{3,29},{4,24},{5,27},{6,26},{7,25},{8,20},{9,... | collective-permute-start | bytes 98312 | tf_op jit(solution)/shard_map/ppermute | solution.py:632
  105.4 40.2 %collective-permute-start.1 = (f32[32,256]{1,0:T(8,128)S(1)}, f32[32,256]{1,0:T(8,128)S(1)}, u32[]{:S(2)}, u32[]{:S(2)}) collective-permute-start(f32[32,256]{1,0:T(8,128)S(1)} %slice_bitcast_fusion.2), channel_id=1, source_target_pairs={{0,3},{1,2},{2,1},{3,0},{4,31},{5,30},{6,29},{7,28},{8,27},{9,26},... | collective-permute-start | bytes 98312 | tf_op jit(solution)/shard_map/ppermute | solution.py:627
  106.6 39.1 %collective-permute-start.3 = (f32[1,256]{1,0:T(1,128)S(1)}, f32[1,256]{1,0:T(1,128)S(1)}, u32[]{:S(2)}, u32[]{:S(2)}) collective-permute-start(f32[1,256]{1,0:T(1,128)S(1)} %slice_bitcast_fusion.3), channel_id=1, source_target_pairs={{0,0},{1,3},{2,2},{3,1},{4,28},{5,31},{6,30},{7,29},{8,24},{9,27},... | collective-permute-start | bytes 3080 | tf_op jit(solution)/shard_map/ppermute | solution.py:637
  155.8 1.0 copy-start.2
  162.7 31.6 %copy-start.3 = (f32[3,8192]{1,0:T(4,128)S(1)}, f32[3,8192]{1,0:T(4,128)}, u32[]{:S(2)}) copy-start(f32[3,8192]{1,0:T(4,128)} %param.23) | copy-start | bytes 294916
  162.7 68.9 %all-to-all-start.1 = ((f32[32,96,128]{2,1,0:T(8,128)}), f32[32,96,128]{2,1,0:T(8,128)S(1)}, u32[]{:S(2)}, u32[]{:S(2)}) async-start(f32[32,96,128]{2,1,0:T(8,128)} %bitcast.35), calls=%async_computation.1 | async-start | bytes 3145728 | tf_op jit(solution)/shard_map/all_to_all | solution.py:706
  194.0 61.4 %all-gather.5.cloned.1.call-start = ((), (), s32[]{:S(2)}) async-start(), calls=%async_computation.3 | async-start | bytes 1638400 | tf_op jit(solution)/shard_map/all_gather | solution.py:718
  195.6 44.8 %copy-start.7 = (f32[4]{0:T(128)S(1)}, f32[4]{0:T(128)}, u32[]{:S(2)}) copy-start(f32[4]{0:T(128)} %param.28) | copy-start | bytes 52
  195.6 44.8 %copy-start.8 = (s32[4]{0:T(128)S(1)}, s32[4]{0:T(128)}, u32[]{:S(2)}) copy-start(s32[4]{0:T(128)} %param.27) | copy-start | bytes 52
  195.6 46.1 %copy-start.4 = (s32[3,8192]{1,0:T(4,128)S(1)}, s32[3,8192]{1,0:T(4,128)}, u32[]{:S(2)}) copy-start(s32[3,8192]{1,0:T(4,128)} %param.22) | copy-start | bytes 294916
  231.5 1.2 copy-start.1
  237.9 39.5 %copy-start.5 = (f32[3,8192]{1,0:T(4,128)S(1)}, f32[3,8192]{1,0:T(4,128)}, u32[]{:S(2)}) copy-start(f32[3,8192]{1,0:T(4,128)} %param.24) | copy-start | bytes 294916
Sparse Core Ops, SparseCore 0:
  11.7 19.4 all-gather.2
  238.1 17.2 all-gather.4

commit v2 on v1

--- a/solution.py
+++ b/solution.py
@@ -224,7 +224,7 @@
 
 def tent(places, cells, fraction):
     away = places - cells
-    return jnp.where(away == 0.0, 1.0 - fraction, jnp.where(away == 1.0, fraction, 0.0))
+    return jnp.where(away == 0, 1.0 - fraction, jnp.where(away == 1, fraction, 0.0))
 
 
 QUAD = 4
@@ -235,63 +235,109 @@
 FWD_ROWS = GROUPS * 2 * QUAD
 BACK_ROWS = FWD_ROWS + 24
 LOT = 512
+SORT_ROWS = 392
+LIST_ROWS = SORT_ROWS + NG
+SPAN = 3
 PACK = 256
 BIG = 56 * 1024 * 1024
 
 
-def deposit_block(acc_ref, rows, zoff, count):
-    y_ids = lax.broadcasted_iota(jnp.int32, (NG, LOT), 0).astype(jnp.float32)
-    weight_x = halves(tent(y_ids, rows[0:1], rows[3:4]))
-    right = jnp.concatenate([weight_x[0], weight_x[1]], axis=0)
-    weight_y = tent(y_ids, rows[1:2], rows[4:5])
-    cell_z = rows[2:3] - zoff
-    for z in range(count):
-        here = float(z)
-        weight_z = jnp.where(
-            cell_z == here, 1.0 - rows[5:6], jnp.where(cell_z == here - 1.0, rows[5:6], 0.0)
+def long_row(ref, start, count):
+    return jnp.concatenate([ref[pl.ds(start + n, 1), :] for n in range(count)], axis=1)
+
+
+def deposit_lots(acc_ref, rows_ref, base, ends_ref, me, bottom, top):
+    span = LOT // NG
+    ids = lax.broadcasted_iota(jnp.int32, (NG, LOT), 0).astype(jnp.float32)
+
+    def step(lot, carry):
+        low = ends_ref[0, lot * span].astype(jnp.int32) - me * QUAD
+        high = ends_ref[1, lot * span + span - 1].astype(jnp.int32) + 1 - me * QUAD
+        low = jnp.maximum(low, bottom)
+        high = jnp.minimum(high, top)
+        size = min(SPAN, top - bottom + 1)
+
+        @pl.when(low <= high)
+        def _():
+            cell_x, cell_y, cell_z, off_x, off_y, off_z = [
+                long_row(rows_ref, base + which * 64 + lot * span, span) for which in range(6)
+            ]
+            right = jnp.concatenate(halves(tent(ids, cell_x, off_x)), axis=0)
+            weight_y = tent(ids, cell_y, off_y)
+
+            def window(turn, inner):
+                start = low + turn * size
+                away = (start + me * QUAD).astype(jnp.float32) - cell_z
+                left = []
+                for z in range(size):
+                    left.extend(halves(weight_y * tent(away + float(z), 0.0, off_z)))
+                lines = mm_t(jnp.concatenate(left, axis=0), right)
+                for z in range(size):
+                    place = pl.ds(pl.multiple_of((start + z - bottom) * NG, NG), NG)
+                    part = lines[2 * z * NG : (2 * z + 2) * NG]
+                    acc_ref[place, :] += part[0:NG] + part[NG : 2 * NG]
+                return inner
+
+            lax.fori_loop(0, (high - low) // size + 1, window, 0)
+
+        return carry
+
+    lax.fori_loop(0, 64 // span, step, 0)
+
+
+ACC_PLANES = QUAD + SPAN - 1
+ENDS = slice(6 * 64, 6 * 64 + 8)
+
+
+def deposit_own(place_ref, rows_ref, acc_ref, ends_ref, sem):
+    ends = pltpu.make_async_copy(rows_ref.at[ENDS, :], ends_ref, sem)
+    ends.start()
+    acc_ref[...] = jnp.zeros_like(acc_ref)
+    ends.wait()
+    deposit_lots(acc_ref, rows_ref, 0, ends_ref, place_ref[0], 0, QUAD - 1)
+
+
+def fetch_ends(rows_ref, ends_ref, sem):
+    copies = [
+        pltpu.make_async_copy(
+            rows_ref.at[n * LIST_ROWS + ENDS.start : n * LIST_ROWS + ENDS.stop, :],
+            ends_ref.at[n],
+            sem.at[n],
         )
-        left = halves(weight_y * weight_z)
-        acc_ref[z * NG : (z + 1) * NG, :] += mm_t(left[0], right) + mm_t(left[1], right)
-
-
-def deposit_own(place_ref, rows_ref, acc_ref):
-    acc_ref[...] = jnp.zeros_like(acc_ref)
-    zoff = (place_ref[0] * QUAD).astype(jnp.float32)
-
-    def step(lot, carry):
-        rows = rows_ref[:, pl.ds(pl.multiple_of(lot * LOT, LOT), LOT)]
-        deposit_block(acc_ref, rows, zoff, PLANES)
+        for n in range(4)
+    ]
+    for copy in copies:
+        copy.start()
+    return copies
+
+
+def deposit_rest(place_ref, rows_ref, start_ref, dens_ref, acc_ref, ends_ref, sem):
+    copies = fetch_ends(rows_ref, ends_ref, sem)
+    acc_ref[...] = start_ref[...]
+    for copy in copies:
+        copy.wait()
+    me = place_ref[0]
+
+    def each(turn, carry):
+        n = lax.rem(me + turn, 4)
+        deposit_lots(acc_ref, rows_ref, n * LIST_ROWS, ends_ref.at[n], me, 0, QUAD - 1)
         return carry
 
-    lax.fori_loop(0, rows_ref.shape[1] // LOT, step, 0)
-
-
-def deposit_rest(place_ref, rows_ref, start_ref, dens_ref, acc_ref):
-    acc_ref[...] = start_ref[...]
-    me = place_ref[0]
-    members = rows_ref.shape[0] // 8
-    zoff = (me * QUAD).astype(jnp.float32)
-    lots = rows_ref.shape[1] // LOT
-
-    def step(item, carry):
-        owner = lax.rem(me + 1 + item // lots, members)
-        lot = lax.rem(item, lots)
-        rows = rows_ref[
-            pl.ds(pl.multiple_of(owner * 8, 8), 8), pl.ds(pl.multiple_of(lot * LOT, LOT), LOT)
-        ]
-        deposit_block(acc_ref, rows, zoff, PLANES)
-        return carry
-
-    lax.fori_loop(0, lots * (members - 1), step, 0)
-    dens_ref[...] = acc_ref[:, 0:NG] + acc_ref[:, NG : 2 * NG]
-
-
-def forward_planes(dens_ref, rim_ref, ty_hi, ty_lo, tx_hi, tx_lo, out_ref, left_ref, right_ref):
+    lax.fori_loop(1, 4, each, 0)
+    live = slice(0, QUAD * NG)
+    dens_ref[...] = acc_ref[live, 0:NG] + acc_ref[live, NG : 2 * NG]
+
+
+def forward_planes(lower_ref, dens_ref, list_ref, ty_hi, ty_lo, tx_hi, tx_lo, out_ref, left_ref, right_ref):
     half = 16 * GROUPS
     for z in range(QUAD):
         plane = dens_ref[z * NG : (z + 1) * NG, :]
         if z == 0:
-            plane = plane + rim_ref[...]
+            rims = [
+                list_ref[n * LIST_ROWS + SORT_ROWS : (n + 1) * LIST_ROWS, :] for n in range(4)
+            ]
+            rim = (rims[0] + rims[1]) + (rims[2] + rims[3])
+            plane = plane + jnp.where(lower_ref[0] > 0, rim, 0.0)
         lines = mm3((ty_hi[...], ty_lo[...]), halves(plane))
         real, imag = lines[0:half], lines[half : 2 * half]
         left_ref[pl.ds(2 * z, half, stride=8), :] = real
@@ -311,11 +357,24 @@
                 out_ref[(th * 4 + t) * 4 + s] = turned[t]
 
 
-def green_pairs(own_ref, far_ref, edge_ref, pick_ref, out_ref, *parts):
+def green_send(lines_ref, far_ref, row_ref, edge_ref, last_ref):
+    for k in range(1, WIDE):
+        far_ref[k] = lines_ref[WIDE - k, WIDE : 2 * WIDE, :]
+        edge_ref[k : k + 1, :] = lines_ref[WIDE - k, 0:1, :]
+    far_ref[0] = lines_ref[0, WIDE : 2 * WIDE, :]
+    edge_ref[0:1, :] = lines_ref[0, 0:1, :]
+    row_ref[...] = lines_ref[0, WIDE : 2 * WIDE, :]
+    last_ref[...] = lines_ref[0, 0:8, :]
+
+
+def green_pairs(own_ref, far_ref, row_ref, edge_ref, last_ref, pick_ref, out_ref, *parts):
     for side in range(2):
         lanes = slice(side * NG, (side + 1) * NG)
         parts[side][...] = own_ref[:, lanes]
-        parts[2 + side][...] = far_ref[:, lanes]
+        parts[2 + side][WIDE : WIDE * WIDE, :] = far_ref[WIDE : WIDE * WIDE, lanes]
+        parts[2 + side][0:WIDE, :] = row_ref[:, lanes]
+    first = lax.broadcasted_iota(jnp.int32, (WIDE, 2 * NG), 0) == 0
+    edge = jnp.where(first, jnp.broadcast_to(last_ref[0:1, :], (WIDE, 2 * NG)), edge_ref[...])
 
     def pull(refs, start, stride):
         return jnp.concatenate(
@@ -331,7 +390,7 @@
                 away.append(jnp.zeros((WIDE, 2 * NG), jnp.float32))
                 continue
             near.append(pull(parts[0:2], j, 2 * WIDE))
-            away.append(edge_ref[...] if j == 0 else pull(parts[2:4], WIDE - j, WIDE))
+            away.append(edge if j == 0 else pull(parts[2:4], WIDE - j, WIDE))
         both = jnp.concatenate(
             [jnp.concatenate(near, axis=0), jnp.concatenate(away, axis=0)], axis=1
         )
@@ -408,36 +467,63 @@
 
 
 SORT_BITS = 13
-
-
-def sort_network(items):
+DEAD = 100
+
+
+def sort_network(items, rolled=False):
     shape = (8, NG)
     lanes = lax.broadcasted_iota(jnp.int32, shape, 1)
     subs = lax.broadcasted_iota(jnp.int32, shape, 0)
-    ranks = [
-        v + subs * 8 + (lanes // 64) * 64 + (lanes % 64) * 128 for v in range(8)
-    ]
-
-    def across(values, bit):
+    base = subs * 8 + (lanes // 64) * 64 + (lanes % 64) * 128
+
+    def exchange(items, others, bit, size):
+        fresh = [[] for _ in items]
+        for v in range(8):
+            rank = base + v
+            keep = (((rank >> bit) ^ (rank >> (size + 1))) & 1) == 0
+            take = (others[0][v] < items[0][v]) == keep
+            for n in range(len(items)):
+                fresh[n].append(jnp.where(take, others[n][v], items[n][v]))
+        return fresh
+
+    def near_stage(items, bit, size):
+        others = [[item[v ^ (1 << bit)] for v in range(8)] for item in items]
+        return exchange(items, others, bit, size)
+
+    def far_stage(items, bit, size, index, axis):
+        others = [[jnp.take_along_axis(value, index, axis=axis) for value in item] for item in items]
+        return exchange(items, others, bit, size)
+
+    def far_bit(items, bit, size):
         if bit < 3:
-            return [values[v ^ (1 << bit)] for v in range(8)]
+            return near_stage(items, bit, size)
         if bit < 6:
-            index = subs ^ (1 << (bit - 3))
-            return [jnp.take_along_axis(value, index, axis=0) for value in values]
-        index = lanes ^ (64 if bit == 6 else 1 << (bit - 7))
-        return [jnp.take_along_axis(value, index, axis=1) for value in values]
-
-    for size in range(SORT_BITS):
+            return far_stage(items, bit, size, subs ^ (1 << (bit - 3)), 0)
+        return far_stage(items, bit, size, lanes ^ (64 if bit == 6 else 1 << (bit - 7)), 1)
+
+    for size in range(3 if rolled else SORT_BITS):
         for bit in range(size, -1, -1):
-            others = [across(item, bit) for item in items]
-            fresh = [[] for _ in items]
-            for v in range(8):
-                keep = (((ranks[v] >> bit) ^ (ranks[v] >> (size + 1))) & 1) == 0
-                take = (others[0][v] < items[0][v]) == keep
-                for n in range(len(items)):
-                    fresh[n].append(jnp.where(take, others[n][v], items[n][v]))
-            items = fresh
-    return items
+            items = far_bit(items, bit, size)
+    if not rolled:
+        return items
+
+    def merge(size, items):
+        def lane_step(n, items):
+            bit = size - n
+            index = lanes ^ jnp.where(bit == 6, 64, 1 << jnp.maximum(bit - 7, 0))
+            return far_stage(items, bit, size, index, 1)
+
+        def sub_step(n, items):
+            bit = jnp.minimum(size, 5) - n
+            return far_stage(items, bit, size, subs ^ (1 << (bit - 3)), 0)
+
+        items = lax.fori_loop(0, jnp.maximum(size - 5, 0), lane_step, items)
+        items = lax.fori_loop(0, jnp.minimum(size, 5) - 2, sub_step, items)
+        for bit in (2, 1, 0):
+            items = near_stage(items, bit, size)
+        return items
+
+    return lax.fori_loop(3, SORT_BITS, merge, items)
 
 
 def laid_out(values):
@@ -445,93 +531,173 @@
     return jnp.concatenate([turned[0:64], turned[64:128]], axis=1)
 
 
-def sort_particles(cells_ref, offs_ref, out_int, out_off):
-    shape = (8, NG)
-    lanes = lax.broadcasted_iota(jnp.int32, shape, 1)
-    subs = lax.broadcasted_iota(jnp.int32, shape, 0)
+def sort_labels(v):
+    lanes = lax.broadcasted_iota(jnp.int32, (8, NG), 1)
+    subs = lax.broadcasted_iota(jnp.int32, (8, NG), 0)
+    return (subs + v * 8) * 128 + (lanes // 64) * 64 + (lanes % 8) * 8 + (lanes // 8) % 8
+
+
+def square_up(cells_ref, offs_ref, ints_ref, flts_ref):
+    for k in range(64):
+        lanes = slice(k * NG, (k + 1) * NG)
+        for d in range(3):
+            ints_ref[d, k : k + 1, :] = cells_ref[d : d + 1, lanes]
+            flts_ref[d, k : k + 1, :] = offs_ref[d : d + 1, lanes]
+
+
+def sort_by_z(
+    place_ref,
+    live_ref,
+    cells_ref,
+    offs_ref,
+    out_ref,
+    rim_ref,
+    ints_ref,
+    flts_ref,
+    top_ref,
+    ends_ref,
+    sem,
+):
+    square_up(cells_ref, offs_ref, ints_ref, flts_ref)
+    lanes = lax.broadcasted_iota(jnp.int32, (8, NG), 1)
+    subs = lax.broadcasted_iota(jnp.int32, (8, NG), 0)
     keys, packs, offs = [], [], [[], [], []]
     for v in range(8):
         rows = slice(v * 8, v * 8 + 8)
-        label = (
-            (subs + v * 8) * 128 + (lanes // 64) * 64 + (lanes % 8) * 8 + (lanes // 8) % 8
-        )
-        keys.append(cells_ref[1, rows, :] * 8192 + label)
-        packs.append(cells_ref[0, rows, :] * 64 + cells_ref[2, rows, :])
+        alive = (subs + v * 8) * NG + lanes < live_ref[0]
+        cell_z = jnp.where(alive, ints_ref[2, rows, :] - place_ref[0], DEAD)
+        keys.append(cell_z * 8192 + sort_labels(v))
+        packs.append(ints_ref[0, rows, :] * NG + ints_ref[1, rows, :])
         for d in range(3):
-            offs[d].append(offs_ref[d, rows, :])
+            offs[d].append(flts_ref[d, rows, :])
     items = [laid_out(item) for item in sort_network([keys, packs] + offs)]
-    out_int[0] = items[0] // 8192
-    out_int[1] = items[0] % 8192
-    out_int[2] = items[1] // 64
-    out_int[3] = items[1] % 64
+    cell_z = (items[0] >> 13).astype(jnp.float32)
+    out_ref[0:64, :] = (items[1] >> 7).astype(jnp.float32)
+    out_ref[64:128, :] = (items[1] & (NG - 1)).astype(jnp.float32)
+    out_ref[128:192, :] = cell_z
     for d in range(3):
-        out_off[d] = items[2 + d]
-
-
-def sample(low_ref, high_ref, pot_ref, int_ref, off_ref, out_ref, field_ref, kick_ref):
-    depth = field_ref.shape[1]
+        out_ref[192 + 64 * d : 256 + 64 * d, :] = items[2 + d]
+    ends = jnp.transpose(cell_z, (1, 0))
+    ends = jnp.concatenate([ends[0:1], ends[NG - 1 : NG], jnp.zeros((6, 64), jnp.float32)], axis=0)
+    out_ref[384:392, :] = jnp.concatenate([ends, ends], axis=1)
+    fetch = pltpu.make_async_copy(out_ref.at[ENDS, :], ends_ref, sem)
+    fetch.start()
+    top_ref[...] = jnp.zeros_like(top_ref)
+    fetch.wait()
+    deposit_lots(top_ref, out_ref, 0, ends_ref, 0, 4 * QUAD, 4 * QUAD)
+    rim_ref[...] = top_ref[:, 0:NG] + top_ref[:, NG : 2 * NG]
+
+
+def sort_by_y(place_ref, cells_ref, offs_ref, out_int, out_off, ints_ref, flts_ref):
+    square_up(cells_ref, offs_ref, ints_ref, flts_ref)
+    keys, packs, offs = [], [], [[], [], []]
+    for v in range(8):
+        rows = slice(v * 8, v * 8 + 8)
+        keys.append(ints_ref[1, rows, :] * 8192 + sort_labels(v))
+        packs.append(ints_ref[0, rows, :] * 64 + ints_ref[2, rows, :] - place_ref[0])
+        for d in range(3):
+            offs[d].append(flts_ref[d, rows, :])
+    items = [laid_out(item) for item in sort_network([keys, packs] + offs, rolled=True)]
+    cell_y = items[0] >> 13
+    out_int[0:64, :] = cell_y
+    out_int[64:128, :] = items[0] & 8191
+    out_int[128:192, :] = items[1] >> 6
+    out_int[192:256, :] = items[1] & 63
+    for d in range(3):
+        out_off[d * 64 : d * 64 + 64, :] = items[2 + d]
+    ends = jnp.transpose(cell_y, (1, 0))
+    ends = jnp.concatenate([ends[0:1], ends[NG - 1 : NG], jnp.zeros((6, 64), jnp.int32)], axis=0)
+    out_int[256:264, :] = jnp.concatenate([ends, ends], axis=1)
+
+
+def sample(
+    place_ref,
+    own_ref,
+    core_ref,
+    chip_ref,
+    last_ref,
+    int_ref,
+    off_ref,
+    out_ref,
+    pot_ref,
+    field_ref,
+    kick_ref,
+    ends_ref,
+    sem,
+):
+    ends = pltpu.make_async_copy(int_ref.at[256:264, :], ends_ref, sem)
+    ends.start()
+    me = place_ref[0]
+    for turn, ref in enumerate((own_ref, core_ref, chip_ref, last_ref)):
+        pot_ref[pl.ds((me ^ turn) * PLANES, PLANES)] = ref[...]
+    depth = field_ref.shape[0] // 3
     rows = lax.broadcasted_iota(jnp.int32, (NG, NG), 0)
     lanes = lax.broadcasted_iota(jnp.int32, (NG, NG), 1)
-    for z in range(depth):
+    blank = jnp.zeros((8, NG), jnp.float32)
+
+    def fields(z, carry):
         plane = pot_ref[z + 1]
         right = jnp.where(lanes == NG - 1, 0.0, pltpu.roll(plane, NG - 1, 1))
         left = jnp.where(lanes == 0, 0.0, pltpu.roll(plane, 1, 1))
-        field_ref[0, z] = -0.5 * (right - left)
+        field_ref[z, 0:NG, :] = -0.5 * (right - left)
         right = jnp.where(rows == NG - 1, 0.0, pltpu.roll(plane, NG - 1, 0))
         left = jnp.where(rows == 0, 0.0, pltpu.roll(plane, 1, 0))
-        field_ref[1, z] = -0.5 * (right - left)
-        field_ref[2, z] = -0.5 * (pot_ref[z + 2] - pot_ref[z])
-
+        field_ref[depth + z, 0:NG, :] = -0.5 * (right - left)
+        field_ref[2 * depth + z, 0:NG, :] = -0.5 * (pot_ref[z + 2] - pot_ref[z])
+        for d in range(3):
+            field_ref[d * depth + z, NG : NG + 8, :] = blank
+        return carry
+
+    lax.fori_loop(0, depth, fields, 0)
     x_ids = lax.broadcasted_iota(jnp.int32, (NG, PACK), 0)
     z_ids = lax.broadcasted_iota(jnp.int32, (24, PACK), 0)
     y_ids = lax.broadcasted_iota(jnp.int32, (8, PACK), 0)
-
-    def row(ref, which, pack):
-        return jnp.concatenate(
-            [ref[which, pl.ds(2 * pack, 1), :], ref[which, pl.ds(2 * pack + 1, 1), :]], axis=1
-        )
-
-    def weights(ids, cells, fraction):
-        away = ids - cells
-        return jnp.where(away == 0, 1.0 - fraction, jnp.where(away == 1, fraction, 0.0))
+    span = PACK // NG
+    ends.wait()
 
     def pack_step(pack, carry):
-        cell_y = row(int_ref, 0, pack)
-        off_y = row(off_ref, 1, pack)
-        weight_x = halves(weights(x_ids, row(int_ref, 2, pack), row(off_ref, 0, pack)))
+        first = pack * span
+        cell_y, cell_x, cell_z = [
+            long_row(int_ref, which * 64 + first, span) for which in (0, 2, 3)
+        ]
+        off_x, off_y, off_z = [long_row(off_ref, which * 64 + first, span) for which in range(3)]
+        weight_x = halves(tent(x_ids, cell_x, off_x))
         tall = [jnp.concatenate([part, part], axis=0) for part in weight_x]
-        weight_z = weights(z_ids, row(int_ref, 3, pack), row(off_ref, 2, pack))
-        low = low_ref[pack] // 8
-        high = (high_ref[pack] + 1) // 8
+        weight_z = tent(z_ids, cell_z, off_z)
+        low = ends_ref[0, first]
+        high = ends_ref[1, first + span - 1] + 1
 
         def chunk_step(chunk, kicks):
-            start = pl.multiple_of(chunk * 8, 8)
-            weight_y = weights(y_ids + start, cell_y, off_y)
+            start = low + chunk * 8
+            weight_y = tent(y_ids + start, cell_y, off_y)
+            table = field_ref[:, pl.ds(start, 8), :].reshape(3 * depth * 8, NG)
+            part = jnp.concatenate(halves(table), axis=1)
+            lines = mm(part, tall[0]) + mm(part, tall[1])
             fresh = []
             for d in range(3):
-                table = field_ref[d, :, pl.ds(start, 8), :].reshape(depth * 8, NG)
-                part = jnp.concatenate(halves(table), axis=1)
-                lines = mm(part, tall[0]) + mm(part, tall[1])
-                total = lines[0:8] * weight_z[0:1]
+                total = lines[d * depth * 8 : d * depth * 8 + 8] * weight_z[0:1]
                 for z in range(1, depth):
-                    total = total + lines[z * 8 : z * 8 + 8] * weight_z[z : z + 1]
+                    row = (d * depth + z) * 8
+                    total = total + lines[row : row + 8] * weight_z[z : z + 1]
                 fresh.append(kicks[d] + jnp.sum(total * weight_y, axis=0, keepdims=True))
             return tuple(fresh)
 
         zero = jnp.zeros((1, PACK), jnp.float32)
-        kicks = lax.fori_loop(low, high + 1, chunk_step, (zero, zero, zero))
+        kicks = lax.fori_loop(0, (high - low) // 8 + 1, chunk_step, (zero, zero, zero))
         for d in range(3):
-            kick_ref[d, pl.ds(2 * pack, 1), :] = kicks[d][:, 0:NG]
-            kick_ref[d, pl.ds(2 * pack + 1, 1), :] = kicks[d][:, NG : 2 * NG]
+            for n in range(span):
+                kick_ref[d, pl.ds(first + n, 1), :] = kicks[d][:, n * NG : (n + 1) * NG]
         return carry
 
-    lax.fori_loop(0, low_ref.shape[0], pack_step, 0)
-    items = [[int_ref[1, v * 8 : v * 8 + 8, :] for v in range(8)]]
+    lax.fori_loop(0, 64 // span, pack_step, 0)
+    items = [[int_ref[64 + v * 8 : v * 8 + 72, :] for v in range(8)]]
     for d in range(3):
         items.append([kick_ref[d, v * 8 : v * 8 + 8, :] for v in range(8)])
     items = sort_network(items)
     for d in range(3):
-        out_ref[d] = laid_out(items[1 + d])
+        kick = laid_out(items[1 + d])
+        for k in range(64):
+            out_ref[d : d + 1, k * NG : (k + 1) * NG] = kick[k : k + 1, :]
 
 
 def plane_tables(trk_count, sub_count, unit_charge):
@@ -594,7 +760,9 @@
         out_shape=out_shape,
         in_specs=[pl.BlockSpec(memory_space=pltpu.SMEM)] * scalars + [space] * (len(args) - scalars),
         out_specs=tuple(space for _ in out_shape),
-        scratch_shapes=[pltpu.VMEM(*shape) for shape in scratch],
+        scratch_shapes=[
+            pltpu.VMEM(*shape) if isinstance(shape, tuple) else shape for shape in scratch
+        ],
         compiler_params=pltpu.CompilerParams(vmem_limit_bytes=BIG),
     )(*args)
     return result
@@ -619,87 +787,111 @@
     pairs = [(t, s) for t in range(trk_count) for s in range(sub_count)]
     width = green_hat.shape[2]
     lines = jnp.transpose(green_hat, (0, 2, 1))
-    far = lax.ppermute(
-        lines[:, width // 2 :, :],
-        both,
-        [(flat(t, s), flat(trk_count - 1 - t, sub_count - 1 - s)) for t, s in pairs],
-    )
-    far_row = lax.ppermute(
-        lines[0, width // 2 :, :],
-        both,
-        [(flat(t, s), flat(trk_count - t, sub_count - 1 - s)) for t, s in pairs],
-    )
-    edge = lax.ppermute(
-        lines[:, 0, :],
-        both,
-        [(flat(t, s), flat(trk_count - 1 - t, sub_count - s)) for t, s in pairs],
-    )
-    edge_row = lax.ppermute(
-        lines[0:1, 0, :],
-        both,
-        [(flat(t, s), flat(trk_count - t, sub_count - s)) for t, s in pairs],
-    )
-
-    trk_id = lax.axis_index("trk")
+    half = width // 2
+    far, row, edge, last = run(
+        green_send,
+        [
+            ((width // 2, half, 2 * NG), f32),
+            ((half, 2 * NG), f32),
+            ((width // 2, 2 * NG), f32),
+            ((8, 2 * NG), f32),
+        ],
+        [],
+        lines,
+    )
+
+    def mirrored(value, trk_shift, sub_shift):
+        moves = [
+            (flat(t, s), flat(trk_count - trk_shift - t, sub_count - sub_shift - s))
+            for t, s in pairs
+        ]
+        return lax.ppermute(value, both, moves)
+
+    def partner(value, turn):
+        return lax.ppermute(value, both, [(flat(t, s), flat(t, s ^ turn)) for t, s in pairs])
+
     place = lax.axis_index("sub").reshape(1)
-    local_z = particle_cells[2] - trk_id * slab_depth
-    row_ids = jnp.arange(count_here, dtype=jnp.int32)
-    live_z = jnp.where(row_ids < live_counts[0], local_z, -100)
-    blank = jnp.zeros((2, count_here), f32)
-    rows = jnp.concatenate(
-        [
-            particle_cells[0:2].astype(f32),
-            live_z.astype(f32)[None],
-            offsets,
-            blank,
-        ],
-        axis=0,
-    )
-    shared = lax.all_gather(rows, "sub", axis=0, tiled=True)
-    acc_shape = ((PLANES * NG, 2 * NG), f32)
-    (start,) = run(deposit_own, [acc_shape], [], place, rows, scalars=1)
+    base = (lax.axis_index("trk") * slab_depth).reshape(1)
+    square = [((3, 64, NG), jnp.int32), ((3, 64, NG), f32)]
+    rows, rim = run(
+        sort_by_z,
+        [((SORT_ROWS, NG), f32), ((NG, NG), f32)],
+        square
+        + [((NG, 2 * NG), f32), pltpu.SMEM((8, NG), f32), pltpu.SemaphoreType.DMA],
+        base,
+        live_counts,
+        particle_cells,
+        offsets,
+        scalars=2,
+    )
+    rim = lax.ppermute(rim, both, [(flat(t, s), flat(t + 1, s)) for t, s in pairs])
+    acc_shape = ((ACC_PLANES * NG, 2 * NG), f32)
+    (start,) = run(
+        deposit_own,
+        [acc_shape],
+        [pltpu.SMEM((8, NG), f32), pltpu.SemaphoreType.DMA],
+        place,
+        rows,
+        scalars=1,
+    )
+    rim, start, far, row, edge, last = lax.optimization_barrier(
+        (rim, start, far, row, edge, last)
+    )
+    shared = lax.all_gather(jnp.concatenate([rows, rim], axis=0), "sub", axis=0, tiled=True)
+    far = mirrored(far, 1, 1)
+    row = mirrored(row, 0, 1)
+    edge = mirrored(edge, 1, 0)
+    last = mirrored(last, 0, 0)
+    lower = lax.axis_index("trk") > 0
+    lower = lower & (lax.axis_index("sub") == 0)
+    ends = [pltpu.SMEM((4, 8, NG), f32), pltpu.SemaphoreType.DMA((4,))]
     (dens,) = run(
-        deposit_rest, [((PLANES * NG, NG), f32)], [acc_shape], place, shared, start, scalars=1
-    )
-    rim = lax.ppermute(
-        dens[QUAD * NG :],
-        both,
-        [(flat(t, sub_count - 1), flat(t + 1, 0)) for t in range(trk_count - 1)],
+        deposit_rest,
+        [((QUAD * NG, NG), f32)],
+        [acc_shape] + ends,
+        place,
+        shared,
+        start,
+        scalars=1,
     )
     (sent,) = run(
         forward_planes,
         [((slabs, FWD_ROWS, NG), f32)],
         [((16 * FWD_ROWS, NG), f32)] * 2,
+        lower.astype(jnp.int32).reshape(1),
         dens,
-        rim,
+        shared,
         *ty,
         *tx,
+        scalars=1,
+    )
+    late_cells, late_offs, far, row, edge, last, _ = lax.optimization_barrier(
+        (particle_cells, offsets, far, row, edge, last, sent)
     )
     got = lax.all_to_all(sent, both, split_axis=0, concat_axis=0, tiled=True)
-
-    cells_sq = jnp.concatenate([particle_cells[0:2], local_z[None]], axis=0).reshape(3, 64, NG)
-    offs_sq = offsets.reshape(3, 64, NG)
     ints, offs = run(
-        sort_particles,
-        [((4, 64, NG), jnp.int32), ((3, 64, NG), f32)],
-        [],
-        cells_sq,
-        offs_sq,
-    )
-    packed = ints[0].reshape(count_here // PACK, PACK)
-    low, high = jnp.min(packed, axis=1), jnp.max(packed, axis=1)
-
-    far = jnp.concatenate([far_row[None], jnp.flip(far[1:], axis=0)], axis=0)
-    edge = jnp.concatenate([edge_row, jnp.flip(edge[1:], axis=0)], axis=0)
+        sort_by_y,
+        [((264, NG), jnp.int32), ((192, NG), f32)],
+        square,
+        base,
+        late_cells,
+        late_offs,
+        scalars=1,
+    )
+    push_x, push_y = multipole_push(late_cells, late_offs, orders, strengths)
+    push = jnp.stack([push_x, push_y, jnp.zeros_like(push_x)])
     (green,) = run(
         green_pairs,
         [((2 * NG, GROUPS * NG), f32)],
         [((2 * WIDE * WIDE, NG), f32)] * 2 + [((WIDE * WIDE, NG), f32)] * 2,
         lines.reshape(-1, 2 * NG),
         far.reshape(-1, 2 * NG),
+        row,
         edge,
+        last,
         pick,
     )
+    got, ints, offs, push = lax.optimization_barrier((got, ints, offs, push))
     (sent,) = run(
         spectrum_stage, [((slabs * BACK_ROWS, NG), f32)], [], got, green, *wf, *wb
     )
@@ -715,21 +907,29 @@
         *ty_back,
         *te_back,
     )
-    pot = lax.all_gather(pot, "sub", axis=0, tiled=True)
+    chip_pot = partner(pot, 2)
+    core_pot = partner(pot, 1)
+    last_pot = partner(chip_pot, 1)
+    depth = slab_depth + 1
     (kick,) = run(
         sample,
-        [((3, 64, NG), f32)],
-        [((3, slab_depth + 1, NG, NG), f32), ((3, 64, NG), f32)],
-        low,
-        high,
+        [((3, count_here), f32)],
+        [
+            ((sub_count * PLANES, NG, NG), f32),
+            ((3 * depth, NG + 8, NG), f32),
+            ((3, 64, NG), f32),
+            pltpu.SMEM((8, NG), jnp.int32),
+            pltpu.SemaphoreType.DMA,
+        ],
+        place,
         pot,
+        core_pot,
+        chip_pot,
+        last_pot,
         ints,
         offs,
-        scalars=2,
-    )
-    kick = kick.reshape(3, count_here)
-    push_x, push_y = multipole_push(particle_cells, offsets, orders, strengths)
-    push = jnp.stack([push_x, push_y, jnp.zeros_like(push_x)])
+        scalars=1,
+    )
     new_momenta = momenta + kick + push
     new_coords = particle_cells.astype(f32) + offsets + new_momenta
     return (new_coords, new_momenta)

time: 289 us -> 203 us (0.70); the launches traced: 286 us -> 203 us
  Pallas kernels: 115 us -> 67.1 us
  blocking collectives: 0 us -> 41.7 us
  waiting for transfers between devices: 82.9 us -> 49.9 us
  starting transfers between devices: 50.2 us -> 21.5 us
  local copies, waits for them, and re-layouts: 10.3 us -> 1.84 us
  other arithmetic: 12 us -> 5.39 us
    pallas_call x8 -> x10, Pallas kernels: 115 us -> 67.1 us  [run(): pl.pallas_call(body, out_shape=out_shape, in_specs=[pl.BlockSpec(memory_s...]
    all_to_all x0 -> x1, blocking collectives: none -> 41.7 us  [spread_device(): lax.all_to_all(sent.reshape(slabs, BACK_ROWS, NG), both, split_axis=0, co...]
    all_to_all x1 -> x0, starting transfers between devices: 31.3 us -> none  [spread_device(): lax.all_to_all(sent.reshape(slabs, BACK_ROWS, NG), both, split_axis=0, co...]
    all_to_all x1 -> x0, waiting for transfers between devices: 31.3 us -> none  [spread_device(): lax.all_to_all(sent.reshape(slabs, BACK_ROWS, NG), both, split_axis=0, co...]
    ppermute x5 -> x8, waiting for transfers between devices: 38.3 us -> 10.3 us  [the longest x3 10.3 us: partner(): lax.ppermute(value, both, [(flat(t, s), flat(t, s ^ turn)) for t, s in pa...]
    all_gather x2 -> x1, waiting for transfers between devices: 13.3 us -> 26.8 us  [spread_device(): lax.all_gather(jnp.concatenate([rows, rim], axis=0), 'sub', axis=0, tiled...]
    all_to_all x1, waiting for transfers between devices: 0.01 us -> 12.8 us  [spread_device(): got = lax.all_to_all(sent, both, split_axis=0, concat_axis=0, tiled=True)]
    ppermute x5 -> x8, starting transfers between devices: 8.13 us -> 13.3 us  [the longest x4 9.27 us: mirrored(): return lax.ppermute(value, both, moves)]
  transfers between devices with their start and end apart: 9 -> 10, of which waited for: 4 -> 4; matrix products, arithmetic and copies ran while one was open for 5% -> 1% of each run, Pallas kernels for 10% -> 16%
where the time goes in v2:
time: 203 us
  Pallas kernels  67.1 us (33%)
  waiting for transfers between devices  49.9 us (25%)
  blocking collectives  41.7 us (21%)
  starting transfers between devices  21.5 us (11%)
  between operations  15.6 us (8%)
  other arithmetic  5.39 us (3%)
    pallas_call x10, Pallas kernels, run(): pl.pallas_call(body, out_shape=out_shape, in_specs=[pl.BlockSpec(memory_s...  67.1 us
    all_to_all x1, blocking collectives, spread_device(): lax.all_to_all(sent.reshape(slabs, BACK_ROWS, NG), both, split_axis=0, co...  41.7 us
    all_gather x1, waiting for transfers between devices, spread_device(): lax.all_gather(jnp.concatenate([rows, rim], axis=0), 'sub', axis=0, tiled...  26.8 us
    all_to_all x1, waiting for transfers between devices, spread_device(): got = lax.all_to_all(sent, both, split_axis=0, concat_axis=0, tiled=True)  12.8 us
    ppermute x3, waiting for transfers between devices, partner(): lax.ppermute(value, both, [(flat(t, s), flat(t, s ^ turn)) for t, s in pa...  10.3 us
    ppermute x4, starting transfers between devices, mirrored(): return lax.ppermute(value, both, moves)  9.27 us
    all_to_all x1, starting transfers between devices, spread_device(): got = lax.all_to_all(sent, both, split_axis=0, concat_axis=0, tiled=True)  8.14 us
  transfers between devices with their start and end apart: 10, of which 4 were waited for; matrix products, arithmetic and copies ran while one was open for 1% of the time, Pallas kernels for 16%

profile of v2, /device:TPU:0, one launch (start us, length us, event | category | flops | bytes accessed | tf_op | source)
XLA Modules:
  0.0 203.0 jit_solution(3923996294061152381)
XLA Ops:
  7.2 0.0 all-gather.2.cloned.1.call-start
  7.9 6.2 %shard_map.221 = (f32[392,128]{1,0:T(8,128)}, f32[128,128]{1,0:T(8,128)}) custom-call(s32[1]{0:T(128)} %bitcast.2.place_ref, s32[1]{0:T(128)S(6)} %copy.24.live_ref, s32[3,8192]{1,0:T(4,128)} %cells_ref.2, f32[3,8192]{1,0:T(4,128)} %offs_ref.2), custom_call_target="tpu_custom_call" | custom-call | tf_op jit(solution)/shard_map/pallas_call | solution.py:758
  14.1 3.0 %collective-permute-start = (f32[128,128]{1,0:T(8,128)}, f32[128,128]{1,0:T(8,128)S(1)}, u32[]{:S(2)}, u32[]{:S(2)}) collective-permute-start(f32[128,128]{1,0:T(8,128)} %get-tuple-element.27), channel_id=1, source_target_pairs={{0,4},{1,5},{2,6},{3,7},{4,8},{5,9},{6,10},{7,11},{8,12},{9,13},{1... | collective-permute-start | bytes 196616 | tf_op jit(solution)/shard_map/ppermute | solution.py:827
  17.1 2.7 %shard_map.223 = (f32[32,32,256]{2,1,0:T(8,128)}, f32[32,256]{1,0:T(8,128)}, f32[32,256]{1,0:T(8,128)}, f32[8,256]{1,0:T(8,128)}) custom-call(f32[32,64,256]{2,1,0:T(8,128)} %bitcast.8), custom_call_target="tpu_custom_call" | custom-call | tf_op jit(solution)/shard_map/pallas_call | solution.py:758
  19.8 0.0 copy-start.12
  19.8 0.0 copy-start.13
  19.8 4.3 %shard_map.222.start_ref = f32[768,256]{1,0:T(8,128)} custom-call(s32[1]{0:T(128)} %bitcast.place_ref, f32[392,128]{1,0:T(8,128)} %get-tuple-element.26.rows_ref), custom_call_target="tpu_custom_call" | custom-call | tf_op jit(solution)/shard_map/pallas_call | solution.py:758
  24.2 0.0 collective-permute-done
  24.2 0.0 copy-done.4
  24.2 0.7 pad_maximum_fusion
  24.9 0.0 all-gather.2.cloned.1.call-update
  24.9 3.5 %collective-permute-start.1 = (f32[32,32,256]{2,1,0:T(8,128)}, f32[32,32,256]{2,1,0:T(8,128)S(1)}, u32[]{:S(2)}, u32[]{:S(2)}) collective-permute-start(f32[32,32,256]{2,1,0:T(8,128)} %get-tuple-element.34), channel_id=1, source_target_pairs={{0,31},{1,30},{2,29},{3,28},{4,27},{5,26},{6,25},{7,24},{8,23},{9,... | collective-permute-start | bytes 3145736 | tf_op jit(solution)/shard_map/ppermute | solution.py:808
  28.4 0.0 copy-done.15
  28.4 0.4 collective-permute-start.2
  28.8 4.7 %collective-permute-start.3 = (f32[32,256]{1,0:T(8,128)S(1)}, f32[32,256]{1,0:T(8,128)S(1)}, u32[]{:S(2)}, u32[]{:S(2)}) collective-permute-start(f32[32,256]{1,0:T(8,128)S(1)} %copy-done.14), channel_id=1, source_target_pairs={{0,28},{1,31},{2,30},{3,29},{4,24},{5,27},{6,26},{7,25},{8,20},{9,... | collective-permute-start | bytes 98312 | tf_op jit(solution)/shard_map/ppermute | solution.py:808
  33.5 0.0 copy-done.16
  33.5 0.7 collective-permute-start.4
  34.2 0.7 fusion
  35.5 26.8 %all-gather.2.cloned.1.call-done.rows_ref.list_ref = f32[2080,128]{1,0:T(8,128)} async-done(((f32[520,128]{1,0:T(8,128)}), f32[2080,128]{1,0:T(8,128)}) %all-gather.2.cloned.1.call-update) | async-done | bytes 1064976 | tf_op jit(solution)/shard_map/all_gather | solution.py:840
  62.3 6.9 %shard_map.224.dens_ref = f32[512,128]{1,0:T(8,128)} custom-call(s32[1]{0:T(128)} %bitcast.place_ref, f32[2080,128]{1,0:T(8,128)} %all-gather.2.cloned.1.call-done.rows_ref.list_ref, f32[768,256]{1,0:T(8,128)} %shard_map.222.start_ref), custom_call_target="tpu_custom_call" | custom-call | tf_op jit(solution)/shard_map/pallas_call | solution.py:758
  69.3 4.2 %shard_map.225 = f32[32,72,128]{2,1,0:T(8,128)} custom-call(s32[1]{0:T(128)} %bitcast.1.lower_ref, f32[512,128]{1,0:T(8,128)} %shard_map.224.dens_ref, f32[2080,128]{1,0:T(8,128)} %all-gather.2.cloned.1.call-done.rows_ref.list_ref, bf16[288,128]{1,0:T(8,128)(2,1)} %constant.65.clone.ty_hi, bf16[288,128]{1,0:T(8,128)(2,1)} %constant.66.clone.ty_lo, ...), custom_call_target="tpu_custom_call" | custom-call | tf_op jit(solution)/shard_map/pallas_call | solution.py:758
  73.5 8.1 %all-to-all-start = ((f32[32,72,128]{2,1,0:T(8,128)}), f32[32,72,128]{2,1,0:T(8,128)S(1)}, u32[]{:S(2)}, u32[]{:S(2)}) async-start(f32[32,72,128]{2,1,0:T(8,128)} %shard_map.225), calls=%async_computation | async-start | bytes 2359296 | tf_op jit(solution)/shard_map/all_to_all | solution.py:871
  81.6 0.0 collective-permute-done.4.last_ref
  81.6 0.0 collective-permute-done.2.row_ref
  81.7 0.0 copy-start.9
  81.7 0.0 collective-permute-done.3.edge_ref
  81.7 0.0 collective-permute-done.1
  81.7 0.0 copy-start.3
  81.7 7.6 %shard_map.226 = (s32[264,128]{1,0:T(8,128)}, f32[192,128]{1,0:T(8,128)}) custom-call(s32[1]{0:T(128)} %bitcast.2.place_ref, s32[3,8192]{1,0:T(4,128)} %cells_ref.2, f32[3,8192]{1,0:T(4,128)} %offs_ref.2), custom_call_target="tpu_custom_call" | custom-call | tf_op jit(solution)/shard_map/pallas_call | solution.py:758
  89.3 0.0 copy-start.1
  89.3 0.0 copy-start.2
  89.3 6.1 %shard_map.227.green_ref = f32[256,1152]{1,0:T(8,128)} custom-call(f32[2048,256]{1,0:T(8,128)} %bitcast.9, f32[1024,256]{1,0:T(8,128)} %bitcast.11, f32[32,256]{1,0:T(8,128)} %copy-done.9, f32[32,256]{1,0:T(8,128)} %copy-done.10, f32[8,256]{1,0:T(8,128)} %copy-done.11, bf16[256,512]{1,0:T(8,128)(2,1)} %constant.79.clone.pick_ref), custom_call_target="tpu_custom_call" | custom-call | tf_op jit(solution)/shard_map/pallas_call | solution.py:758
  95.4 2.2 %multiply_subtract_fusion = (f32[1,8192]{1,0:T(1,128)S(1)}, f32[1,8192]{1,0:T(1,128)S(1)}) fusion(f32[]{:T(128)} %get-tuple-element.52, f32[]{:T(128)} %get-tuple-element.53, f32[]{:T(128)} %get-tuple-element.51, f32[]{:T(128)S(6)} %mul.106, f32[3,8192]{1,0:T(4,128)S(1)} %copy-done.1, s32[3,8192]{1,0:T(4,128)S(1)} %copy-done.2), kind=kLoop, calls=%fused_computation.6 | loop fusion | flops 327680 | bytes 196624 | tf_op jit(solution)/shard_map/sub | solution.py:28
  97.6 0.1 pad_maximum_fusion.1
  97.7 12.8 %all-to-all-done.in_ref = f32[32,72,128]{2,1,0:T(8,128)S(1)} async-done(((f32[32,72,128]{2,1,0:T(8,128)}), f32[32,72,128]{2,1,0:T(8,128)S(1)}, u32[]{:S(2)}, u32[]{:S(2)}) %all-to-all-start) | async-done | bytes 1179680 | tf_op jit(solution)/shard_map/all_to_all | solution.py:871
  110.5 1.0 copy-done
  111.5 5.8 %shard_map.228 = f32[3072,128]{1,0:T(8,128)} custom-call(f32[32,72,128]{2,1,0:T(8,128)} %copy-done, f32[256,1152]{1,0:T(8,128)} %shard_map.227.green_ref, bf16[512,256]{1,0:T(8,128)(2,1)} %constant.69.clone.wf_hi, bf16[512,256]{1,0:T(8,128)(2,1)} %constant.70.clone.wf_lo, bf16[320,512]{1,0:T(8,128)(2,1)} %constant.71.clone.wb_hi, ...), custom_call_target="tpu_custom_call" | custom-call | tf_op jit(solution)/shard_map/pallas_call | solution.py:758
  117.4 41.7 %all_to_all.10.in_ref = f32[32,96,128]{2,1,0:T(8,128)} all-to-all(f32[32,96,128]{2,1,0:T(8,128)} %bitcast.10), channel_id=1, replica_groups=mesh['trk'=8,'sub'=4] {'trk','sub'}, dimensions={0} | all-to-all | bytes 3145728 | tf_op jit(solution)/shard_map/all_to_all | solution.py:898
  159.1 5.2 %shard_map.229.own_ref = f32[5,128,128]{2,1,0:T(8,128)} custom-call(f32[32,96,128]{2,1,0:T(8,128)} %all_to_all.10.in_ref, bf16[256,256]{1,0:T(8,128)(2,1)} %constant.73.clone.tx_hi, bf16[256,256]{1,0:T(8,128)(2,1)} %constant.74.clone.tx_lo, bf16[128,288]{1,0:T(8,128)(2,1)} %constant.75.clone.ty_hi, bf16[128,288]{1,0:T(8,128)(2,1)} %constant.76.clone.ty_lo, ...), custom_call_target="tpu_custom_call" | custom-call | tf_op jit(solution)/shard_map/pallas_call | solution.py:758
  164.3 1.0 collective-permute-start.6
  165.3 0.1 collective-permute-start.5
  165.4 8.7 %collective-permute-done.6.chip_ref = f32[5,128,128]{2,1,0:T(8,128)S(1)} collective-permute-done((f32[5,128,128]{2,1,0:T(8,128)}, f32[5,128,128]{2,1,0:T(8,128)S(1)}, u32[]{:S(2)}, u32[]{:S(2)}) %collective-permute-start.6) | collective-permute-done | bytes 327712 | tf_op jit(solution)/shard_map/ppermute | solution.py:811
  174.1 0.0 collective-permute-start.7
  174.1 0.0 collective-permute-done.5.core_ref
  174.1 1.6 collective-permute-done.7.last_ref
  175.7 0.7 copy-done.7
  176.4 18.0 %shard_map.230 = f32[3,8192]{1,0:T(4,128)} custom-call(s32[1]{0:T(128)} %bitcast.place_ref, f32[5,128,128]{2,1,0:T(8,128)} %shard_map.229.own_ref, f32[5,128,128]{2,1,0:T(8,128)} %copy-done.6, f32[5,128,128]{2,1,0:T(8,128)} %copy-done.5, f32[5,128,128]{2,1,0:T(8,128)} %copy-done.7, s32[264,128]{1,0:T(8,128)} %get-tuple-element.47.int_ref, ...), custom_call_target="tpu_custom_call" | custom-call | tf_op jit(solution)/shard_map/pallas_call | solution.py:758
  194.5 1.7 add_add_fusion.1
  (24 shorter events, 0.1 us)
Async XLA Ops:
  7.2 55.2 %all-gather.2.cloned.1.call-start = ((), (), s32[]{:S(2)}) async-start(), calls=%async_computation.2 | async-start | bytes 1331200 | tf_op jit(solution)/shard_map/all_gather | solution.py:840
  14.1 10.0 %collective-permute-start = (f32[128,128]{1,0:T(8,128)}, f32[128,128]{1,0:T(8,128)S(1)}, u32[]{:S(2)}, u32[]{:S(2)}) collective-permute-start(f32[128,128]{1,0:T(8,128)} %get-tuple-element.27), channel_id=1, source_target_pairs={{0,4},{1,5},{2,6},{3,7},{4,8},{5,9},{6,10},{7,11},{8,12},{9,13},{1... | collective-permute-start | bytes 196616 | tf_op jit(solution)/shard_map/ppermute | solution.py:827
  17.1 7.1 %copy-start.4 = (f32[392,128]{1,0:T(8,128)S(1)}, f32[392,128]{1,0:T(8,128)}, u32[]{:S(2)}) copy-start(f32[392,128]{1,0:T(8,128)} %get-tuple-element.26.rows_ref) | copy-start | bytes 602116
  19.8 8.6 %copy-start.15 = (f32[32,256]{1,0:T(8,128)S(1)}, f32[32,256]{1,0:T(8,128)}, u32[]{:S(2)}) copy-start(f32[32,256]{1,0:T(8,128)} %get-tuple-element.35) | copy-start | bytes 98308
  19.8 9.0 %copy-start.14 = (f32[32,256]{1,0:T(8,128)S(1)}, f32[32,256]{1,0:T(8,128)}, u32[]{:S(2)}) copy-start(f32[32,256]{1,0:T(8,128)} %get-tuple-element.36) | copy-start | bytes 98308
  19.8 13.7 %copy-start.16 = (f32[8,256]{1,0:T(8,128)S(1)}, f32[8,256]{1,0:T(8,128)}, u32[]{:S(2)}) copy-start(f32[8,256]{1,0:T(8,128)} %get-tuple-element.37) | copy-start | bytes 24580
  19.8 14.4 %copy-start.12 = (f32[4]{0:T(128)S(1)}, f32[4]{0:T(128)}, u32[]{:S(2)}) copy-start(f32[4]{0:T(128)} %param.28) | copy-start | bytes 52
  19.8 14.4 %copy-start.13 = (s32[4]{0:T(128)S(1)}, s32[4]{0:T(128)}, u32[]{:S(2)}) copy-start(s32[4]{0:T(128)} %param.27) | copy-start | bytes 52
  24.9 56.8 %collective-permute-start.1 = (f32[32,32,256]{2,1,0:T(8,128)}, f32[32,32,256]{2,1,0:T(8,128)S(1)}, u32[]{:S(2)}, u32[]{:S(2)}) collective-permute-start(f32[32,32,256]{2,1,0:T(8,128)} %get-tuple-element.34), channel_id=1, source_target_pairs={{0,31},{1,30},{2,29},{3,28},{4,27},{5,26},{6,25},{7,24},{8,23},{9,... | collective-permute-start | bytes 3145736 | tf_op jit(solution)/shard_map/ppermute | solution.py:808
  28.4 53.2 %collective-permute-start.2 = (f32[32,256]{1,0:T(8,128)S(1)}, f32[32,256]{1,0:T(8,128)S(1)}, u32[]{:S(2)}, u32[]{:S(2)}) collective-permute-start(f32[32,256]{1,0:T(8,128)S(1)} %copy-done.15), channel_id=1, source_target_pairs={{0,3},{1,2},{2,1},{3,0},{4,31},{5,30},{6,29},{7,28},{8,27},{9,26},... | collective-permute-start | bytes 98312 | tf_op jit(solution)/shard_map/ppermute | solution.py:808
  28.8 52.8 %collective-permute-start.3 = (f32[32,256]{1,0:T(8,128)S(1)}, f32[32,256]{1,0:T(8,128)S(1)}, u32[]{:S(2)}, u32[]{:S(2)}) collective-permute-start(f32[32,256]{1,0:T(8,128)S(1)} %copy-done.14), channel_id=1, source_target_pairs={{0,28},{1,31},{2,30},{3,29},{4,24},{5,27},{6,26},{7,25},{8,20},{9,... | collective-permute-start | bytes 98312 | tf_op jit(solution)/shard_map/ppermute | solution.py:808
  33.5 48.1 %collective-permute-start.4 = (f32[8,256]{1,0:T(8,128)S(1)}, f32[8,256]{1,0:T(8,128)S(1)}, u32[]{:S(2)}, u32[]{:S(2)}) collective-permute-start(f32[8,256]{1,0:T(8,128)S(1)} %copy-done.16), channel_id=1, source_target_pairs={{0,0},{1,3},{2,2},{3,1},{4,28},{5,31},{6,30},{7,29},{8,24},{9,27},... | collective-permute-start | bytes 24584 | tf_op jit(solution)/shard_map/ppermute | solution.py:808
  73.5 37.0 %all-to-all-start = ((f32[32,72,128]{2,1,0:T(8,128)}), f32[32,72,128]{2,1,0:T(8,128)S(1)}, u32[]{:S(2)}, u32[]{:S(2)}) async-start(f32[32,72,128]{2,1,0:T(8,128)} %shard_map.225), calls=%async_computation | async-start | bytes 2359296 | tf_op jit(solution)/shard_map/all_to_all | solution.py:871
  81.6 7.6 %copy-start.11 = (f32[8,256]{1,0:T(8,128)}, f32[8,256]{1,0:T(8,128)S(1)}, u32[]{:S(2)}) copy-start(f32[8,256]{1,0:T(8,128)S(1)} %collective-permute-done.4.last_ref) | copy-start | bytes 24580
  81.7 7.6 %copy-start.9 = (f32[32,256]{1,0:T(8,128)}, f32[32,256]{1,0:T(8,128)S(1)}, u32[]{:S(2)}) copy-start(f32[32,256]{1,0:T(8,128)S(1)} %collective-permute-done.2.row_ref) | copy-start | bytes 98308
  81.7 7.6 %copy-start.10 = (f32[32,256]{1,0:T(8,128)}, f32[32,256]{1,0:T(8,128)S(1)}, u32[]{:S(2)}) copy-start(f32[32,256]{1,0:T(8,128)S(1)} %collective-permute-done.3.edge_ref) | copy-start | bytes 98308
  81.7 7.6 %copy-start.3 = (f32[32,32,256]{2,1,0:T(8,128)}, f32[32,32,256]{2,1,0:T(8,128)S(1)}, u32[]{:S(2)}) copy-start(f32[32,32,256]{2,1,0:T(8,128)S(1)} %collective-permute-done.1) | copy-start | bytes 3145732
  89.3 6.1 %copy-start.1 = (f32[3,8192]{1,0:T(4,128)S(1)}, f32[3,8192]{1,0:T(4,128)}, u32[]{:S(2)}) copy-start(f32[3,8192]{1,0:T(4,128)} %offs_ref.2) | copy-start | bytes 294916
  89.3 6.1 %copy-start.2 = (s32[3,8192]{1,0:T(4,128)S(1)}, s32[3,8192]{1,0:T(4,128)}, u32[]{:S(2)}) copy-start(s32[3,8192]{1,0:T(4,128)} %cells_ref.2) | copy-start | bytes 294916
  110.5 1.0 copy-start
  164.3 30.1 %copy-start.8 = (f32[3,8192]{1,0:T(4,128)S(1)}, f32[3,8192]{1,0:T(4,128)}, u32[]{:S(2)}) copy-start(f32[3,8192]{1,0:T(4,128)} %param.24) | copy-start | bytes 294916
  164.3 9.7 %collective-permute-start.6 = (f32[5,128,128]{2,1,0:T(8,128)}, f32[5,128,128]{2,1,0:T(8,128)S(1)}, u32[]{:S(2)}, u32[]{:S(2)}) collective-permute-start(f32[5,128,128]{2,1,0:T(8,128)} %shard_map.229.own_ref), channel_id=1, source_target_pairs={{0,2},{1,3},{2,0},{3,1},{4,6},{5,7},{6,4},{7,5},{8,10},{9,11},{10,... | collective-permute-start | bytes 983048 | tf_op jit(solution)/shard_map/ppermute | solution.py:811
  165.3 8.7 %collective-permute-start.5 = (f32[5,128,128]{2,1,0:T(8,128)}, f32[5,128,128]{2,1,0:T(8,128)S(1)}, u32[]{:S(2)}, u32[]{:S(2)}) collective-permute-start(f32[5,128,128]{2,1,0:T(8,128)} %shard_map.229.own_ref), channel_id=1, source_target_pairs={{0,1},{1,0},{2,3},{3,2},{4,5},{5,4},{6,7},{7,6},{8,9},{9,8},{10,11... | collective-permute-start | bytes 983048 | tf_op jit(solution)/shard_map/ppermute | solution.py:811
  174.1 1.6 copy-start.5
  174.1 1.6 collective-permute-start.7
  174.1 1.6 copy-start.6
  175.7 0.7 copy-start.7
Sparse Core Ops, SparseCore 0:
  25.0 37.2 all-gather.1

commit v3 on v2

--- a/solution.py
+++ b/solution.py
@@ -235,6 +235,7 @@
 FWD_ROWS = GROUPS * 2 * QUAD
 BACK_ROWS = FWD_ROWS + 24
 LOT = 512
+CUTS = (0, 12, WIDE)
 SORT_ROWS = 392
 LIST_ROWS = SORT_ROWS + NG
 SPAN = 3
@@ -357,21 +358,26 @@
                 out_ref[(th * 4 + t) * 4 + s] = turned[t]
 
 
-def green_send(lines_ref, far_ref, row_ref, edge_ref, last_ref):
+def green_send(lines_ref, first_ref, second_ref, row_ref, edge_ref, last_ref):
+    fars = (first_ref, second_ref)
     for k in range(1, WIDE):
-        far_ref[k] = lines_ref[WIDE - k, WIDE : 2 * WIDE, :]
+        piece = int(k >= CUTS[1])
+        fars[piece][k - CUTS[piece]] = lines_ref[WIDE - k, WIDE : 2 * WIDE, :]
         edge_ref[k : k + 1, :] = lines_ref[WIDE - k, 0:1, :]
-    far_ref[0] = lines_ref[0, WIDE : 2 * WIDE, :]
+    first_ref[0] = lines_ref[0, WIDE : 2 * WIDE, :]
     edge_ref[0:1, :] = lines_ref[0, 0:1, :]
     row_ref[...] = lines_ref[0, WIDE : 2 * WIDE, :]
     last_ref[...] = lines_ref[0, 0:8, :]
 
 
-def green_pairs(own_ref, far_ref, row_ref, edge_ref, last_ref, pick_ref, out_ref, *parts):
+def green_pairs(
+    own_ref, first_ref, second_ref, row_ref, edge_ref, last_ref, pick_ref, out_ref, *parts
+):
     for side in range(2):
         lanes = slice(side * NG, (side + 1) * NG)
         parts[side][...] = own_ref[:, lanes]
-        parts[2 + side][WIDE : WIDE * WIDE, :] = far_ref[WIDE : WIDE * WIDE, lanes]
+        for piece, ref in enumerate((first_ref, second_ref)):
+            parts[2 + side][CUTS[piece] * WIDE : CUTS[piece + 1] * WIDE, :] = ref[:, lanes]
         parts[2 + side][0:WIDE, :] = row_ref[:, lanes]
     first = lax.broadcasted_iota(jnp.int32, (WIDE, 2 * NG), 0) == 0
     edge = jnp.where(first, jnp.broadcast_to(last_ref[0:1, :], (WIDE, 2 * NG)), edge_ref[...])
@@ -618,6 +624,10 @@
     last_ref,
     int_ref,
     off_ref,
+    mom_ref,
+    push_ref,
+    home_ref,
+    coord_ref,
     out_ref,
     pot_ref,
     field_ref,
@@ -667,8 +677,8 @@
         low = ends_ref[0, first]
         high = ends_ref[1, first + span - 1] + 1
 
-        def chunk_step(chunk, kicks):
-            start = low + chunk * 8
+        def chunk(turn):
+            start = low + turn * 8
             weight_y = tent(y_ids + start, cell_y, off_y)
             table = field_ref[:, pl.ds(start, 8), :].reshape(3 * depth * 8, NG)
             part = jnp.concatenate(halves(table), axis=1)
@@ -679,17 +689,28 @@
                 for z in range(1, depth):
                     row = (d * depth + z) * 8
                     total = total + lines[row : row + 8] * weight_z[z : z + 1]
-                fresh.append(kicks[d] + jnp.sum(total * weight_y, axis=0, keepdims=True))
-            return tuple(fresh)
-
-        zero = jnp.zeros((1, PACK), jnp.float32)
-        kicks = lax.fori_loop(0, (high - low) // 8 + 1, chunk_step, (zero, zero, zero))
-        for d in range(3):
+                fresh.append(jnp.sum(total * weight_y, axis=0, keepdims=True))
+            return fresh
+
+        for d, kick in enumerate(chunk(0)):
             for n in range(span):
-                kick_ref[d, pl.ds(first + n, 1), :] = kicks[d][:, n * NG : (n + 1) * NG]
+                kick_ref[d, pl.ds(first + n, 1), :] = kick[:, n * NG : (n + 1) * NG]
+        return (low, high, first, chunk)
+
+    def pair_step(pair, carry):
+        packs = [pack_step(2 * pair + n, 0) for n in range(2)]
+        for low, high, first, chunk in packs:
+
+            def more(turn, inner):
+                for d, kick in enumerate(chunk(turn)):
+                    for n in range(span):
+                        kick_ref[d, pl.ds(first + n, 1), :] += kick[:, n * NG : (n + 1) * NG]
+                return inner
+
+            lax.fori_loop(1, (high - low) // 8 + 1, more, 0)
         return carry
 
-    lax.fori_loop(0, 64 // span, pack_step, 0)
+    lax.fori_loop(0, 32 // span, pair_step, 0)
     items = [[int_ref[64 + v * 8 : v * 8 + 72, :] for v in range(8)]]
     for d in range(3):
         items.append([kick_ref[d, v * 8 : v * 8 + 8, :] for v in range(8)])
@@ -698,6 +719,9 @@
         kick = laid_out(items[1 + d])
         for k in range(64):
             out_ref[d : d + 1, k * NG : (k + 1) * NG] = kick[k : k + 1, :]
+    fresh = (mom_ref[...] + out_ref[...]) + push_ref[...]
+    out_ref[...] = fresh
+    coord_ref[...] = home_ref[...] + fresh
 
 
 def plane_tables(trk_count, sub_count, unit_charge):
@@ -788,10 +812,10 @@
     width = green_hat.shape[2]
     lines = jnp.transpose(green_hat, (0, 2, 1))
     half = width // 2
-    far, row, edge, last = run(
+    first, second, row, edge, last = run(
         green_send,
-        [
-            ((width // 2, half, 2 * NG), f32),
+        [((CUTS[n + 1] - CUTS[n], half, 2 * NG), f32) for n in range(2)]
+        + [
             ((half, 2 * NG), f32),
             ((width // 2, 2 * NG), f32),
             ((8, 2 * NG), f32),
@@ -806,6 +830,8 @@
             for t, s in pairs
         ]
         return lax.ppermute(value, both, moves)
+
+    first = mirrored(first, 1, 1)
 
     def partner(value, turn):
         return lax.ppermute(value, both, [(flat(t, s), flat(t, s ^ turn)) for t, s in pairs])
@@ -834,11 +860,11 @@
         rows,
         scalars=1,
     )
-    rim, start, far, row, edge, last = lax.optimization_barrier(
-        (rim, start, far, row, edge, last)
+    rim, start, first, second, row, edge, last = lax.optimization_barrier(
+        (rim, start, first, second, row, edge, last)
     )
     shared = lax.all_gather(jnp.concatenate([rows, rim], axis=0), "sub", axis=0, tiled=True)
-    far = mirrored(far, 1, 1)
+    second = mirrored(second, 1, 1)
     row = mirrored(row, 0, 1)
     edge = mirrored(edge, 1, 0)
     last = mirrored(last, 0, 0)
@@ -865,8 +891,8 @@
         *tx,
         scalars=1,
     )
-    late_cells, late_offs, far, row, edge, last, _ = lax.optimization_barrier(
-        (particle_cells, offsets, far, row, edge, last, sent)
+    late_cells, late_offs, first, second, row, edge, last, _ = lax.optimization_barrier(
+        (particle_cells, offsets, first, second, row, edge, last, sent)
     )
     got = lax.all_to_all(sent, both, split_axis=0, concat_axis=0, tiled=True)
     ints, offs = run(
@@ -885,13 +911,15 @@
         [((2 * NG, GROUPS * NG), f32)],
         [((2 * WIDE * WIDE, NG), f32)] * 2 + [((WIDE * WIDE, NG), f32)] * 2,
         lines.reshape(-1, 2 * NG),
-        far.reshape(-1, 2 * NG),
+        first.reshape(-1, 2 * NG),
+        second.reshape(-1, 2 * NG),
         row,
         edge,
         last,
         pick,
     )
-    got, ints, offs, push = lax.optimization_barrier((got, ints, offs, push))
+    home = late_cells.astype(f32) + late_offs
+    got, ints, offs, push, home = lax.optimization_barrier((got, ints, offs, push, home))
     (sent,) = run(
         spectrum_stage, [((slabs * BACK_ROWS, NG), f32)], [], got, green, *wf, *wb
     )
@@ -911,9 +939,9 @@
     core_pot = partner(pot, 1)
     last_pot = partner(chip_pot, 1)
     depth = slab_depth + 1
-    (kick,) = run(
+    coords, fresh = run(
         sample,
-        [((3, count_here), f32)],
+        [((3, count_here), f32)] * 2,
         [
             ((sub_count * PLANES, NG, NG), f32),
             ((3 * depth, NG + 8, NG), f32),
@@ -928,11 +956,12 @@
         last_pot,
         ints,
         offs,
+        momenta,
+        push,
+        home,
         scalars=1,
     )
-    new_momenta = momenta + kick + push
-    new_coords = particle_cells.astype(f32) + offsets + new_momenta
-    return (new_coords, new_momenta)
+    return (coords, fresh)
 
 
 def solution(mesh):

time: 203 us -> 194 us (0.956)
  waiting for transfers between devices: 49.9 us -> 42.5 us
  Pallas kernels: 67.1 us -> 63 us
  starting transfers between devices: 21.5 us -> 23.7 us
    all_gather x1, waiting for transfers between devices: 26.8 us -> 16.5 us  [spread_device(): lax.all_gather(jnp.concatenate([rows, rim], axis=0), 'sub', axis=0, tiled...]
    ppermute x4 -> x5, starting transfers between devices: 9.27 us -> 17.5 us  [mirrored(): return lax.ppermute(value, both, moves)]
    pallas_call x10, Pallas kernels: 67.1 us -> 63 us  [run(): pl.pallas_call(body, out_shape=out_shape, in_specs=[pl.BlockSpec(memory_s...]
    all_to_all x1, starting transfers between devices: 8.14 us -> 4.55 us  [spread_device(): got = lax.all_to_all(sent, both, split_axis=0, concat_axis=0, tiled=True)]
    ppermute x1, waiting for transfers between devices: 0.01 us -> 3.41 us  [spread_device(): lax.ppermute(rim, both, [(flat(t, s), flat(t + 1, s)) for t, s in pairs])]
    ppermute x1, starting transfers between devices: 2.99 us -> 0.59 us  [spread_device(): lax.ppermute(rim, both, [(flat(t, s), flat(t + 1, s)) for t, s in pairs])]
  transfers between devices with their start and end apart: 10 -> 11, of which waited for: 4 -> 5; matrix products, arithmetic and copies ran while one was open for 1% -> 2% of each run, Pallas kernels for 16% -> 18%
where the time goes in v3:
time: 194 us
  Pallas kernels  63 us (32%)
  waiting for transfers between devices  42.5 us (22%)
  blocking collectives  41.7 us (21%)
  starting transfers between devices  23.7 us (12%)
  between operations  15.6 us (8%)
  other arithmetic  5.46 us (3%)
    pallas_call x10, Pallas kernels, run(): pl.pallas_call(body, out_shape=out_shape, in_specs=[pl.BlockSpec(memory_s...  63 us
    all_to_all x1, blocking collectives, spread_device(): lax.all_to_all(sent.reshape(slabs, BACK_ROWS, NG), both, split_axis=0, co...  41.7 us
    ppermute x5, starting transfers between devices, mirrored(): return lax.ppermute(value, both, moves)  17.5 us
    all_gather x1, waiting for transfers between devices, spread_device(): lax.all_gather(jnp.concatenate([rows, rim], axis=0), 'sub', axis=0, tiled...  16.5 us
    all_to_all x1, waiting for transfers between devices, spread_device(): got = lax.all_to_all(sent, both, split_axis=0, concat_axis=0, tiled=True)  12.3 us
    ppermute x3, waiting for transfers between devices, partner(): lax.ppermute(value, both, [(flat(t, s), flat(t, s ^ turn)) for t, s in pa...  10.3 us
    all_to_all x1, starting transfers between devices, spread_device(): got = lax.all_to_all(sent, both, split_axis=0, concat_axis=0, tiled=True)  4.55 us
  transfers between devices with their start and end apart: 11, of which 5 were waited for; matrix products, arithmetic and copies ran while one was open for 2% of the time, Pallas kernels for 18%

profile of v3, /device:TPU:0, one launch (start us, length us, event | category | flops | bytes accessed | tf_op | source)
XLA Modules:
  0.0 193.9 jit_solution(13731181731037396124)
XLA Ops:
  7.2 0.0 all-gather.2.cloned.1.call-start
  7.2 2.7 %shard_map.223 = (f32[12,32,256]{2,1,0:T(8,128)}, f32[20,32,256]{2,1,0:T(8,128)}, f32[32,256]{1,0:T(8,128)}, f32[32,256]{1,0:T(8,128)}, f32[8,256]{1,0:T(8,128)}) custom-call(f32[32,64,256]{2,1,0:T(8,128)} %bitcast.9), custom_call_target="tpu_custom_call" | custom-call | tf_op jit(solution)/shard_map/pallas_call | solution.py:782
  9.9 0.0 copy-start.16
  9.9 0.0 copy-start.13
  9.9 0.0 copy-start.14
  9.9 6.4 %collective-permute-start.1 = (f32[12,32,256]{2,1,0:T(8,128)}, f32[12,32,256]{2,1,0:T(8,128)S(1)}, u32[]{:S(2)}, u32[]{:S(2)}) collective-permute-start(f32[12,32,256]{2,1,0:T(8,128)} %get-tuple-element.32), channel_id=1, source_target_pairs={{0,31},{1,30},{2,29},{3,28},{4,27},{5,26},{6,25},{7,24},{8,23},{9,... | collective-permute-start | bytes 1179656 | tf_op jit(solution)/shard_map/ppermute | solution.py:832
  17.0 6.2 %shard_map.221 = (f32[392,128]{1,0:T(8,128)}, f32[128,128]{1,0:T(8,128)}) custom-call(s32[1]{0:T(128)} %bitcast.2.place_ref, s32[1]{0:T(128)S(6)} %copy.24.live_ref, s32[3,8192]{1,0:T(4,128)} %cells_ref.2, f32[3,8192]{1,0:T(4,128)} %offs_ref.2), custom_call_target="tpu_custom_call" | custom-call | tf_op jit(solution)/shard_map/pallas_call | solution.py:782
  23.2 0.6 collective-permute-start
  23.8 3.7 %shard_map.222.start_ref = f32[768,256]{1,0:T(8,128)} custom-call(s32[1]{0:T(128)} %bitcast.place_ref, f32[392,128]{1,0:T(8,128)} %get-tuple-element.30.rows_ref), custom_call_target="tpu_custom_call" | custom-call | tf_op jit(solution)/shard_map/pallas_call | solution.py:782
  27.6 3.4 %collective-permute-done = f32[128,128]{1,0:T(8,128)S(1)} collective-permute-done((f32[128,128]{1,0:T(8,128)}, f32[128,128]{1,0:T(8,128)S(1)}, u32[]{:S(2)}, u32[]{:S(2)}) %collective-permute-start) | collective-permute-done | bytes 65568 | tf_op jit(solution)/shard_map/ppermute | solution.py:853
  31.0 0.0 collective-permute-done.1
  31.0 1.8 pad_maximum_fusion
  32.8 0.0 all-gather.2.cloned.1.call-update
  32.8 1.7 collective-permute-start.2
  34.5 0.0 copy-done.18
  34.6 0.7 collective-permute-start.5
  35.2 2.9 %collective-permute-start.3 = (f32[32,256]{1,0:T(8,128)S(1)}, f32[32,256]{1,0:T(8,128)S(1)}, u32[]{:S(2)}, u32[]{:S(2)}) collective-permute-start(f32[32,256]{1,0:T(8,128)S(1)} %copy-done.17), channel_id=1, source_target_pairs={{0,3},{1,2},{2,1},{3,0},{4,31},{5,30},{6,29},{7,28},{8,27},{9,26},... | collective-permute-start | bytes 98312 | tf_op jit(solution)/shard_map/ppermute | solution.py:832
  38.1 5.7 %collective-permute-start.4 = (f32[32,256]{1,0:T(8,128)S(1)}, f32[32,256]{1,0:T(8,128)S(1)}, u32[]{:S(2)}, u32[]{:S(2)}) collective-permute-start(f32[32,256]{1,0:T(8,128)S(1)} %copy-done.16), channel_id=1, source_target_pairs={{0,28},{1,31},{2,30},{3,29},{4,24},{5,27},{6,26},{7,25},{8,20},{9,... | collective-permute-start | bytes 98312 | tf_op jit(solution)/shard_map/ppermute | solution.py:832
  43.9 0.6 fusion
  45.2 16.5 %all-gather.2.cloned.1.call-done.rows_ref.list_ref = f32[2080,128]{1,0:T(8,128)} async-done(((f32[520,128]{1,0:T(8,128)}), f32[2080,128]{1,0:T(8,128)}) %all-gather.2.cloned.1.call-update) | async-done | bytes 1064976 | tf_op jit(solution)/shard_map/all_gather | solution.py:866
  61.7 6.9 %shard_map.224.dens_ref = f32[512,128]{1,0:T(8,128)} custom-call(s32[1]{0:T(128)} %bitcast.place_ref, f32[2080,128]{1,0:T(8,128)} %all-gather.2.cloned.1.call-done.rows_ref.list_ref, f32[768,256]{1,0:T(8,128)} %shard_map.222.start_ref), custom_call_target="tpu_custom_call" | custom-call | tf_op jit(solution)/shard_map/pallas_call | solution.py:782
  68.6 4.2 %shard_map.225 = f32[32,72,128]{2,1,0:T(8,128)} custom-call(s32[1]{0:T(128)} %bitcast.1.lower_ref, f32[512,128]{1,0:T(8,128)} %shard_map.224.dens_ref, f32[2080,128]{1,0:T(8,128)} %all-gather.2.cloned.1.call-done.rows_ref.list_ref, bf16[288,128]{1,0:T(8,128)(2,1)} %constant.65.clone.ty_hi, bf16[288,128]{1,0:T(8,128)(2,1)} %constant.66.clone.ty_lo, ...), custom_call_target="tpu_custom_call" | custom-call | tf_op jit(solution)/shard_map/pallas_call | solution.py:782
  72.8 4.5 %all-to-all-start = ((f32[32,72,128]{2,1,0:T(8,128)}), f32[32,72,128]{2,1,0:T(8,128)S(1)}, u32[]{:S(2)}, u32[]{:S(2)}) async-start(f32[32,72,128]{2,1,0:T(8,128)} %shard_map.225), calls=%async_computation | async-start | bytes 2359296 | tf_op jit(solution)/shard_map/all_to_all | solution.py:897
  77.4 0.0 collective-permute-done.5.last_ref
  77.4 0.0 collective-permute-done.3.row_ref
  77.4 0.0 copy-start.10
  77.4 0.0 collective-permute-done.4.edge_ref
  77.4 0.0 copy-start.11
  77.4 0.0 collective-permute-done.2
  77.5 2.2 %multiply_subtract_fusion = (f32[1,8192]{1,0:T(1,128)S(1)}, f32[1,8192]{1,0:T(1,128)S(1)}) fusion(f32[]{:T(128)} %get-tuple-element.60, f32[]{:T(128)} %get-tuple-element.61, f32[]{:T(128)} %get-tuple-element.59, f32[]{:T(128)S(6)} %mul.106, f32[3,8192]{1,0:T(4,128)S(1)} %copy-done.3, s32[3,8192]{1,0:T(4,128)S(1)} %copy-done.1), kind=kLoop, calls=%fused_computation.5 | loop fusion | flops 327680 | bytes 196624 | tf_op jit(solution)/shard_map/sub | solution.py:28
  79.7 7.3 %shard_map.226 = (s32[264,128]{1,0:T(8,128)}, f32[192,128]{1,0:T(8,128)}) custom-call(s32[1]{0:T(128)} %bitcast.2.place_ref, s32[3,8192]{1,0:T(4,128)} %cells_ref.2, f32[3,8192]{1,0:T(4,128)} %offs_ref.2), custom_call_target="tpu_custom_call" | custom-call | tf_op jit(solution)/shard_map/pallas_call | solution.py:782
  87.0 0.0 copy-start.2
  87.0 0.0 copy-start.4
  87.0 6.1 %shard_map.227.green_ref = f32[256,1152]{1,0:T(8,128)} custom-call(f32[2048,256]{1,0:T(8,128)} %bitcast.10, f32[384,256]{1,0:T(8,128)} %bitcast.13, f32[640,256]{1,0:T(8,128)} %bitcast.12, f32[32,256]{1,0:T(8,128)} %copy-done.10, f32[32,256]{1,0:T(8,128)} %copy-done.11, f32[8,256]{1,0:T(8,128)} %copy-done.12, bf16[256,512]{1,0:T(8,128)(2,1)} %constant.79.clone.pick_ref), custom_call_target="tpu_custom_call" | custom-call | tf_op jit(solution)/shard_map/pallas_call | solution.py:782
  93.2 0.8 pad_maximum_fusion.1
  94.0 12.3 %all-to-all-done.in_ref = f32[32,72,128]{2,1,0:T(8,128)S(1)} async-done(((f32[32,72,128]{2,1,0:T(8,128)}), f32[32,72,128]{2,1,0:T(8,128)S(1)}, u32[]{:S(2)}, u32[]{:S(2)}) %all-to-all-start) | async-done | bytes 1179680 | tf_op jit(solution)/shard_map/all_to_all | solution.py:897
  106.3 1.0 copy-done
  107.3 5.9 %shard_map.228 = f32[3072,128]{1,0:T(8,128)} custom-call(f32[32,72,128]{2,1,0:T(8,128)} %copy-done, f32[256,1152]{1,0:T(8,128)} %shard_map.227.green_ref, bf16[512,256]{1,0:T(8,128)(2,1)} %constant.69.clone.wf_hi, bf16[512,256]{1,0:T(8,128)(2,1)} %constant.70.clone.wf_lo, bf16[320,512]{1,0:T(8,128)(2,1)} %constant.71.clone.wb_hi, ...), custom_call_target="tpu_custom_call" | custom-call | tf_op jit(solution)/shard_map/pallas_call | solution.py:782
  113.2 41.7 %all_to_all.10.in_ref = f32[32,96,128]{2,1,0:T(8,128)} all-to-all(f32[32,96,128]{2,1,0:T(8,128)} %bitcast.11), channel_id=1, replica_groups=mesh['trk'=8,'sub'=4] {'trk','sub'}, dimensions={0} | all-to-all | bytes 3145728 | tf_op jit(solution)/shard_map/all_to_all | solution.py:926
  154.9 5.2 %shard_map.229.own_ref = f32[5,128,128]{2,1,0:T(8,128)} custom-call(f32[32,96,128]{2,1,0:T(8,128)} %all_to_all.10.in_ref, bf16[256,256]{1,0:T(8,128)(2,1)} %constant.73.clone.tx_hi, bf16[256,256]{1,0:T(8,128)(2,1)} %constant.74.clone.tx_lo, bf16[128,288]{1,0:T(8,128)(2,1)} %constant.75.clone.ty_hi, bf16[128,288]{1,0:T(8,128)(2,1)} %constant.76.clone.ty_lo, ...), custom_call_target="tpu_custom_call" | custom-call | tf_op jit(solution)/shard_map/pallas_call | solution.py:782
  160.1 1.0 collective-permute-start.7
  161.1 0.0 collective-permute-start.6
  161.2 8.7 %collective-permute-done.7.chip_ref = f32[5,128,128]{2,1,0:T(8,128)S(1)} collective-permute-done((f32[5,128,128]{2,1,0:T(8,128)}, f32[5,128,128]{2,1,0:T(8,128)S(1)}, u32[]{:S(2)}, u32[]{:S(2)}) %collective-permute-start.7) | collective-permute-done | bytes 327712 | tf_op jit(solution)/shard_map/ppermute | solution.py:837
  169.9 0.0 collective-permute-start.8
  169.9 0.0 collective-permute-done.6.core_ref
  169.9 1.6 collective-permute-done.8.last_ref
  171.5 0.7 copy-done.9
  172.2 14.8 %shard_map.230 = (f32[3,8192]{1,0:T(4,128)}, f32[3,8192]{1,0:T(4,128)}) custom-call(s32[1]{0:T(128)} %bitcast.place_ref, f32[5,128,128]{2,1,0:T(8,128)} %shard_map.229.own_ref, f32[5,128,128]{2,1,0:T(8,128)} %copy-done.8, f32[5,128,128]{2,1,0:T(8,128)} %copy-done.7, f32[5,128,128]{2,1,0:T(8,128)} %copy-done.9, s32[264,128]{1,0:T(8,128)} %get-tuple-element.54.int_ref, ...), custom_call_target="tpu_custom_call" | custom-call | tf_op jit(solution)/shard_map/pallas_call | solution.py:782
  (29 shorter events, 0.1 us)
Async XLA Ops:
  7.2 54.5 %all-gather.2.cloned.1.call-start = ((), (), s32[]{:S(2)}) async-start(), calls=%async_computation.2 | async-start | bytes 1331200 | tf_op jit(solution)/shard_map/all_gather | solution.py:866
  9.9 22.9 %copy-start.15 = (f32[20,32,256]{2,1,0:T(8,128)S(1)}, f32[20,32,256]{2,1,0:T(8,128)}, u32[]{:S(2)}) copy-start(f32[20,32,256]{2,1,0:T(8,128)} %get-tuple-element.40) | copy-start | bytes 1966084
  9.9 24.7 %copy-start.18 = (f32[8,256]{1,0:T(8,128)S(1)}, f32[8,256]{1,0:T(8,128)}, u32[]{:S(2)}) copy-start(f32[8,256]{1,0:T(8,128)} %get-tuple-element.43) | copy-start | bytes 24580
  9.9 25.3 %copy-start.17 = (f32[32,256]{1,0:T(8,128)S(1)}, f32[32,256]{1,0:T(8,128)}, u32[]{:S(2)}) copy-start(f32[32,256]{1,0:T(8,128)} %get-tuple-element.41) | copy-start | bytes 98308
  9.9 28.3 %copy-start.16 = (f32[32,256]{1,0:T(8,128)S(1)}, f32[32,256]{1,0:T(8,128)}, u32[]{:S(2)}) copy-start(f32[32,256]{1,0:T(8,128)} %get-tuple-element.42) | copy-start | bytes 98308
  9.9 34.0 %copy-start.13 = (f32[4]{0:T(128)S(1)}, f32[4]{0:T(128)}, u32[]{:S(2)}) copy-start(f32[4]{0:T(128)} %param.28) | copy-start | bytes 52
  9.9 34.0 %copy-start.14 = (s32[4]{0:T(128)S(1)}, s32[4]{0:T(128)}, u32[]{:S(2)}) copy-start(s32[4]{0:T(128)} %param.27) | copy-start | bytes 52
  9.9 21.1 %collective-permute-start.1 = (f32[12,32,256]{2,1,0:T(8,128)}, f32[12,32,256]{2,1,0:T(8,128)S(1)}, u32[]{:S(2)}, u32[]{:S(2)}) collective-permute-start(f32[12,32,256]{2,1,0:T(8,128)} %get-tuple-element.32), channel_id=1, source_target_pairs={{0,31},{1,30},{2,29},{3,28},{4,27},{5,26},{6,25},{7,24},{8,23},{9,... | collective-permute-start | bytes 1179656 | tf_op jit(solution)/shard_map/ppermute | solution.py:832
  23.2 7.7 %collective-permute-start = (f32[128,128]{1,0:T(8,128)}, f32[128,128]{1,0:T(8,128)S(1)}, u32[]{:S(2)}, u32[]{:S(2)}) collective-permute-start(f32[128,128]{1,0:T(8,128)} %get-tuple-element.31), channel_id=1, source_target_pairs={{0,4},{1,5},{2,6},{3,7},{4,8},{5,9},{6,10},{7,11},{8,12},{9,13},{1... | collective-permute-start | bytes 196616 | tf_op jit(solution)/shard_map/ppermute | solution.py:853
  31.0 37.6 %copy-start.6 = (f32[12,32,256]{2,1,0:T(8,128)}, f32[12,32,256]{2,1,0:T(8,128)S(1)}, u32[]{:S(2)}) copy-start(f32[12,32,256]{2,1,0:T(8,128)S(1)} %collective-permute-done.1) | copy-start | bytes 1179652
  32.8 44.6 %collective-permute-start.2 = (f32[20,32,256]{2,1,0:T(8,128)S(1)}, f32[20,32,256]{2,1,0:T(8,128)S(1)}, u32[]{:S(2)}, u32[]{:S(2)}) collective-permute-start(f32[20,32,256]{2,1,0:T(8,128)S(1)} %copy-done.15), channel_id=1, source_target_pairs={{0,31},{1,30},{2,29},{3,28},{4,27},{5,26},{6,25},{7,24},{8,23},{9,... | collective-permute-start | bytes 1966088 | tf_op jit(solution)/shard_map/ppermute | solution.py:832
  34.6 42.8 %collective-permute-start.5 = (f32[8,256]{1,0:T(8,128)S(1)}, f32[8,256]{1,0:T(8,128)S(1)}, u32[]{:S(2)}, u32[]{:S(2)}) collective-permute-start(f32[8,256]{1,0:T(8,128)S(1)} %copy-done.18), channel_id=1, source_target_pairs={{0,0},{1,3},{2,2},{3,1},{4,28},{5,31},{6,30},{7,29},{8,24},{9,27},... | collective-permute-start | bytes 24584 | tf_op jit(solution)/shard_map/ppermute | solution.py:832
  35.2 42.2 %collective-permute-start.3 = (f32[32,256]{1,0:T(8,128)S(1)}, f32[32,256]{1,0:T(8,128)S(1)}, u32[]{:S(2)}, u32[]{:S(2)}) collective-permute-start(f32[32,256]{1,0:T(8,128)S(1)} %copy-done.17), channel_id=1, source_target_pairs={{0,3},{1,2},{2,1},{3,0},{4,31},{5,30},{6,29},{7,28},{8,27},{9,26},... | collective-permute-start | bytes 98312 | tf_op jit(solution)/shard_map/ppermute | solution.py:832
  38.1 39.3 %collective-permute-start.4 = (f32[32,256]{1,0:T(8,128)S(1)}, f32[32,256]{1,0:T(8,128)S(1)}, u32[]{:S(2)}, u32[]{:S(2)}) collective-permute-start(f32[32,256]{1,0:T(8,128)S(1)} %copy-done.16), channel_id=1, source_target_pairs={{0,28},{1,31},{2,30},{3,29},{4,24},{5,27},{6,26},{7,25},{8,20},{9,... | collective-permute-start | bytes 98312 | tf_op jit(solution)/shard_map/ppermute | solution.py:832
  72.8 4.6 %copy-start.1 = (s32[3,8192]{1,0:T(4,128)S(1)}, s32[3,8192]{1,0:T(4,128)}, u32[]{:S(2)}) copy-start(s32[3,8192]{1,0:T(4,128)} %cells_ref.2) | copy-start | bytes 294916
  72.8 4.7 %copy-start.3 = (f32[3,8192]{1,0:T(4,128)S(1)}, f32[3,8192]{1,0:T(4,128)}, u32[]{:S(2)}) copy-start(f32[3,8192]{1,0:T(4,128)} %offs_ref.2) | copy-start | bytes 294916
  72.8 33.5 %all-to-all-start = ((f32[32,72,128]{2,1,0:T(8,128)}), f32[32,72,128]{2,1,0:T(8,128)S(1)}, u32[]{:S(2)}, u32[]{:S(2)}) async-start(f32[32,72,128]{2,1,0:T(8,128)} %shard_map.225), calls=%async_computation | async-start | bytes 2359296 | tf_op jit(solution)/shard_map/all_to_all | solution.py:897
  77.4 9.6 %copy-start.12 = (f32[8,256]{1,0:T(8,128)}, f32[8,256]{1,0:T(8,128)S(1)}, u32[]{:S(2)}) copy-start(f32[8,256]{1,0:T(8,128)S(1)} %collective-permute-done.5.last_ref) | copy-start | bytes 24580
  77.4 9.6 %copy-start.10 = (f32[32,256]{1,0:T(8,128)}, f32[32,256]{1,0:T(8,128)S(1)}, u32[]{:S(2)}) copy-start(f32[32,256]{1,0:T(8,128)S(1)} %collective-permute-done.3.row_ref) | copy-start | bytes 98308
  77.4 9.6 %copy-start.11 = (f32[32,256]{1,0:T(8,128)}, f32[32,256]{1,0:T(8,128)S(1)}, u32[]{:S(2)}) copy-start(f32[32,256]{1,0:T(8,128)S(1)} %collective-permute-done.4.edge_ref) | copy-start | bytes 98308
  77.5 9.5 %copy-start.5 = (f32[20,32,256]{2,1,0:T(8,128)}, f32[20,32,256]{2,1,0:T(8,128)S(1)}, u32[]{:S(2)}) copy-start(f32[20,32,256]{2,1,0:T(8,128)S(1)} %collective-permute-done.2) | copy-start | bytes 1966084
  87.0 6.1 %copy-start.2 = (s32[3,8192]{1,0:T(4,128)S(1)}, s32[3,8192]{1,0:T(4,128)}, u32[]{:S(2)}) copy-start(s32[3,8192]{1,0:T(4,128)} %cells_ref.2) | copy-start | bytes 294916
  87.0 6.1 %copy-start.4 = (f32[3,8192]{1,0:T(4,128)S(1)}, f32[3,8192]{1,0:T(4,128)}, u32[]{:S(2)}) copy-start(f32[3,8192]{1,0:T(4,128)} %offs_ref.2) | copy-start | bytes 294916
  106.3 1.0 copy-start
  160.1 9.7 %collective-permute-start.7 = (f32[5,128,128]{2,1,0:T(8,128)}, f32[5,128,128]{2,1,0:T(8,128)S(1)}, u32[]{:S(2)}, u32[]{:S(2)}) collective-permute-start(f32[5,128,128]{2,1,0:T(8,128)} %shard_map.229.own_ref), channel_id=1, source_target_pairs={{0,2},{1,3},{2,0},{3,1},{4,6},{5,7},{6,4},{7,5},{8,10},{9,11},{10,... | collective-permute-start | bytes 983048 | tf_op jit(solution)/shard_map/ppermute | solution.py:837
  161.1 8.7 %collective-permute-start.6 = (f32[5,128,128]{2,1,0:T(8,128)}, f32[5,128,128]{2,1,0:T(8,128)S(1)}, u32[]{:S(2)}, u32[]{:S(2)}) collective-permute-start(f32[5,128,128]{2,1,0:T(8,128)} %shard_map.229.own_ref), channel_id=1, source_target_pairs={{0,1},{1,0},{2,3},{3,2},{4,5},{5,4},{6,7},{7,6},{8,9},{9,8},{10,11... | collective-permute-start | bytes 983048 | tf_op jit(solution)/shard_map/ppermute | solution.py:837
  169.9 1.6 copy-start.7
  169.9 1.6 collective-permute-start.8
  169.9 1.6 copy-start.8
  171.5 0.7 copy-start.9
Sparse Core Ops, SparseCore 0:
  32.9 28.7 all-gather.1

commit v4 on v3

--- a/solution.py
+++ b/solution.py
@@ -233,7 +233,8 @@
 GROUPS = 9
 SLOTS = 4 * GROUPS
 FWD_ROWS = GROUPS * 2 * QUAD
-BACK_ROWS = FWD_ROWS + 24
+BACK_ROWS = FWD_ROWS + 16
+TOP_ROWS = 16 * 16 + 32
 LOT = 512
 CUTS = (0, 12, WIDE)
 SORT_ROWS = 392
@@ -428,11 +429,15 @@
                 out_ref[row : row + 8, :] = part[slab * 8 : slab * 8 + 8]
             for c in range(2):
                 start = slabs * (8 + c)
-                out_ref[pl.ds(FWD_ROWS + 2 * g + c, slabs, stride=BACK_ROWS), :] = part[
-                    start : start + slabs
-                ]
-    for row in range(FWD_ROWS + 2 * GROUPS, BACK_ROWS):
-        out_ref[pl.ds(row, slabs, stride=BACK_ROWS), :] = jnp.zeros((slabs, NG), jnp.float32)
+                top = part[start : start + slabs]
+                if g < GROUPS - 1:
+                    out_ref[pl.ds(FWD_ROWS + 2 * g + c, slabs, stride=BACK_ROWS), :] = top
+                else:
+                    spot = pl.ds(8 * g + c, slabs, stride=BACK_ROWS)
+                    lanes = lax.broadcasted_iota(jnp.int32, (slabs, NG), 1)
+                    moved = pltpu.roll(top, WIDE, 1)
+                    mine = (lanes >= WIDE) & (lanes < 2 * WIDE)
+                    out_ref[spot, :] = jnp.where(mine, moved, out_ref[spot, :])
 
 
 def inverse_planes(
@@ -440,7 +445,7 @@
 ):
     extra = BACK_ROWS - FWD_ROWS
     for s in range(4):
-        main, rest = [[], [], [], []], [[], [], [], []]
+        main, rest, last = [[], [], [], []], [[], [], [], []], []
         for th in range(2):
             parts = [in_ref[(th * 4 + t) * 4 + s, 0:FWD_ROWS, :] for t in range(4)]
             tops = [in_ref[(th * 4 + t) * 4 + s, FWD_ROWS:BACK_ROWS, :] for t in range(4)]
@@ -448,6 +453,8 @@
                 main[i].append(block)
             for i, block in enumerate(turn_blocks(tops)):
                 rest[i].append(block)
+            tail = [pltpu.roll(part[FWD_ROWS - 8 :], NG - WIDE, 1) for part in parts]
+            last.append(turn_blocks(tail)[0])
         for i in range(4):
             row = (i * 4 + s) * FWD_ROWS
             lines = jnp.concatenate(main[i], axis=1)
@@ -459,6 +466,10 @@
             lines = mm3(halves(lines), (tx_hi[...], tx_lo[...]))
             top_cos[row : row + extra, :] = lines[:, 0:NG]
             top_sin[row : row + extra, :] = lines[:, NG : 2 * NG]
+        row = 16 * extra + 8 * s
+        lines = mm3(halves(jnp.concatenate(last, axis=1)), (tx_hi[...], tx_lo[...]))
+        top_cos[row : row + 8, :] = lines[:, 0:NG]
+        top_sin[row : row + 8, :] = lines[:, NG : 2 * NG]
 
     def finish(cos_ref, sin_ref, start, count, stride, table):
         real, imag = pl.ds(start, count, stride=stride), pl.ds(start + 1, count, stride=stride)
@@ -469,7 +480,7 @@
 
     for z in range(QUAD):
         out_ref[z] = finish(mid_cos, mid_sin, 2 * z, 16 * GROUPS, 8, (ty_hi, ty_lo))
-    out_ref[QUAD] = finish(top_cos, top_sin, 0, 8 * extra, 2, (te_hi, te_lo))
+    out_ref[QUAD] = finish(top_cos, top_sin, 0, TOP_ROWS // 2, 2, (te_hi, te_lo))
 
 
 SORT_BITS = 13
@@ -698,7 +709,7 @@
         return (low, high, first, chunk)
 
     def pair_step(pair, carry):
-        packs = [pack_step(2 * pair + n, 0) for n in range(2)]
+        packs = [pack_step(4 * pair + n, 0) for n in range(4)]
         for low, high, first, chunk in packs:
 
             def more(turn, inner):
@@ -710,7 +721,7 @@
             lax.fori_loop(1, (high - low) // 8 + 1, more, 0)
         return carry
 
-    lax.fori_loop(0, 32 // span, pair_step, 0)
+    lax.fori_loop(0, 16 // span, pair_step, 0)
     items = [[int_ref[64 + v * 8 : v * 8 + 72, :] for v in range(8)]]
     for d in range(3):
         items.append([kick_ref[d, v * 8 : v * 8 + 8, :] for v in range(8)])
@@ -741,7 +752,10 @@
     back = np.concatenate([np.cos(angle) * share_line, -np.sin(angle) * share_line], axis=0)
     ty_back = back.T / doubled
     pieces = back.reshape(2, 4 * sub_count, GROUPS, NG)
-    pieces = np.concatenate([pieces, np.zeros((2, 4 * sub_count, 12 - GROUPS, NG))], axis=2)
+    tail = np.zeros((2, sub_count, 4, NG))
+    tail[:, :, 0] = pieces[:, :sub_count, GROUPS - 1]
+    body = pieces[:, :, : GROUPS - 1].reshape(2, -1, NG)
+    pieces = np.concatenate([body, tail.reshape(2, -1, NG)], axis=1)
     te_back = pieces.reshape(-1, NG).T / doubled
     angle = turn * ((cells[:, None] * np.arange(doubled)[None, :]) % doubled)
     tx = np.concatenate([np.cos(angle), np.sin(angle)], axis=0)
@@ -929,7 +943,7 @@
     (pot,) = run(
         inverse_planes,
         [((PLANES, NG, NG), f32)],
-        [((16 * FWD_ROWS, NG), f32)] * 2 + [((16 * (BACK_ROWS - FWD_ROWS), NG), f32)] * 2,
+        [((16 * FWD_ROWS, NG), f32)] * 2 + [((TOP_ROWS, NG), f32)] * 2,
         got,
         *tx_back,
         *ty_back,

time: 194 us -> 190 us (0.979)
  blocking collectives: 41.7 us -> 39.3 us
    all_to_all x1, blocking collectives: 41.7 us -> 39.3 us  [spread_device(): lax.all_to_all(sent.reshape(slabs, BACK_ROWS, NG), both, split_axis=0, co...]
  transfers between devices with their start and end apart: 11 -> 11, of which waited for: 5 -> 5; matrix products, arithmetic and copies ran while one was open for 2% -> 2% of each run, Pallas kernels for 18% -> 19%
where the time goes in v4:
time: 190 us; the launch traced here: 189 us
  Pallas kernels  61.7 us (32%)
  waiting for transfers between devices  41.9 us (22%)
  blocking collectives  39.3 us (21%)
  starting transfers between devices  23.3 us (12%)
  between operations  15.6 us (8%)
  other arithmetic  5.45 us (3%)
    pallas_call x10, Pallas kernels, run(): pl.pallas_call(body, out_shape=out_shape, in_specs=[pl.BlockSpec(memory_s...  61.7 us
    all_to_all x1, blocking collectives, spread_device(): lax.all_to_all(sent.reshape(slabs, BACK_ROWS, NG), both, split_axis=0, co...  39.3 us
    ppermute x5, starting transfers between devices, mirrored(): return lax.ppermute(value, both, moves)  17.3 us
    all_gather x1, waiting for transfers between devices, spread_device(): lax.all_gather(jnp.concatenate([rows, rim], axis=0), 'sub', axis=0, tiled...  16.6 us
    all_to_all x1, waiting for transfers between devices, spread_device(): got = lax.all_to_all(sent, both, split_axis=0, concat_axis=0, tiled=True)  12.3 us
    ppermute x3, waiting for transfers between devices, partner(): lax.ppermute(value, both, [(flat(t, s), flat(t, s ^ turn)) for t, s in pa...  10.1 us
    all_to_all x1, starting transfers between devices, spread_device(): got = lax.all_to_all(sent, both, split_axis=0, concat_axis=0, tiled=True)  4.64 us
  transfers between devices with their start and end apart: 11, of which 5 were waited for; matrix products, arithmetic and copies ran while one was open for 2% of the time, Pallas kernels for 19%

profile of v4, /device:TPU:0, one launch (start us, length us, event | category | flops | bytes accessed | tf_op | source)
XLA Modules:
  0.0 189.1 jit_solution(7106237110097866208)
XLA Ops:
  7.2 0.0 all-gather.2.cloned.1.call-start
  7.2 2.7 %shard_map.223 = (f32[12,32,256]{2,1,0:T(8,128)}, f32[20,32,256]{2,1,0:T(8,128)}, f32[32,256]{1,0:T(8,128)}, f32[32,256]{1,0:T(8,128)}, f32[8,256]{1,0:T(8,128)}) custom-call(f32[32,64,256]{2,1,0:T(8,128)} %bitcast.9), custom_call_target="tpu_custom_call" | custom-call | tf_op jit(solution)/shard_map/pallas_call | solution.py:796
  9.9 0.0 copy-start.13
  9.9 0.0 copy-start.14
  9.9 6.4 %collective-permute-start.1 = (f32[12,32,256]{2,1,0:T(8,128)}, f32[12,32,256]{2,1,0:T(8,128)S(1)}, u32[]{:S(2)}, u32[]{:S(2)}) collective-permute-start(f32[12,32,256]{2,1,0:T(8,128)} %get-tuple-element.32), channel_id=1, source_target_pairs={{0,31},{1,30},{2,29},{3,28},{4,27},{5,26},{6,25},{7,24},{8,23},{9,... | collective-permute-start | bytes 1179656 | tf_op jit(solution)/shard_map/ppermute | solution.py:846
  17.0 6.2 %shard_map.221 = (f32[392,128]{1,0:T(8,128)}, f32[128,128]{1,0:T(8,128)}) custom-call(s32[1]{0:T(128)} %bitcast.2.place_ref, s32[1]{0:T(128)S(6)} %copy.24.live_ref, s32[3,8192]{1,0:T(4,128)} %cells_ref.2, f32[3,8192]{1,0:T(4,128)} %offs_ref.2), custom_call_target="tpu_custom_call" | custom-call | tf_op jit(solution)/shard_map/pallas_call | solution.py:796
  23.2 0.6 collective-permute-start
  23.8 4.3 %shard_map.222.start_ref = f32[768,256]{1,0:T(8,128)} custom-call(s32[1]{0:T(128)} %bitcast.place_ref, f32[392,128]{1,0:T(8,128)} %get-tuple-element.30.rows_ref), custom_call_target="tpu_custom_call" | custom-call | tf_op jit(solution)/shard_map/pallas_call | solution.py:796
  28.1 2.9 %collective-permute-done = f32[128,128]{1,0:T(8,128)S(1)} collective-permute-done((f32[128,128]{1,0:T(8,128)}, f32[128,128]{1,0:T(8,128)S(1)}, u32[]{:S(2)}, u32[]{:S(2)}) %collective-permute-start) | collective-permute-done | bytes 65568 | tf_op jit(solution)/shard_map/ppermute | solution.py:867
  31.0 0.0 collective-permute-done.1
  31.0 1.8 pad_maximum_fusion
  32.8 0.0 all-gather.2.cloned.1.call-update
  32.8 0.0 copy-done.15
  32.8 1.4 collective-permute-start.2
  34.2 0.7 collective-permute-start.5
  34.9 3.1 %collective-permute-start.3 = (f32[32,256]{1,0:T(8,128)S(1)}, f32[32,256]{1,0:T(8,128)S(1)}, u32[]{:S(2)}, u32[]{:S(2)}) collective-permute-start(f32[32,256]{1,0:T(8,128)S(1)} %copy-done.17), channel_id=1, source_target_pairs={{0,3},{1,2},{2,1},{3,0},{4,31},{5,30},{6,29},{7,28},{8,27},{9,26},... | collective-permute-start | bytes 98312 | tf_op jit(solution)/shard_map/ppermute | solution.py:846
  38.0 5.7 %collective-permute-start.4 = (f32[32,256]{1,0:T(8,128)S(1)}, f32[32,256]{1,0:T(8,128)S(1)}, u32[]{:S(2)}, u32[]{:S(2)}) collective-permute-start(f32[32,256]{1,0:T(8,128)S(1)} %copy-done.16), channel_id=1, source_target_pairs={{0,28},{1,31},{2,30},{3,29},{4,24},{5,27},{6,26},{7,25},{8,20},{9,... | collective-permute-start | bytes 98312 | tf_op jit(solution)/shard_map/ppermute | solution.py:846
  43.7 0.0 copy-done.14
  43.7 0.6 fusion
  45.0 16.6 %all-gather.2.cloned.1.call-done.rows_ref.list_ref = f32[2080,128]{1,0:T(8,128)} async-done(((f32[520,128]{1,0:T(8,128)}), f32[2080,128]{1,0:T(8,128)}) %all-gather.2.cloned.1.call-update) | async-done | bytes 1064976 | tf_op jit(solution)/shard_map/all_gather | solution.py:880
  61.6 6.9 %shard_map.224.dens_ref = f32[512,128]{1,0:T(8,128)} custom-call(s32[1]{0:T(128)} %bitcast.place_ref, f32[2080,128]{1,0:T(8,128)} %all-gather.2.cloned.1.call-done.rows_ref.list_ref, f32[768,256]{1,0:T(8,128)} %shard_map.222.start_ref), custom_call_target="tpu_custom_call" | custom-call | tf_op jit(solution)/shard_map/pallas_call | solution.py:796
  68.5 4.2 %shard_map.225 = f32[32,72,128]{2,1,0:T(8,128)} custom-call(s32[1]{0:T(128)} %bitcast.1.lower_ref, f32[512,128]{1,0:T(8,128)} %shard_map.224.dens_ref, f32[2080,128]{1,0:T(8,128)} %all-gather.2.cloned.1.call-done.rows_ref.list_ref, bf16[288,128]{1,0:T(8,128)(2,1)} %constant.65.clone.ty_hi, bf16[288,128]{1,0:T(8,128)(2,1)} %constant.66.clone.ty_lo, ...), custom_call_target="tpu_custom_call" | custom-call | tf_op jit(solution)/shard_map/pallas_call | solution.py:796
  72.7 4.6 %all-to-all-start = ((f32[32,72,128]{2,1,0:T(8,128)}), f32[32,72,128]{2,1,0:T(8,128)S(1)}, u32[]{:S(2)}, u32[]{:S(2)}) async-start(f32[32,72,128]{2,1,0:T(8,128)} %shard_map.225), calls=%async_computation | async-start | bytes 2359296 | tf_op jit(solution)/shard_map/all_to_all | solution.py:911
  77.4 0.0 collective-permute-done.5.last_ref
  77.4 0.0 collective-permute-done.3.row_ref
  77.4 0.0 copy-start.10
  77.4 0.0 collective-permute-done.4.edge_ref
  77.4 0.0 copy-start.11
  77.5 0.0 collective-permute-done.2
  77.5 2.2 %multiply_subtract_fusion = (f32[1,8192]{1,0:T(1,128)S(1)}, f32[1,8192]{1,0:T(1,128)S(1)}) fusion(f32[]{:T(128)} %get-tuple-element.60, f32[]{:T(128)} %get-tuple-element.61, f32[]{:T(128)} %get-tuple-element.59, f32[]{:T(128)S(6)} %mul.106, f32[3,8192]{1,0:T(4,128)S(1)} %copy-done.3, s32[3,8192]{1,0:T(4,128)S(1)} %copy-done.1), kind=kLoop, calls=%fused_computation.5 | loop fusion | flops 327680 | bytes 196624 | tf_op jit(solution)/shard_map/sub | solution.py:28
  79.7 7.3 %shard_map.226 = (s32[264,128]{1,0:T(8,128)}, f32[192,128]{1,0:T(8,128)}) custom-call(s32[1]{0:T(128)} %bitcast.2.place_ref, s32[3,8192]{1,0:T(4,128)} %cells_ref.2, f32[3,8192]{1,0:T(4,128)} %offs_ref.2), custom_call_target="tpu_custom_call" | custom-call | tf_op jit(solution)/shard_map/pallas_call | solution.py:796
  87.0 0.0 copy-start.2
  87.0 0.0 copy-start.4
  87.0 6.1 %shard_map.227.green_ref = f32[256,1152]{1,0:T(8,128)} custom-call(f32[2048,256]{1,0:T(8,128)} %bitcast.10, f32[384,256]{1,0:T(8,128)} %bitcast.13, f32[640,256]{1,0:T(8,128)} %bitcast.12, f32[32,256]{1,0:T(8,128)} %copy-done.10, f32[32,256]{1,0:T(8,128)} %copy-done.11, f32[8,256]{1,0:T(8,128)} %copy-done.12, bf16[256,512]{1,0:T(8,128)(2,1)} %constant.79.clone.pick_ref), custom_call_target="tpu_custom_call" | custom-call | tf_op jit(solution)/shard_map/pallas_call | solution.py:796
  93.1 0.8 pad_maximum_fusion.1
  94.0 12.3 %all-to-all-done.in_ref = f32[32,72,128]{2,1,0:T(8,128)S(1)} async-done(((f32[32,72,128]{2,1,0:T(8,128)}), f32[32,72,128]{2,1,0:T(8,128)S(1)}, u32[]{:S(2)}, u32[]{:S(2)}) %all-to-all-start) | async-done | bytes 1179680 | tf_op jit(solution)/shard_map/all_to_all | solution.py:911
  106.3 1.0 copy-done
  107.3 5.7 %shard_map.228 = f32[2816,128]{1,0:T(8,128)} custom-call(f32[32,72,128]{2,1,0:T(8,128)} %copy-done, f32[256,1152]{1,0:T(8,128)} %shard_map.227.green_ref, bf16[512,256]{1,0:T(8,128)(2,1)} %constant.69.clone.wf_hi, bf16[512,256]{1,0:T(8,128)(2,1)} %constant.70.clone.wf_lo, bf16[320,512]{1,0:T(8,128)(2,1)} %constant.71.clone.wb_hi, ...), custom_call_target="tpu_custom_call" | custom-call | tf_op jit(solution)/shard_map/pallas_call | solution.py:796
  113.0 39.3 %all_to_all.10.in_ref = f32[32,88,128]{2,1,0:T(8,128)} all-to-all(f32[32,88,128]{2,1,0:T(8,128)} %bitcast.11), channel_id=1, replica_groups=mesh['trk'=8,'sub'=4] {'trk','sub'}, dimensions={0} | all-to-all | bytes 2883584 | tf_op jit(solution)/shard_map/all_to_all | solution.py:940
  152.3 5.2 %shard_map.229.own_ref = f32[5,128,128]{2,1,0:T(8,128)} custom-call(f32[32,88,128]{2,1,0:T(8,128)} %all_to_all.10.in_ref, bf16[256,256]{1,0:T(8,128)(2,1)} %constant.73.clone.tx_hi, bf16[256,256]{1,0:T(8,128)(2,1)} %constant.74.clone.tx_lo, bf16[128,288]{1,0:T(8,128)(2,1)} %constant.75.clone.ty_hi, bf16[128,288]{1,0:T(8,128)(2,1)} %constant.76.clone.ty_lo, ...), custom_call_target="tpu_custom_call" | custom-call | tf_op jit(solution)/shard_map/pallas_call | solution.py:796
  157.5 0.5 collective-permute-start.7
  158.1 0.2 collective-permute-start.6
  158.2 8.5 %collective-permute-done.7.chip_ref = f32[5,128,128]{2,1,0:T(8,128)S(1)} collective-permute-done((f32[5,128,128]{2,1,0:T(8,128)}, f32[5,128,128]{2,1,0:T(8,128)S(1)}, u32[]{:S(2)}, u32[]{:S(2)}) %collective-permute-start.7) | collective-permute-done | bytes 327712 | tf_op jit(solution)/shard_map/ppermute | solution.py:851
  166.7 0.0 collective-permute-start.8
  166.7 0.0 collective-permute-done.6.core_ref
  166.7 1.6 collective-permute-done.8.last_ref
  168.3 0.7 copy-done.9
  169.1 13.2 %shard_map.230 = (f32[3,8192]{1,0:T(4,128)}, f32[3,8192]{1,0:T(4,128)}) custom-call(s32[1]{0:T(128)} %bitcast.place_ref, f32[5,128,128]{2,1,0:T(8,128)} %shard_map.229.own_ref, f32[5,128,128]{2,1,0:T(8,128)} %copy-done.8, f32[5,128,128]{2,1,0:T(8,128)} %copy-done.7, f32[5,128,128]{2,1,0:T(8,128)} %copy-done.9, s32[264,128]{1,0:T(8,128)} %get-tuple-element.54.int_ref, ...), custom_call_target="tpu_custom_call" | custom-call | tf_op jit(solution)/shard_map/pallas_call | solution.py:796
  (29 shorter events, 0.1 us)
Async XLA Ops:
  7.2 54.4 %all-gather.2.cloned.1.call-start = ((), (), s32[]{:S(2)}) async-start(), calls=%async_computation.2 | async-start | bytes 1331200 | tf_op jit(solution)/shard_map/all_gather | solution.py:880
  9.9 22.9 %copy-start.15 = (f32[20,32,256]{2,1,0:T(8,128)S(1)}, f32[20,32,256]{2,1,0:T(8,128)}, u32[]{:S(2)}) copy-start(f32[20,32,256]{2,1,0:T(8,128)} %get-tuple-element.40) | copy-start | bytes 1966084
  9.9 24.4 %copy-start.18 = (f32[8,256]{1,0:T(8,128)S(1)}, f32[8,256]{1,0:T(8,128)}, u32[]{:S(2)}) copy-start(f32[8,256]{1,0:T(8,128)} %get-tuple-element.43) | copy-start | bytes 24580
  9.9 25.0 %copy-start.17 = (f32[32,256]{1,0:T(8,128)S(1)}, f32[32,256]{1,0:T(8,128)}, u32[]{:S(2)}) copy-start(f32[32,256]{1,0:T(8,128)} %get-tuple-element.41) | copy-start | bytes 98308
  9.9 28.2 %copy-start.16 = (f32[32,256]{1,0:T(8,128)S(1)}, f32[32,256]{1,0:T(8,128)}, u32[]{:S(2)}) copy-start(f32[32,256]{1,0:T(8,128)} %get-tuple-element.42) | copy-start | bytes 98308
  9.9 33.8 %copy-start.13 = (f32[4]{0:T(128)S(1)}, f32[4]{0:T(128)}, u32[]{:S(2)}) copy-start(f32[4]{0:T(128)} %param.28) | copy-start | bytes 52
  9.9 33.8 %copy-start.14 = (s32[4]{0:T(128)S(1)}, s32[4]{0:T(128)}, u32[]{:S(2)}) copy-start(s32[4]{0:T(128)} %param.27) | copy-start | bytes 52
  9.9 21.1 %collective-permute-start.1 = (f32[12,32,256]{2,1,0:T(8,128)}, f32[12,32,256]{2,1,0:T(8,128)S(1)}, u32[]{:S(2)}, u32[]{:S(2)}) collective-permute-start(f32[12,32,256]{2,1,0:T(8,128)} %get-tuple-element.32), channel_id=1, source_target_pairs={{0,31},{1,30},{2,29},{3,28},{4,27},{5,26},{6,25},{7,24},{8,23},{9,... | collective-permute-start | bytes 1179656 | tf_op jit(solution)/shard_map/ppermute | solution.py:846
  23.2 7.7 %collective-permute-start = (f32[128,128]{1,0:T(8,128)}, f32[128,128]{1,0:T(8,128)S(1)}, u32[]{:S(2)}, u32[]{:S(2)}) collective-permute-start(f32[128,128]{1,0:T(8,128)} %get-tuple-element.31), channel_id=1, source_target_pairs={{0,4},{1,5},{2,6},{3,7},{4,8},{5,9},{6,10},{7,11},{8,12},{9,13},{1... | collective-permute-start | bytes 196616 | tf_op jit(solution)/shard_map/ppermute | solution.py:867
  31.0 37.5 %copy-start.6 = (f32[12,32,256]{2,1,0:T(8,128)}, f32[12,32,256]{2,1,0:T(8,128)S(1)}, u32[]{:S(2)}) copy-start(f32[12,32,256]{2,1,0:T(8,128)S(1)} %collective-permute-done.1) | copy-start | bytes 1179652
  32.8 44.7 %collective-permute-start.2 = (f32[20,32,256]{2,1,0:T(8,128)S(1)}, f32[20,32,256]{2,1,0:T(8,128)S(1)}, u32[]{:S(2)}, u32[]{:S(2)}) collective-permute-start(f32[20,32,256]{2,1,0:T(8,128)S(1)} %copy-done.15), channel_id=1, source_target_pairs={{0,31},{1,30},{2,29},{3,28},{4,27},{5,26},{6,25},{7,24},{8,23},{9,... | collective-permute-start | bytes 1966088 | tf_op jit(solution)/shard_map/ppermute | solution.py:846
  34.2 43.2 %collective-permute-start.5 = (f32[8,256]{1,0:T(8,128)S(1)}, f32[8,256]{1,0:T(8,128)S(1)}, u32[]{:S(2)}, u32[]{:S(2)}) collective-permute-start(f32[8,256]{1,0:T(8,128)S(1)} %copy-done.18), channel_id=1, source_target_pairs={{0,0},{1,3},{2,2},{3,1},{4,28},{5,31},{6,30},{7,29},{8,24},{9,27},... | collective-permute-start | bytes 24584 | tf_op jit(solution)/shard_map/ppermute | solution.py:846
  34.9 42.5 %collective-permute-start.3 = (f32[32,256]{1,0:T(8,128)S(1)}, f32[32,256]{1,0:T(8,128)S(1)}, u32[]{:S(2)}, u32[]{:S(2)}) collective-permute-start(f32[32,256]{1,0:T(8,128)S(1)} %copy-done.17), channel_id=1, source_target_pairs={{0,3},{1,2},{2,1},{3,0},{4,31},{5,30},{6,29},{7,28},{8,27},{9,26},... | collective-permute-start | bytes 98312 | tf_op jit(solution)/shard_map/ppermute | solution.py:846
  38.0 39.4 %collective-permute-start.4 = (f32[32,256]{1,0:T(8,128)S(1)}, f32[32,256]{1,0:T(8,128)S(1)}, u32[]{:S(2)}, u32[]{:S(2)}) collective-permute-start(f32[32,256]{1,0:T(8,128)S(1)} %copy-done.16), channel_id=1, source_target_pairs={{0,28},{1,31},{2,30},{3,29},{4,24},{5,27},{6,26},{7,25},{8,20},{9,... | collective-permute-start | bytes 98312 | tf_op jit(solution)/shard_map/ppermute | solution.py:846
  72.7 4.7 %copy-start.1 = (s32[3,8192]{1,0:T(4,128)S(1)}, s32[3,8192]{1,0:T(4,128)}, u32[]{:S(2)}) copy-start(s32[3,8192]{1,0:T(4,128)} %cells_ref.2) | copy-start | bytes 294916
  72.7 4.8 %copy-start.3 = (f32[3,8192]{1,0:T(4,128)S(1)}, f32[3,8192]{1,0:T(4,128)}, u32[]{:S(2)}) copy-start(f32[3,8192]{1,0:T(4,128)} %offs_ref.2) | copy-start | bytes 294916
  72.7 33.6 %all-to-all-start = ((f32[32,72,128]{2,1,0:T(8,128)}), f32[32,72,128]{2,1,0:T(8,128)S(1)}, u32[]{:S(2)}, u32[]{:S(2)}) async-start(f32[32,72,128]{2,1,0:T(8,128)} %shard_map.225), calls=%async_computation | async-start | bytes 2359296 | tf_op jit(solution)/shard_map/all_to_all | solution.py:911
  77.4 9.6 %copy-start.12 = (f32[8,256]{1,0:T(8,128)}, f32[8,256]{1,0:T(8,128)S(1)}, u32[]{:S(2)}) copy-start(f32[8,256]{1,0:T(8,128)S(1)} %collective-permute-done.5.last_ref) | copy-start | bytes 24580
  77.4 9.6 %copy-start.10 = (f32[32,256]{1,0:T(8,128)}, f32[32,256]{1,0:T(8,128)S(1)}, u32[]{:S(2)}) copy-start(f32[32,256]{1,0:T(8,128)S(1)} %collective-permute-done.3.row_ref) | copy-start | bytes 98308
  77.4 9.5 %copy-start.11 = (f32[32,256]{1,0:T(8,128)}, f32[32,256]{1,0:T(8,128)S(1)}, u32[]{:S(2)}) copy-start(f32[32,256]{1,0:T(8,128)S(1)} %collective-permute-done.4.edge_ref) | copy-start | bytes 98308
  77.5 9.5 %copy-start.5 = (f32[20,32,256]{2,1,0:T(8,128)}, f32[20,32,256]{2,1,0:T(8,128)S(1)}, u32[]{:S(2)}) copy-start(f32[20,32,256]{2,1,0:T(8,128)S(1)} %collective-permute-done.2) | copy-start | bytes 1966084
  87.0 6.1 %copy-start.2 = (s32[3,8192]{1,0:T(4,128)S(1)}, s32[3,8192]{1,0:T(4,128)}, u32[]{:S(2)}) copy-start(s32[3,8192]{1,0:T(4,128)} %cells_ref.2) | copy-start | bytes 294916
  87.0 6.1 %copy-start.4 = (f32[3,8192]{1,0:T(4,128)S(1)}, f32[3,8192]{1,0:T(4,128)}, u32[]{:S(2)}) copy-start(f32[3,8192]{1,0:T(4,128)} %offs_ref.2) | copy-start | bytes 294916
  106.3 1.0 copy-start
  157.5 9.2 %collective-permute-start.7 = (f32[5,128,128]{2,1,0:T(8,128)}, f32[5,128,128]{2,1,0:T(8,128)S(1)}, u32[]{:S(2)}, u32[]{:S(2)}) collective-permute-start(f32[5,128,128]{2,1,0:T(8,128)} %shard_map.229.own_ref), channel_id=1, source_target_pairs={{0,2},{1,3},{2,0},{3,1},{4,6},{5,7},{6,4},{7,5},{8,10},{9,11},{10,... | collective-permute-start | bytes 983048 | tf_op jit(solution)/shard_map/ppermute | solution.py:851
  158.1 8.6 %collective-permute-start.6 = (f32[5,128,128]{2,1,0:T(8,128)}, f32[5,128,128]{2,1,0:T(8,128)S(1)}, u32[]{:S(2)}, u32[]{:S(2)}) collective-permute-start(f32[5,128,128]{2,1,0:T(8,128)} %shard_map.229.own_ref), channel_id=1, source_target_pairs={{0,1},{1,0},{2,3},{3,2},{4,5},{5,4},{6,7},{7,6},{8,9},{9,8},{10,11... | collective-permute-start | bytes 983048 | tf_op jit(solution)/shard_map/ppermute | solution.py:851
  166.7 1.6 copy-start.7
  166.7 1.6 collective-permute-start.8
  166.7 1.6 copy-start.8
  168.3 0.7 copy-start.9
Sparse Core Ops, SparseCore 0:
  32.9 28.5 all-gather.1

commit v5 on v4

--- a/solution.py
+++ b/solution.py
@@ -709,7 +709,7 @@
         return (low, high, first, chunk)
 
     def pair_step(pair, carry):
-        packs = [pack_step(4 * pair + n, 0) for n in range(4)]
+        packs = [pack_step(8 * pair + n, 0) for n in range(8)]
         for low, high, first, chunk in packs:
 
             def more(turn, inner):
@@ -721,7 +721,7 @@
             lax.fori_loop(1, (high - low) // 8 + 1, more, 0)
         return carry
 
-    lax.fori_loop(0, 16 // span, pair_step, 0)
+    lax.fori_loop(0, 8 // span, pair_step, 0)
     items = [[int_ref[64 + v * 8 : v * 8 + 72, :] for v in range(8)]]
     for d in range(3):
         items.append([kick_ref[d, v * 8 : v * 8 + 8, :] for v in range(8)])

time: 190 us -> 189 us (level)
  transfers between devices with their start and end apart: 11 -> 11, of which waited for: 5 -> 5; matrix products, arithmetic and copies ran while one was open for 2% -> 2% of each run, Pallas kernels for 19% -> 18%
where the time goes in v5:
time: 189 us
  Pallas kernels  60.5 us (32%)
  waiting for transfers between devices  42.5 us (22%)
  blocking collectives  39.3 us (21%)
  starting transfers between devices  23.7 us (13%)
  between operations  15.6 us (8%)
  other arithmetic  5.45 us (3%)
    pallas_call x10, Pallas kernels, run(): pl.pallas_call(body, out_shape=out_shape, in_specs=[pl.BlockSpec(memory_s...  60.5 us
    all_to_all x1, blocking collectives, spread_device(): lax.all_to_all(sent.reshape(slabs, BACK_ROWS, NG), both, split_axis=0, co...  39.3 us
    ppermute x5, starting transfers between devices, mirrored(): return lax.ppermute(value, both, moves)  17.3 us
    all_gather x1, waiting for transfers between devices, spread_device(): lax.all_gather(jnp.concatenate([rows, rim], axis=0), 'sub', axis=0, tiled...  16.7 us
    all_to_all x1, waiting for transfers between devices, spread_device(): got = lax.all_to_all(sent, both, split_axis=0, concat_axis=0, tiled=True)  12.3 us
    ppermute x3, waiting for transfers between devices, partner(): lax.ppermute(value, both, [(flat(t, s), flat(t, s ^ turn)) for t, s in pa...  10.1 us
    all_to_all x1, starting transfers between devices, spread_device(): got = lax.all_to_all(sent, both, split_axis=0, concat_axis=0, tiled=True)  5.05 us
  transfers between devices with their start and end apart: 11, of which 5 were waited for; matrix products, arithmetic and copies ran while one was open for 2% of the time, Pallas kernels for 18%

profile of v5, /device:TPU:0, one launch (start us, length us, event | category | flops | bytes accessed | tf_op | source)
XLA Modules:
  0.0 188.9 jit_solution(13201648204034202984)
XLA Ops:
  7.2 0.0 all-gather.2.cloned.1.call-start
  7.2 2.7 %shard_map.223 = (f32[12,32,256]{2,1,0:T(8,128)}, f32[20,32,256]{2,1,0:T(8,128)}, f32[32,256]{1,0:T(8,128)}, f32[32,256]{1,0:T(8,128)}, f32[8,256]{1,0:T(8,128)}) custom-call(f32[32,64,256]{2,1,0:T(8,128)} %bitcast.9), custom_call_target="tpu_custom_call" | custom-call | tf_op jit(solution)/shard_map/pallas_call | solution.py:796
  9.9 0.0 copy-start.13
  9.9 0.0 copy-start.14
  9.9 6.4 %collective-permute-start.1 = (f32[12,32,256]{2,1,0:T(8,128)}, f32[12,32,256]{2,1,0:T(8,128)S(1)}, u32[]{:S(2)}, u32[]{:S(2)}) collective-permute-start(f32[12,32,256]{2,1,0:T(8,128)} %get-tuple-element.32), channel_id=1, source_target_pairs={{0,31},{1,30},{2,29},{3,28},{4,27},{5,26},{6,25},{7,24},{8,23},{9,... | collective-permute-start | bytes 1179656 | tf_op jit(solution)/shard_map/ppermute | solution.py:846
  17.0 6.2 %shard_map.221 = (f32[392,128]{1,0:T(8,128)}, f32[128,128]{1,0:T(8,128)}) custom-call(s32[1]{0:T(128)} %bitcast.2.place_ref, s32[1]{0:T(128)S(6)} %copy.24.live_ref, s32[3,8192]{1,0:T(4,128)} %cells_ref.2, f32[3,8192]{1,0:T(4,128)} %offs_ref.2), custom_call_target="tpu_custom_call" | custom-call | tf_op jit(solution)/shard_map/pallas_call | solution.py:796
  23.2 0.6 collective-permute-start
  23.8 3.7 %shard_map.222.start_ref = f32[768,256]{1,0:T(8,128)} custom-call(s32[1]{0:T(128)} %bitcast.place_ref, f32[392,128]{1,0:T(8,128)} %get-tuple-element.30.rows_ref), custom_call_target="tpu_custom_call" | custom-call | tf_op jit(solution)/shard_map/pallas_call | solution.py:796
  27.6 3.4 %collective-permute-done = f32[128,128]{1,0:T(8,128)S(1)} collective-permute-done((f32[128,128]{1,0:T(8,128)}, f32[128,128]{1,0:T(8,128)S(1)}, u32[]{:S(2)}, u32[]{:S(2)}) %collective-permute-start) | collective-permute-done | bytes 65568 | tf_op jit(solution)/shard_map/ppermute | solution.py:867
  31.0 0.0 collective-permute-done.1
  31.0 1.8 pad_maximum_fusion
  32.8 0.0 all-gather.2.cloned.1.call-update
  32.8 0.0 copy-done.15
  32.8 1.4 collective-permute-start.2
  34.2 0.7 collective-permute-start.5
  34.9 3.3 %collective-permute-start.3 = (f32[32,256]{1,0:T(8,128)S(1)}, f32[32,256]{1,0:T(8,128)S(1)}, u32[]{:S(2)}, u32[]{:S(2)}) collective-permute-start(f32[32,256]{1,0:T(8,128)S(1)} %copy-done.17), channel_id=1, source_target_pairs={{0,3},{1,2},{2,1},{3,0},{4,31},{5,30},{6,29},{7,28},{8,27},{9,26},... | collective-permute-start | bytes 98312 | tf_op jit(solution)/shard_map/ppermute | solution.py:846
  38.1 5.6 %collective-permute-start.4 = (f32[32,256]{1,0:T(8,128)S(1)}, f32[32,256]{1,0:T(8,128)S(1)}, u32[]{:S(2)}, u32[]{:S(2)}) collective-permute-start(f32[32,256]{1,0:T(8,128)S(1)} %copy-done.16), channel_id=1, source_target_pairs={{0,28},{1,31},{2,30},{3,29},{4,24},{5,27},{6,26},{7,25},{8,20},{9,... | collective-permute-start | bytes 98312 | tf_op jit(solution)/shard_map/ppermute | solution.py:846
  43.7 0.0 copy-done.14
  43.7 0.6 fusion
  45.0 16.7 %all-gather.2.cloned.1.call-done.rows_ref.list_ref = f32[2080,128]{1,0:T(8,128)} async-done(((f32[520,128]{1,0:T(8,128)}), f32[2080,128]{1,0:T(8,128)}) %all-gather.2.cloned.1.call-update) | async-done | bytes 1064976 | tf_op jit(solution)/shard_map/all_gather | solution.py:880
  61.7 6.9 %shard_map.224.dens_ref = f32[512,128]{1,0:T(8,128)} custom-call(s32[1]{0:T(128)} %bitcast.place_ref, f32[2080,128]{1,0:T(8,128)} %all-gather.2.cloned.1.call-done.rows_ref.list_ref, f32[768,256]{1,0:T(8,128)} %shard_map.222.start_ref), custom_call_target="tpu_custom_call" | custom-call | tf_op jit(solution)/shard_map/pallas_call | solution.py:796
  68.6 4.2 %shard_map.225 = f32[32,72,128]{2,1,0:T(8,128)} custom-call(s32[1]{0:T(128)} %bitcast.1.lower_ref, f32[512,128]{1,0:T(8,128)} %shard_map.224.dens_ref, f32[2080,128]{1,0:T(8,128)} %all-gather.2.cloned.1.call-done.rows_ref.list_ref, bf16[288,128]{1,0:T(8,128)(2,1)} %constant.65.clone.ty_hi, bf16[288,128]{1,0:T(8,128)(2,1)} %constant.66.clone.ty_lo, ...), custom_call_target="tpu_custom_call" | custom-call | tf_op jit(solution)/shard_map/pallas_call | solution.py:796
  72.9 5.1 %all-to-all-start = ((f32[32,72,128]{2,1,0:T(8,128)}), f32[32,72,128]{2,1,0:T(8,128)S(1)}, u32[]{:S(2)}, u32[]{:S(2)}) async-start(f32[32,72,128]{2,1,0:T(8,128)} %shard_map.225), calls=%async_computation | async-start | bytes 2359296 | tf_op jit(solution)/shard_map/all_to_all | solution.py:911
  77.9 0.0 collective-permute-done.5.last_ref
  77.9 0.0 collective-permute-done.3.row_ref
  77.9 0.0 copy-start.10
  78.0 0.0 collective-permute-done.4.edge_ref
  78.0 0.0 copy-start.11
  78.0 0.0 collective-permute-done.2
  78.0 2.2 %multiply_subtract_fusion = (f32[1,8192]{1,0:T(1,128)S(1)}, f32[1,8192]{1,0:T(1,128)S(1)}) fusion(f32[]{:T(128)} %get-tuple-element.60, f32[]{:T(128)} %get-tuple-element.61, f32[]{:T(128)} %get-tuple-element.59, f32[]{:T(128)S(6)} %mul.106, f32[3,8192]{1,0:T(4,128)S(1)} %copy-done.3, s32[3,8192]{1,0:T(4,128)S(1)} %copy-done.1), kind=kLoop, calls=%fused_computation.5 | loop fusion | flops 327680 | bytes 196624 | tf_op jit(solution)/shard_map/sub | solution.py:28
  80.2 7.3 %shard_map.226 = (s32[264,128]{1,0:T(8,128)}, f32[192,128]{1,0:T(8,128)}) custom-call(s32[1]{0:T(128)} %bitcast.2.place_ref, s32[3,8192]{1,0:T(4,128)} %cells_ref.2, f32[3,8192]{1,0:T(4,128)} %offs_ref.2), custom_call_target="tpu_custom_call" | custom-call | tf_op jit(solution)/shard_map/pallas_call | solution.py:796
  87.5 0.0 copy-start.2
  87.5 0.0 copy-start.4
  87.5 6.1 %shard_map.227.green_ref = f32[256,1152]{1,0:T(8,128)} custom-call(f32[2048,256]{1,0:T(8,128)} %bitcast.10, f32[384,256]{1,0:T(8,128)} %bitcast.13, f32[640,256]{1,0:T(8,128)} %bitcast.12, f32[32,256]{1,0:T(8,128)} %copy-done.10, f32[32,256]{1,0:T(8,128)} %copy-done.11, f32[8,256]{1,0:T(8,128)} %copy-done.12, bf16[256,512]{1,0:T(8,128)(2,1)} %constant.79.clone.pick_ref), custom_call_target="tpu_custom_call" | custom-call | tf_op jit(solution)/shard_map/pallas_call | solution.py:796
  93.7 0.8 pad_maximum_fusion.1
  94.5 12.3 %all-to-all-done.in_ref = f32[32,72,128]{2,1,0:T(8,128)S(1)} async-done(((f32[32,72,128]{2,1,0:T(8,128)}), f32[32,72,128]{2,1,0:T(8,128)S(1)}, u32[]{:S(2)}, u32[]{:S(2)}) %all-to-all-start) | async-done | bytes 1179680 | tf_op jit(solution)/shard_map/all_to_all | solution.py:911
  106.8 1.0 copy-done
  107.8 5.7 %shard_map.228 = f32[2816,128]{1,0:T(8,128)} custom-call(f32[32,72,128]{2,1,0:T(8,128)} %copy-done, f32[256,1152]{1,0:T(8,128)} %shard_map.227.green_ref, bf16[512,256]{1,0:T(8,128)(2,1)} %constant.69.clone.wf_hi, bf16[512,256]{1,0:T(8,128)(2,1)} %constant.70.clone.wf_lo, bf16[320,512]{1,0:T(8,128)(2,1)} %constant.71.clone.wb_hi, ...), custom_call_target="tpu_custom_call" | custom-call | tf_op jit(solution)/shard_map/pallas_call | solution.py:796
  113.5 39.3 %all_to_all.10.in_ref = f32[32,88,128]{2,1,0:T(8,128)} all-to-all(f32[32,88,128]{2,1,0:T(8,128)} %bitcast.11), channel_id=1, replica_groups=mesh['trk'=8,'sub'=4] {'trk','sub'}, dimensions={0} | all-to-all | bytes 2883584 | tf_op jit(solution)/shard_map/all_to_all | solution.py:940
  152.9 5.2 %shard_map.229.own_ref = f32[5,128,128]{2,1,0:T(8,128)} custom-call(f32[32,88,128]{2,1,0:T(8,128)} %all_to_all.10.in_ref, bf16[256,256]{1,0:T(8,128)(2,1)} %constant.73.clone.tx_hi, bf16[256,256]{1,0:T(8,128)(2,1)} %constant.74.clone.tx_lo, bf16[128,288]{1,0:T(8,128)(2,1)} %constant.75.clone.ty_hi, bf16[128,288]{1,0:T(8,128)(2,1)} %constant.76.clone.ty_lo, ...), custom_call_target="tpu_custom_call" | custom-call | tf_op jit(solution)/shard_map/pallas_call | solution.py:796
  158.0 0.5 collective-permute-start.7
  158.6 0.2 collective-permute-start.6
  158.7 8.5 %collective-permute-done.7.chip_ref = f32[5,128,128]{2,1,0:T(8,128)S(1)} collective-permute-done((f32[5,128,128]{2,1,0:T(8,128)}, f32[5,128,128]{2,1,0:T(8,128)S(1)}, u32[]{:S(2)}, u32[]{:S(2)}) %collective-permute-start.7) | collective-permute-done | bytes 327712 | tf_op jit(solution)/shard_map/ppermute | solution.py:851
  167.2 0.0 collective-permute-start.8
  167.2 0.0 collective-permute-done.6.core_ref
  167.2 1.6 collective-permute-done.8.last_ref
  168.8 0.7 copy-done.9
  169.6 12.5 %shard_map.230 = (f32[3,8192]{1,0:T(4,128)}, f32[3,8192]{1,0:T(4,128)}) custom-call(s32[1]{0:T(128)} %bitcast.place_ref, f32[5,128,128]{2,1,0:T(8,128)} %shard_map.229.own_ref, f32[5,128,128]{2,1,0:T(8,128)} %copy-done.8, f32[5,128,128]{2,1,0:T(8,128)} %copy-done.7, f32[5,128,128]{2,1,0:T(8,128)} %copy-done.9, s32[264,128]{1,0:T(8,128)} %get-tuple-element.54.int_ref, ...), custom_call_target="tpu_custom_call" | custom-call | tf_op jit(solution)/shard_map/pallas_call | solution.py:796
  (29 shorter events, 0.1 us)
Async XLA Ops:
  7.2 54.5 %all-gather.2.cloned.1.call-start = ((), (), s32[]{:S(2)}) async-start(), calls=%async_computation.2 | async-start | bytes 1331200 | tf_op jit(solution)/shard_map/all_gather | solution.py:880
  9.9 22.9 %copy-start.15 = (f32[20,32,256]{2,1,0:T(8,128)S(1)}, f32[20,32,256]{2,1,0:T(8,128)}, u32[]{:S(2)}) copy-start(f32[20,32,256]{2,1,0:T(8,128)} %get-tuple-element.40) | copy-start | bytes 1966084
  9.9 24.3 %copy-start.18 = (f32[8,256]{1,0:T(8,128)S(1)}, f32[8,256]{1,0:T(8,128)}, u32[]{:S(2)}) copy-start(f32[8,256]{1,0:T(8,128)} %get-tuple-element.43) | copy-start | bytes 24580
  9.9 25.0 %copy-start.17 = (f32[32,256]{1,0:T(8,128)S(1)}, f32[32,256]{1,0:T(8,128)}, u32[]{:S(2)}) copy-start(f32[32,256]{1,0:T(8,128)} %get-tuple-element.41) | copy-start | bytes 98308
  9.9 28.3 %copy-start.16 = (f32[32,256]{1,0:T(8,128)S(1)}, f32[32,256]{1,0:T(8,128)}, u32[]{:S(2)}) copy-start(f32[32,256]{1,0:T(8,128)} %get-tuple-element.42) | copy-start | bytes 98308
  9.9 33.8 %copy-start.13 = (f32[4]{0:T(128)S(1)}, f32[4]{0:T(128)}, u32[]{:S(2)}) copy-start(f32[4]{0:T(128)} %param.28) | copy-start | bytes 52
  9.9 33.8 %copy-start.14 = (s32[4]{0:T(128)S(1)}, s32[4]{0:T(128)}, u32[]{:S(2)}) copy-start(s32[4]{0:T(128)} %param.27) | copy-start | bytes 52
  9.9 21.1 %collective-permute-start.1 = (f32[12,32,256]{2,1,0:T(8,128)}, f32[12,32,256]{2,1,0:T(8,128)S(1)}, u32[]{:S(2)}, u32[]{:S(2)}) collective-permute-start(f32[12,32,256]{2,1,0:T(8,128)} %get-tuple-element.32), channel_id=1, source_target_pairs={{0,31},{1,30},{2,29},{3,28},{4,27},{5,26},{6,25},{7,24},{8,23},{9,... | collective-permute-start | bytes 1179656 | tf_op jit(solution)/shard_map/ppermute | solution.py:846
  23.2 7.7 %collective-permute-start = (f32[128,128]{1,0:T(8,128)}, f32[128,128]{1,0:T(8,128)S(1)}, u32[]{:S(2)}, u32[]{:S(2)}) collective-permute-start(f32[128,128]{1,0:T(8,128)} %get-tuple-element.31), channel_id=1, source_target_pairs={{0,4},{1,5},{2,6},{3,7},{4,8},{5,9},{6,10},{7,11},{8,12},{9,13},{1... | collective-permute-start | bytes 196616 | tf_op jit(solution)/shard_map/ppermute | solution.py:867
  31.0 37.6 %copy-start.6 = (f32[12,32,256]{2,1,0:T(8,128)}, f32[12,32,256]{2,1,0:T(8,128)S(1)}, u32[]{:S(2)}) copy-start(f32[12,32,256]{2,1,0:T(8,128)S(1)} %collective-permute-done.1) | copy-start | bytes 1179652
  32.8 45.2 %collective-permute-start.2 = (f32[20,32,256]{2,1,0:T(8,128)S(1)}, f32[20,32,256]{2,1,0:T(8,128)S(1)}, u32[]{:S(2)}, u32[]{:S(2)}) collective-permute-start(f32[20,32,256]{2,1,0:T(8,128)S(1)} %copy-done.15), channel_id=1, source_target_pairs={{0,31},{1,30},{2,29},{3,28},{4,27},{5,26},{6,25},{7,24},{8,23},{9,... | collective-permute-start | bytes 1966088 | tf_op jit(solution)/shard_map/ppermute | solution.py:846
  34.2 43.7 %collective-permute-start.5 = (f32[8,256]{1,0:T(8,128)S(1)}, f32[8,256]{1,0:T(8,128)S(1)}, u32[]{:S(2)}, u32[]{:S(2)}) collective-permute-start(f32[8,256]{1,0:T(8,128)S(1)} %copy-done.18), channel_id=1, source_target_pairs={{0,0},{1,3},{2,2},{3,1},{4,28},{5,31},{6,30},{7,29},{8,24},{9,27},... | collective-permute-start | bytes 24584 | tf_op jit(solution)/shard_map/ppermute | solution.py:846
  34.9 43.1 %collective-permute-start.3 = (f32[32,256]{1,0:T(8,128)S(1)}, f32[32,256]{1,0:T(8,128)S(1)}, u32[]{:S(2)}, u32[]{:S(2)}) collective-permute-start(f32[32,256]{1,0:T(8,128)S(1)} %copy-done.17), channel_id=1, source_target_pairs={{0,3},{1,2},{2,1},{3,0},{4,31},{5,30},{6,29},{7,28},{8,27},{9,26},... | collective-permute-start | bytes 98312 | tf_op jit(solution)/shard_map/ppermute | solution.py:846
  38.1 39.8 %collective-permute-start.4 = (f32[32,256]{1,0:T(8,128)S(1)}, f32[32,256]{1,0:T(8,128)S(1)}, u32[]{:S(2)}, u32[]{:S(2)}) collective-permute-start(f32[32,256]{1,0:T(8,128)S(1)} %copy-done.16), channel_id=1, source_target_pairs={{0,28},{1,31},{2,30},{3,29},{4,24},{5,27},{6,26},{7,25},{8,20},{9,... | collective-permute-start | bytes 98312 | tf_op jit(solution)/shard_map/ppermute | solution.py:846
  72.9 5.2 %copy-start.1 = (s32[3,8192]{1,0:T(4,128)S(1)}, s32[3,8192]{1,0:T(4,128)}, u32[]{:S(2)}) copy-start(s32[3,8192]{1,0:T(4,128)} %cells_ref.2) | copy-start | bytes 294916
  72.9 5.2 %copy-start.3 = (f32[3,8192]{1,0:T(4,128)S(1)}, f32[3,8192]{1,0:T(4,128)}, u32[]{:S(2)}) copy-start(f32[3,8192]{1,0:T(4,128)} %offs_ref.2) | copy-start | bytes 294916
  72.9 34.0 %all-to-all-start = ((f32[32,72,128]{2,1,0:T(8,128)}), f32[32,72,128]{2,1,0:T(8,128)S(1)}, u32[]{:S(2)}, u32[]{:S(2)}) async-start(f32[32,72,128]{2,1,0:T(8,128)} %shard_map.225), calls=%async_computation | async-start | bytes 2359296 | tf_op jit(solution)/shard_map/all_to_all | solution.py:911
  77.9 9.6 %copy-start.12 = (f32[8,256]{1,0:T(8,128)}, f32[8,256]{1,0:T(8,128)S(1)}, u32[]{:S(2)}) copy-start(f32[8,256]{1,0:T(8,128)S(1)} %collective-permute-done.5.last_ref) | copy-start | bytes 24580
  77.9 9.6 %copy-start.10 = (f32[32,256]{1,0:T(8,128)}, f32[32,256]{1,0:T(8,128)S(1)}, u32[]{:S(2)}) copy-start(f32[32,256]{1,0:T(8,128)S(1)} %collective-permute-done.3.row_ref) | copy-start | bytes 98308
  78.0 9.5 %copy-start.11 = (f32[32,256]{1,0:T(8,128)}, f32[32,256]{1,0:T(8,128)S(1)}, u32[]{:S(2)}) copy-start(f32[32,256]{1,0:T(8,128)S(1)} %collective-permute-done.4.edge_ref) | copy-start | bytes 98308
  78.0 9.5 %copy-start.5 = (f32[20,32,256]{2,1,0:T(8,128)}, f32[20,32,256]{2,1,0:T(8,128)S(1)}, u32[]{:S(2)}) copy-start(f32[20,32,256]{2,1,0:T(8,128)S(1)} %collective-permute-done.2) | copy-start | bytes 1966084
  87.5 6.1 %copy-start.2 = (s32[3,8192]{1,0:T(4,128)S(1)}, s32[3,8192]{1,0:T(4,128)}, u32[]{:S(2)}) copy-start(s32[3,8192]{1,0:T(4,128)} %cells_ref.2) | copy-start | bytes 294916
  87.5 6.1 %copy-start.4 = (f32[3,8192]{1,0:T(4,128)S(1)}, f32[3,8192]{1,0:T(4,128)}, u32[]{:S(2)}) copy-start(f32[3,8192]{1,0:T(4,128)} %offs_ref.2) | copy-start | bytes 294916
  106.8 1.0 copy-start
  158.0 9.2 %collective-permute-start.7 = (f32[5,128,128]{2,1,0:T(8,128)}, f32[5,128,128]{2,1,0:T(8,128)S(1)}, u32[]{:S(2)}, u32[]{:S(2)}) collective-permute-start(f32[5,128,128]{2,1,0:T(8,128)} %shard_map.229.own_ref), channel_id=1, source_target_pairs={{0,2},{1,3},{2,0},{3,1},{4,6},{5,7},{6,4},{7,5},{8,10},{9,11},{10,... | collective-permute-start | bytes 983048 | tf_op jit(solution)/shard_map/ppermute | solution.py:851
  158.6 8.6 %collective-permute-start.6 = (f32[5,128,128]{2,1,0:T(8,128)}, f32[5,128,128]{2,1,0:T(8,128)S(1)}, u32[]{:S(2)}, u32[]{:S(2)}) collective-permute-start(f32[5,128,128]{2,1,0:T(8,128)} %shard_map.229.own_ref), channel_id=1, source_target_pairs={{0,1},{1,0},{2,3},{3,2},{4,5},{5,4},{6,7},{7,6},{8,9},{9,8},{10,11... | collective-permute-start | bytes 983048 | tf_op jit(solution)/shard_map/ppermute | solution.py:851
  167.2 1.6 copy-start.7
  167.2 1.6 collective-permute-start.8
  167.2 1.6 copy-start.8
  168.8 0.7 copy-start.9
Sparse Core Ops, SparseCore 0:
  32.9 28.7 all-gather.1
